TPU v7x, 32 devices: a whole 2x2x4 slice. The times are simulated.
32 devices in a mesh: dp: 4 (over x, core), seq: 2 (over y), tensor: 4 (over z).
Axes of the slice: x: 2, y: 2, z: 4, core: 2. Of those that a mesh axis runs over, the one named last changes fastest.
Arguments:
- history: bfloat16 [4, 8, 1024, 2048], P(None, 'dp', 'seq'), may hold values from -6 to 6
- positions: int32 [8, 1024], P('dp', 'seq'), may hold values from 0 to 2046, as said below
- lengths: int32 [8], P('dp'), may hold values from 256 to 1024, as said below
- cotangent: bfloat16 [8, 1024, 2048], P('dp', 'seq'), may hold values from -6 to 6
- mix_gain: float32 [2048], replicated, may hold values from 0.5 to 1.5
- mix_w1: bfloat16 [2048, 16], P(('dp', 'seq')), may hold values from -0.125 to 0.125
- mix_w2: float32 [16, 16], replicated, may hold values from -1.5 to 1.5
- ln_gain: float32 [4, 2048], replicated, may hold values from 0.5 to 1.5
- ln_bias: float32 [4, 2048], replicated, may hold values from -1.8 to 1.8
- qkv_weight: bfloat16 [3, 2048, 2048], P(None, ('dp', 'seq'), 'tensor'), may hold values from -0.125 to 0.125
- qkv_bias: float32 [3, 2048], P(None, 'tensor'), may hold values from -1.8 to 1.8
- out_weight: bfloat16 [2048, 2048], P(('dp', 'seq'), 'tensor'), may hold values from -2 to 2
- out_bias: float32 [2048], replicated, may hold values from -1.8 to 1.8
- up_weight: bfloat16 [2048, 8192], P(('dp', 'seq'), 'tensor'), may hold values from -0.125 to 0.125
- up_bias: float32 [8192], P('tensor'), may hold values from -1.8 to 1.8
- down_weight: bfloat16 [2048, 8192], P(('dp', 'seq'), 'tensor'), may hold values from -0.0625 to 0.0625
- down_bias: float32 [2048], replicated, may hold values from -1.8 to 1.8
Outputs:
- layer_out: bfloat16 [8, 1024, 2048], P('dp', 'seq')
- grad_history: float32 [4, 8, 1024, 2048], P(None, 'dp', 'seq')
- grad_mix_gain: float32 [2048], replicated
- grad_mix_w1: float32 [2048, 16], P(('dp', 'seq'))
- grad_mix_w2: float32 [16, 16], replicated
- grad_ln_gain: float32 [4, 2048], replicated
- grad_ln_bias: float32 [4, 2048], replicated
- grad_qkv_weight: float32 [3, 2048, 2048], P(None, ('dp', 'seq'), 'tensor')
- grad_qkv_bias: float32 [3, 2048], P(None, 'tensor')
- grad_out_weight: float32 [2048, 2048], P(('dp', 'seq'), 'tensor')
- grad_out_bias: float32 [2048], replicated
- grad_up_weight: float32 [2048, 8192], P(('dp', 'seq'), 'tensor')
- grad_up_bias: float32 [8192], P('tensor')
- grad_down_weight: float32 [2048, 8192], P(('dp', 'seq'), 'tensor')
- grad_down_bias: float32 [2048], replicated
Inputs may be any that keep to these rules, and one draw needn't show every extreme that they name: Some slot has exactly 1024 valid tokens; the valid tokens of slot s are its first lengths[s] positions. `positions`: strictly increasing along each slot by steps of 1 or 2, the first being 0 or 1; some slot starts at 0 and steps by 2 throughout.
All inputs are finite; a program needn't handle non-finite values.
Results may differ from a plain program's by a relative error of at most 0.014.
The roundings to bfloat16 on the way count: a program that leaves them out, or rounds other values in their place, can miss the bound.
Values may be sent and summed in bfloat16 or wider, within the bound.
A program may use at most 320 MiB of HBM per device.

v0:
```python
import math

import jax
import jax.numpy as jnp
from jax import lax
from jax.sharding import PartitionSpec as P

HEAD_DIM = 128
ROT = 32
STREAMS = 4


EXACT = lax.Precision.HIGHEST
RMS_EPSILON = 1e-06
NORM_EPSILON = 1e-05


def layer_norm(values, norm_gain, norm_bias):
    centred = values - jnp.mean(values, axis=-1, keepdims=True)
    variance = jnp.mean(centred * centred, axis=-1, keepdims=True)
    return centred * lax.rsqrt(variance + NORM_EPSILON) * norm_gain + norm_bias


def rms_scale(values, norm_gain):
    return (
        values
        * lax.rsqrt(jnp.mean(values * values, axis=-1, keepdims=True) + RMS_EPSILON)
        * norm_gain
    )


def exact_gelu(values):
    return jax.nn.gelu(values, approximate=False)


def rotary_tables(positions):
    exponents = jnp.arange(0, ROT, 2).astype(jnp.float32) / ROT
    inverse = jnp.power(10000.0, -exponents)
    phases = positions.astype(jnp.float32)[:, None] * inverse[None, :]
    phases = jnp.concatenate([phases, phases], axis=-1)[:, None, :]
    return (jnp.cos(phases), jnp.sin(phases))


def rotary(values, cosines, sines):
    rot_width = cosines.shape[-1]
    half_width = rot_width // 2
    turned = values[..., :rot_width]
    rotated = jnp.concatenate([-turned[..., half_width:], turned[..., :half_width]], axis=-1)
    return jnp.concatenate([turned * cosines + rotated * sines, values[..., rot_width:]], axis=-1)


def combine_layers(layers, latest, mix_weights):
    combined = []
    for target in range(mix_weights.shape[1]):
        running = latest
        for source in range(layers.shape[0]):
            running = running + mix_weights[:, target, source][:, None] * layers[source].astype(
                jnp.float32
            )
        combined.append(running)
    return combined


def masked_scores(queries, key_rows, allowed, scaling):
    scores = (
        jnp.einsum("sqhd,skhd->shqk", queries, key_rows, preferred_element_type=jnp.float32)
        * scaling
    )
    return jnp.where(allowed, scores, -1e30)


def row_product(left, right):
    return lax.dot_general(
        left, right, (((0,), (0,)), ((), ())), preferred_element_type=jnp.float32
    )


def col_product(left, right):
    return lax.dot_general(
        left, right, (((1,), (1,)), ((), ())), preferred_element_type=jnp.float32
    )


def shards(
    history,
    positions,
    lengths,
    cotangent,
    mix_gain,
    mix_w1,
    mix_w2,
    ln_gain,
    ln_bias,
    qkv_weight,
    qkv_bias,
    out_weight,
    out_bias,
    up_weight,
    up_bias,
    down_weight,
    down_bias,
):
    depth_count, slot_count, block_len, feature_count = history.shape
    row_count = slot_count * block_len
    local_width = qkv_weight.shape[2]
    heads_local = local_width // HEAD_DIM
    key_count = block_len * lax.axis_size("seq")
    scaling = 1.0 / math.sqrt(HEAD_DIM)
    layers = history.reshape(depth_count, row_count, feature_count)
    latest = layers[depth_count - 1].astype(jnp.float32)
    w_mix, w_qkv, w_out, w_up, w_down = (
        lax.all_gather(mix_w1, ("dp", "seq"), axis=0, tiled=True),
        lax.all_gather(qkv_weight, ("dp", "seq"), axis=1, tiled=True),
        lax.all_gather(out_weight, ("dp", "seq"), axis=0, tiled=True),
        lax.all_gather(up_weight, ("dp", "seq"), axis=0, tiled=True),
        lax.all_gather(down_weight, ("dp", "seq"), axis=0, tiled=True),
    )
    normed = rms_scale(latest, mix_gain).astype(jnp.bfloat16)
    mix_pre = jnp.dot(normed, w_mix, preferred_element_type=jnp.float32)
    mix_act = exact_gelu(mix_pre)
    mix_weights = jnp.dot(mix_act, mix_w2, precision=EXACT).reshape(row_count, STREAMS, depth_count)
    combined = combine_layers(layers, latest, mix_weights)
    cosines, sines = rotary_tables(positions.reshape(row_count))
    normed_in = [
        layer_norm(combined[branch], ln_gain[branch], ln_bias[branch]).astype(jnp.bfloat16)
        for branch in range(3)
    ]
    projected = [
        jnp.dot(normed_in[branch], w_qkv[branch], preferred_element_type=jnp.float32)
        + qkv_bias[branch]
        for branch in range(3)
    ]
    head_shape = (row_count, heads_local, HEAD_DIM)
    slot_shape = (slot_count, block_len, local_width)
    queries = rotary(projected[0].reshape(head_shape), cosines, sines).astype(jnp.bfloat16)
    key_rows = (
        rotary(projected[1].reshape(head_shape), cosines, sines)
        .astype(jnp.bfloat16)
        .reshape(slot_shape)
    )
    value_rows = projected[2].astype(jnp.bfloat16).reshape(slot_shape)
    keys_all, values_all = (
        lax.all_gather(key_rows, "seq", axis=1, tiled=True),
        lax.all_gather(value_rows, "seq", axis=1, tiled=True),
    )
    queries4 = queries.reshape(slot_count, block_len, heads_local, HEAD_DIM)
    full_shape = (slot_count, key_count, heads_local, HEAD_DIM)
    query_place = lax.axis_index("seq") * block_len + jnp.arange(block_len, dtype=jnp.int32)
    key_place = jnp.arange(key_count, dtype=jnp.int32)
    allowed = (key_place[None, None, :] <= query_place[None, :, None]) & (
        key_place[None, None, :] < lengths[:, None, None]
    )
    allowed = allowed[:, None, :, :]
    scores = masked_scores(queries4, keys_all.reshape(full_shape), allowed, scaling)
    row_max = jnp.max(scores, axis=-1, keepdims=True)
    log_total = row_max + jnp.log(jnp.sum(jnp.exp(scores - row_max), axis=-1, keepdims=True))
    probs_low = jnp.exp(scores - log_total).astype(jnp.bfloat16)
    attended = jnp.einsum(
        "shqk,skhd->sqhd",
        probs_low,
        values_all.reshape(full_shape),
        preferred_element_type=jnp.float32,
    )
    attn_vals = attended.reshape(row_count, local_width).astype(jnp.bfloat16)
    attn_part = col_product(attn_vals, w_out)
    hidden = combined[3] + (lax.psum(attn_part, "tensor") + out_bias)
    mlp_in = layer_norm(hidden, ln_gain[3], ln_bias[3]).astype(jnp.bfloat16)
    up_lin = jnp.dot(mlp_in, w_up, preferred_element_type=jnp.float32) + up_bias
    up_act = exact_gelu(up_lin).astype(jnp.bfloat16)
    down_part = col_product(up_act, w_down)
    result = hidden + (
        lax.psum(down_part.astype(jnp.bfloat16), "tensor").astype(jnp.float32) + down_bias
    )
    layer_out = result.astype(jnp.bfloat16).reshape(slot_count, block_len, feature_count)
    valid_rows = (query_place[None, :] < lengths[:, None]).reshape(row_count, 1)
    grad_result = jnp.where(
        valid_rows, cotangent.reshape(row_count, feature_count).astype(jnp.float32), 0.0
    )
    grad_mlp = grad_result.astype(jnp.bfloat16)
    mix_again, qkv_again, out_again, up_again, down_again = (
        lax.all_gather(mix_w1, ("dp", "seq"), axis=0, tiled=True),
        lax.all_gather(qkv_weight, ("dp", "seq"), axis=1, tiled=True),
        lax.all_gather(out_weight, ("dp", "seq"), axis=0, tiled=True),
        lax.all_gather(up_weight, ("dp", "seq"), axis=0, tiled=True),
        lax.all_gather(down_weight, ("dp", "seq"), axis=0, tiled=True),
    )
    keys_again, values_again = (
        lax.all_gather(key_rows, "seq", axis=1, tiled=True),
        lax.all_gather(value_rows, "seq", axis=1, tiled=True),
    )
    grad_down_bias = jnp.sum(grad_mlp.astype(jnp.float32), axis=0)
    grad_down_weight = row_product(grad_mlp, up_act)
    grad_up_act = jnp.dot(grad_mlp, down_again, preferred_element_type=jnp.float32)
    grad_up = jax.vjp(exact_gelu, up_lin)[1](grad_up_act)[0].astype(jnp.bfloat16)
    grad_up_bias = jnp.sum(grad_up.astype(jnp.float32), axis=0)
    grad_up_weight = row_product(mlp_in, grad_up)
    grad_mlp_in = lax.psum(col_product(grad_up, up_again), "tensor")
    hidden_back = jax.vjp(layer_norm, hidden, ln_gain[3], ln_bias[3])[1](grad_mlp_in)
    grad_hidden = grad_result + hidden_back[0]
    grad_attn = grad_hidden.astype(jnp.bfloat16)
    grad_out_bias = jnp.sum(grad_attn.astype(jnp.float32), axis=0)
    grad_out_weight = row_product(grad_attn, attn_vals)
    grad_vals = jnp.dot(grad_attn, out_again, preferred_element_type=jnp.float32).astype(
        jnp.bfloat16
    )
    grad_vals = grad_vals.reshape(slot_count, block_len, heads_local, HEAD_DIM)
    keys_full = keys_again.reshape(full_shape)
    values_full = values_again.reshape(full_shape)
    scores_again = masked_scores(queries4, keys_full, allowed, scaling)
    probabilities = jnp.exp(scores_again - log_total)
    grad_probs = jnp.einsum(
        "sqhd,skhd->shqk", grad_vals, values_full, preferred_element_type=jnp.float32
    )
    row_dot = jnp.sum(probabilities * grad_probs, axis=-1, keepdims=True)
    grad_scores = (probabilities * (grad_probs - row_dot)).astype(jnp.bfloat16)
    grad_queries = (
        jnp.einsum("shqk,skhd->sqhd", grad_scores, keys_full, preferred_element_type=jnp.float32)
        * scaling
    )
    grad_keys_all = (
        jnp.einsum("shqk,sqhd->skhd", grad_scores, queries4, preferred_element_type=jnp.float32)
        * scaling
    )
    grad_values_all = jnp.einsum(
        "shqk,sqhd->skhd",
        probabilities.astype(jnp.bfloat16),
        grad_vals,
        preferred_element_type=jnp.float32,
    )
    grad_keys, grad_values = (
        lax.psum_scatter(
            grad_keys_all.reshape(slot_count, key_count, local_width),
            "seq",
            scatter_dimension=1,
            tiled=True,
        ),
        lax.psum_scatter(
            grad_values_all.reshape(slot_count, key_count, local_width),
            "seq",
            scatter_dimension=1,
            tiled=True,
        ),
    )
    unturn = jax.vjp(
        lambda values: rotary(values, cosines, sines), projected[0].reshape(head_shape)
    )[1]
    grad_lin = [
        unturn(grad_queries.reshape(head_shape))[0]
        .reshape(row_count, local_width)
        .astype(jnp.bfloat16),
        unturn(grad_keys.reshape(head_shape))[0]
        .reshape(row_count, local_width)
        .astype(jnp.bfloat16),
        grad_values.reshape(row_count, local_width).astype(jnp.bfloat16),
    ]
    grad_qkv_bias = jnp.stack(
        [jnp.sum(grad_lin[branch].astype(jnp.float32), axis=0) for branch in range(3)]
    )
    grad_qkv_weight = jnp.stack(
        [row_product(normed_in[branch], grad_lin[branch]) for branch in range(3)]
    )
    grad_inputs = lax.psum(
        (
            col_product(grad_lin[0], qkv_again[0]),
            col_product(grad_lin[1], qkv_again[1]),
            col_product(grad_lin[2], qkv_again[2]),
        ),
        "tensor",
    )
    grad_combined = []
    grad_gains = []
    grad_biases = []
    for branch in range(3):
        norm_back = jax.vjp(layer_norm, combined[branch], ln_gain[branch], ln_bias[branch])[1](
            grad_inputs[branch]
        )
        grad_combined.append(norm_back[0])
        grad_gains.append(norm_back[1])
        grad_biases.append(norm_back[2])
    grad_combined.append(grad_hidden)
    grad_gains.append(hidden_back[1])
    grad_biases.append(hidden_back[2])
    grad_ln_gain = jnp.stack(grad_gains)
    grad_ln_bias = jnp.stack(grad_biases)
    grad_stack = jnp.stack(grad_combined)
    layers_wide = layers.astype(jnp.float32)
    grad_mix = jnp.einsum("snd,jnd->nsj", grad_stack, layers_wide, precision=EXACT)
    grad_layers = jnp.einsum("nsj,snd->jnd", mix_weights, grad_stack, precision=EXACT)
    grad_mix_flat = grad_mix.reshape(row_count, STREAMS * depth_count)
    grad_mix_w2 = jnp.dot(mix_act.T, grad_mix_flat, precision=EXACT)
    grad_mix_act = jnp.dot(grad_mix_flat, mix_w2.T, precision=EXACT)
    grad_mix_pre = jax.vjp(exact_gelu, mix_pre)[1](grad_mix_act)[0].astype(jnp.bfloat16)
    grad_mix_w1 = row_product(normed, grad_mix_pre)
    grad_normed = col_product(grad_mix_pre, mix_again)
    rms_back = jax.vjp(rms_scale, latest, mix_gain)[1](grad_normed)
    grad_mix_gain = rms_back[1]
    grad_latest = grad_layers[depth_count - 1] + jnp.sum(grad_stack, axis=0) + rms_back[0]
    grad_layers = jnp.concatenate([grad_layers[: depth_count - 1], grad_latest[None]], axis=0)
    grad_history = grad_layers.reshape(depth_count, slot_count, block_len, feature_count)
    shard_mix_w1, shard_qkv, shard_out, shard_up, shard_down = (
        lax.psum_scatter(grad_mix_w1, ("dp", "seq"), scatter_dimension=0, tiled=True),
        lax.psum_scatter(grad_qkv_weight, ("dp", "seq"), scatter_dimension=1, tiled=True),
        lax.psum_scatter(grad_out_weight, ("dp", "seq"), scatter_dimension=0, tiled=True),
        lax.psum_scatter(grad_up_weight, ("dp", "seq"), scatter_dimension=0, tiled=True),
        lax.psum_scatter(grad_down_weight, ("dp", "seq"), scatter_dimension=0, tiled=True),
    )
    summed_small = lax.psum(
        (
            grad_mix_gain,
            grad_mix_w2,
            grad_ln_gain,
            grad_ln_bias,
            grad_qkv_bias,
            grad_out_bias,
            grad_up_bias,
            grad_down_bias,
        ),
        ("dp", "seq"),
    )
    return (
        layer_out,
        grad_history,
        summed_small[0],
        shard_mix_w1,
        summed_small[1],
        summed_small[2],
        summed_small[3],
        shard_qkv,
        summed_small[4],
        shard_out,
        summed_small[5],
        shard_up,
        summed_small[6],
        shard_down,
        summed_small[7],
    )


def solution(mesh):
    in_specs = (
        P(None, "dp", "seq", None),
        P("dp", "seq"),
        P("dp"),
        P("dp", "seq", None),
        P(),
        P(("dp", "seq"), None),
        P(),
        P(),
        P(),
        P(None, ("dp", "seq"), "tensor"),
        P(None, "tensor"),
        P(("dp", "seq"), "tensor"),
        P(),
        P(("dp", "seq"), "tensor"),
        P("tensor"),
        P(("dp", "seq"), "tensor"),
        P(),
    )
    out_specs = (
        P("dp", "seq", None),
        P(None, "dp", "seq", None),
        P(),
        P(("dp", "seq"), None),
        P(),
        P(),
        P(),
        P(None, ("dp", "seq"), "tensor"),
        P(None, "tensor"),
        P(("dp", "seq"), "tensor"),
        P(),
        P(("dp", "seq"), "tensor"),
        P("tensor"),
        P(("dp", "seq"), "tensor"),
        P(),
    )
    return jax.shard_map(shards, mesh=mesh, in_specs=in_specs, out_specs=out_specs, check_vma=False)
```

profile of v0, /device:TPU:0, one launch (start us, length us, event | category | flops | bytes accessed | tf_op | source)
XLA Modules:
  0.0 2624.2 jit_solution(13404315260656551162)
XLA Ops:
  12.4 15.0 all_gather.28
  105.1 12.6 all-gather.9.cloned.1.call-done
  121.7 31.4 %all-gather.11.cloned.1.call-done = bf16[2,1024,512]{2,1,0:T(8,128)(2,1)} async-done(((bf16[2,512,512]{2,1,0:T(8,128)(2,1)}), bf16[2,1024,512]{2,1,0:T(8,128)(2,1)}) %all-gather.11.cloned.1.call-update) | async-done | bytes 2097168 | tf_op jit(solution)/shard_map/all_gather | solution.py:143
  197.0 283.9 %all-reduce.16.cloned.1.call-done = f32[1024,2048]{1,0:T(8,128)} async-done(((f32[1024,2048]{1,0:T(8,128)}), f32[1024,2048]{1,0:T(8,128)}) %all-reduce.16.cloned.1.call-update) | async-done | bytes 8388624 | tf_op jit(solution)/shard_map/psum | solution.py:166
  480.9 11.3 fusion.110
  496.5 39.6 %all-gather.15.cloned.1.call-done = bf16[2048,2048]{1,0:T(8,128)(2,1)} async-done(((bf16[256,2048]{1,0:T(8,128)(2,1)}), bf16[2048,2048]{1,0:T(8,128)(2,1)}) %all-gather.15.cloned.1.call-update) | async-done | bytes 8388624 | tf_op jit(solution)/shard_map/all_gather | solution.py:115
  536.1 15.9 fusion.101
  552.0 40.4 %all-gather.17.cloned.1.call-done = bf16[2048,2048]{1,0:T(8,128)(2,1)} async-done(((bf16[256,2048]{1,0:T(8,128)(2,1)}), bf16[2048,2048]{1,0:T(8,128)(2,1)}) %all-gather.17.cloned.1.call-update) | async-done | bytes 8388624 | tf_op jit(solution)/shard_map/all_gather | solution.py:116
  592.4 33.8 %convert_reduce_fusion.1 = (f32[2048]{0:T(1024)}, bf16[1024,2048]{1,0:T(8,128)(2,1)S(1)}, f32[1024,2048]{1,0:T(8,128)}) fusion(f32[1024,2048]{1,0:T(8,128)} %fusion.101, f32[2048]{0:T(1024)S(1)} %copy-done.84, bf16[1024,2048]{1,0:T(8,128)(2,1)} %fusion.50, bf16[2048,2048]{1,0:T(8,128)(2,1)} %all-gather.17.cloned.1.call-done), kind=kOutput, calls=%fused_computation.99 | convolution fusion | flops 8747218944 | bytes 33570816 | tf_op jit(solution)/shard_map/dot_general | solution.py:193
  628.1 11.2 fusion.124
  650.6 12.6 convolution_convert_fusion
  663.4 266.9 %all-reduce.20.cloned.1.call-done = f32[1024,2048]{1,0:T(8,128)} async-done(((f32[1024,2048]{1,0:T(8,128)}), f32[1024,2048]{1,0:T(8,128)}) %all-reduce.20.cloned.1.call-update) | async-done | bytes 8388624 | tf_op jit(solution)/shard_map/psum | solution.py:197
  938.3 149.0 %all-reduce.18.cloned.1.call-done = bf16[1024,2048]{1,0:T(8,128)(2,1)} async-done(((bf16[1024,2048]{1,0:T(8,128)(2,1)}), bf16[1024,2048]{1,0:T(8,128)(2,1)}) %all-reduce.18.cloned.1.call-update) | async-done | bytes 4194320 | tf_op jit(solution)/shard_map/psum | solution.py:172
  1111.7 13.7 multiply_reduce_fusion
  1125.4 12.9 multiply_convert_fusion
  1180.2 21.6 reduce-scatter.8.cloned.1.call-done
  1214.1 45.0 %reduce-scatter.10.cloned.1.call-done = f32[2,512,512]{2,1,0:T(8,128)} async-done(((f32[2,1024,512]{2,1,0:T(8,128)}), f32[2,512,512]{2,1,0:T(8,128)}) %reduce-scatter.10.cloned.1.call-update) | async-done | bytes 2097168 | tf_op jit(solution)/shard_map/reduce_scatter | solution.py:237
  1292.3 16.4 fusion.100
  1308.8 15.5 fusion.125
  1346.5 772.3 %all-reduce.24.cloned.1.call-done = (f32[1024,2048]{1,0:T(8,128)}, f32[1024,2048]{1,0:T(8,128)}, f32[1024,2048]{1,0:T(8,128)}) async-done(((f32[1024,2048]{1,0:T(8,128)}, f32[1024,2048]{1,0:T(8,128)}, f32[1024,2048]{1,0:T(8,128)}), (f32[1024,2048]{1,0:T(8,128)}, f32[1024,2048]{1,0:T(8,128)}, f32[1024,2048]{1,0:T(8,128)})) %all-reduce.24.cloned.1.call-update) | async-done | bytes 25165840 | tf_op jit(solution)/shard_map/psum | solution.py:262
  2118.9 15.7 multiply_reduce_fusion.2
  2144.5 11.6 multiply_reduce_fusion.3
  2164.4 18.6 fusion.103
  2207.3 20.8 pad_maximum_fusion
  2228.2 124.8 %fusion = f32[1024,4,4]{2,1,0:T(4,128)S(1)} fusion(f32[4,1024,2048]{2,1,0:T(8,128)} %pad_maximum_fusion, bf16[4,1024,2048]{2,1,0:T(8,128)(2,1)} %bitcast.319), kind=kOutput, calls=%fused_computation.3 | convolution fusion | flops 402653184 | bytes 50397184 | tf_op jit(solution)/shard_map/snd,jnd->nsj/dot_general | solution.py:287
  2366.3 88.2 %fusion.2 = f32[1024,2048,4]{1,2,0:T(4,128)} fusion(f32[1024,4,4]{1,2,0:T(4,128)S(1)} %copy-done.15, f32[4,1024,2048]{2,1,0:T(8,128)} %pad_maximum_fusion), kind=kOutput, calls=%fused_computation.5 | convolution fusion | flops 402653184 | bytes 67174400 | tf_op jit(solution)/shard_map/nsj,snd->jnd/dot_general | solution.py:288
  2454.6 28.6 %copy.189 = f32[1024,2048,4]{1,0,2:T(8,128)S(1)} copy(f32[1024,2048,4]{1,2,0:T(4,128)} %fusion.2) | data formatting | bytes 67108864 | tf_op jit(solution)/shard_map/nsj,snd->jnd/dot_general | solution.py:288
  2483.2 12.2 copy-done.3
  2504.0 18.2 fusion.8
  2522.3 20.8 pad_maximum_fusion.1
  2543.1 26.1 all-reduce.22.cloned.1.call-done
  2569.2 37.4 %reduce-scatter.12.cloned.1.call-done = f32[256,16]{0,1:T(8,128)} async-done(((f32[2048,16]{0,1:T(8,128)}), f32[256,16]{0,1:T(8,128)}) %reduce-scatter.12.cloned.1.call-update) | async-done | bytes 16400 | tf_op jit(solution)/shard_map/reduce_scatter | solution.py:301
  (419 shorter events, 364.4 us)
Async XLA Ops:
  7.2 69.6 %all-gather.7.cloned.1.call-start = ((), (), s32[]{:S(2)}) async-start(), calls=%async_computation.7 | async-start | bytes 7077888 | tf_op jit(solution)/shard_map/all_gather | solution.py:113
  7.9 109.8 %all-gather.9.cloned.1.call-start = ((), (), s32[]{:S(2)}) async-start(), calls=%async_computation.8 | async-start | bytes 3145728 | tf_op jit(solution)/shard_map/all_gather | solution.py:144
  34.5 156.9 %copy-start.36 = (f32[1024,4,4]{0,2,1:T(4,128)}, f32[1024,4,4]{0,2,1:T(4,128)S(1)}, u32[]{:S(2)}) copy-start(f32[1024,4,4]{0,2,1:T(4,128)S(1)} %reshape.1011) | copy-start | bytes 196612
  67.1 468.9 %copy-start.86 = (f32[1,2048]{1,0:T(1,128)}, f32[1,2048]{1,0:T(1,128)S(1)}, u32[]{:S(2)}) copy-start(f32[1,2048]{1,0:T(1,128)S(1)} %get-tuple-element.121) | copy-start | bytes 24580
  83.0 70.1 %all-gather.11.cloned.1.call-start = ((), (), s32[]{:S(2)}) async-start(), calls=%async_computation.9 | async-start | bytes 3145728 | tf_op jit(solution)/shard_map/all_gather | solution.py:143
  97.3 85.4 %all-gather.13.cloned.1.call-start = ((), (), s32[]{:S(2)}) async-start(), calls=%async_computation.10 | async-start | bytes 2359296 | tf_op jit(solution)/shard_map/all_gather | solution.py:114
  97.9 383.0 %all-reduce.16.cloned.1.call-start = ((), (), s32[]{:S(2)}) async-start(), calls=%async_computation.11 | async-start | bytes 16777216 | tf_op jit(solution)/shard_map/psum | solution.py:166
  189.9 291.0 %copy-start.83 = (f32[2048]{0:T(1024)S(1)}, f32[2048]{0:T(1024)}, u32[]{:S(2)}) copy-start(f32[2048]{0:T(1024)} %param.29) | copy-start | bytes 24580
  189.9 346.1 %all-gather.15.cloned.1.call-start = ((), (), s32[]{:S(2)}) async-start(), calls=%async_computation.12 | async-start | bytes 9437184 | tf_op jit(solution)/shard_map/all_gather | solution.py:115
  190.5 401.9 %all-gather.17.cloned.1.call-start = ((), (), s32[]{:S(2)}) async-start(), calls=%async_computation.13 | async-start | bytes 9437184 | tf_op jit(solution)/shard_map/all_gather | solution.py:116
  191.3 739.1 %all-reduce.20.cloned.1.call-start = ((), (), s32[]{:S(2)}) async-start(), calls=%async_computation.15 | async-start | bytes 16777216 | tf_op jit(solution)/shard_map/psum | solution.py:197
  191.4 300.9 %copy-start.61 = (pred[2,512]{1,0:T(4,128)(4,1)}, pred[2,512]{1,0:T(4,128)(4,1)S(1)}, u32[]{:S(2)}) copy-start(pred[2,512]{1,0:T(4,128)(4,1)S(1)} %broadcast_compare_fusion) | copy-start | bytes 3076
  191.4 289.5 %copy-start.81 = (pred[1024]{0:T(1024)(128)(4,1)}, pred[1024]{0:T(1024)(128)(4,1)S(1)}, u32[]{:S(2)}) copy-start(pred[1024]{0:T(1024)(128)(4,1)S(1)} %lt.45) | copy-start | bytes 3076
  639.3 448.0 %all-reduce.18.cloned.1.call-start = ((), (), s32[]{:S(2)}) async-start(), calls=%async_computation.14 | async-start | bytes 8388608 | tf_op jit(solution)/shard_map/psum | solution.py:172
  663.2 424.1 %copy-start.85 = (f32[2048]{0:T(1024)S(1)}, f32[2048]{0:T(1024)}, u32[]{:S(2)}) copy-start(f32[2048]{0:T(1024)} %param.33) | copy-start | bytes 24580
  663.2 538.6 %reduce-scatter.8.cloned.1.call-start = ((), (), s32[]{:S(2)}) async-start(), calls=%async_computation.16 | async-start | bytes 6291456 | tf_op jit(solution)/shard_map/reduce_scatter | solution.py:231
  938.3 159.9 %copy-start.82 = (pred[1024]{0:T(1024)(128)(4,1)S(1)}, pred[1024]{0:T(1024)(128)(4,1)}, u32[]{:S(2)}) copy-start(pred[1024]{0:T(1024)(128)(4,1)} %copy-done.81) | copy-start | bytes 3076
  1148.3 110.7 %reduce-scatter.10.cloned.1.call-start = ((), (), s32[]{:S(2)}) async-start(), calls=%async_computation.17 | async-start | bytes 6291456 | tf_op jit(solution)/shard_map/reduce_scatter | solution.py:237
  1164.0 954.8 %all-reduce.24.cloned.1.call-start = ((), (), s32[]{:S(2)}) async-start(), calls=%async_computation.24 | async-start | bytes 50331648 | tf_op jit(solution)/shard_map/psum | solution.py:262
  1283.2 1259.8 %reduce-scatter.16.cloned.1.call-start = ((), (), s32[]{:S(2)}) async-start(), calls=%async_computation.20 | async-start | bytes 4718592 | tf_op jit(solution)/shard_map/reduce_scatter | solution.py:303
  1292.3 1250.8 %reduce-scatter.18.cloned.1.call-start = ((), (), s32[]{:S(2)}) async-start(), calls=%async_computation.21 | async-start | bytes 18874368 | tf_op jit(solution)/shard_map/reduce_scatter | solution.py:304
  1308.7 1234.3 %reduce-scatter.20.cloned.1.call-start = ((), (), s32[]{:S(2)}) async-start(), calls=%async_computation.22 | async-start | bytes 18874368 | tf_op jit(solution)/shard_map/reduce_scatter | solution.py:305
  1324.3 1218.7 %reduce-scatter.14.cloned.1.call-start = ((), (), s32[]{:S(2)}) async-start(), calls=%async_computation.19 | async-start | bytes 14155776 | tf_op jit(solution)/shard_map/reduce_scatter | solution.py:302
  1345.4 773.5 %copy-start.49 = (f32[1,2048]{1,0:T(1,128)S(1)}, f32[1,2048]{1,0:T(1,128)}, u32[]{:S(2)}) copy-start(f32[1,2048]{1,0:T(1,128)} %copy-done.48) | copy-start | bytes 24580
  1345.4 773.5 %copy-start.71 = (f32[1024,1,1]{0,2,1:T(1,128)S(1)}, f32[1024,1,1]{0,2,1:T(1,128)}, u32[]{:S(2)}) copy-start(f32[1024,1,1]{0,2,1:T(1,128)} %get-tuple-element.107) | copy-start | bytes 12292
  1345.4 773.5 %copy-start.72 = (f32[1024,1,1]{0,2,1:T(1,128)S(1)}, f32[1024,1,1]{0,2,1:T(1,128)}, u32[]{:S(2)}) copy-start(f32[1024,1,1]{0,2,1:T(1,128)} %get-tuple-element.108) | copy-start | bytes 12292
  1345.4 773.5 %copy-start.73 = (f32[1024,1,1]{0,2,1:T(1,128)S(1)}, f32[1024,1,1]{0,2,1:T(1,128)}, u32[]{:S(2)}) copy-start(f32[1024,1,1]{0,2,1:T(1,128)} %get-tuple-element.109) | copy-start | bytes 12292
  1345.4 773.5 %copy-start.74 = (f32[1024,1,1]{0,2,1:T(1,128)S(1)}, f32[1024,1,1]{0,2,1:T(1,128)}, u32[]{:S(2)}) copy-start(f32[1024,1,1]{0,2,1:T(1,128)} %get-tuple-element.110) | copy-start | bytes 12292
  1345.4 1223.8 %all-reduce.22.cloned.1.call-start = ((), (), s32[]{:S(2)}) async-start(), calls=%async_computation.23 | async-start | bytes 229376 | tf_op jit(solution)/shard_map/psum | solution.py:307
  2228.2 131.1 %copy-start.51 = (bf16[2048,16]{0,1:T(8,128)(2,1)S(1)}, bf16[2048,16]{0,1:T(8,128)(2,1)}, u32[]{:S(2)}) copy-start(bf16[2048,16]{0,1:T(8,128)(2,1)} %copy-done.50) | copy-start | bytes 196612
  2228.2 131.1 %copy-start.53 = (f32[1024]{0:T(1024)S(1)}, f32[1024]{0:T(1024)}, u32[]{:S(2)}) copy-start(f32[1024]{0:T(1024)} %copy-done.52) | copy-start | bytes 12292
  2454.5 152.1 %reduce-scatter.12.cloned.1.call-start = ((), (), s32[]{:S(2)}) async-start(), calls=%async_computation.18 | async-start | bytes 147456 | tf_op jit(solution)/shard_map/reduce_scatter | solution.py:301
  (95 other events, 1710.9 us)
Sparse Core Ops, SparseCore 0:
  9.9 48.3 all-gather.6
  83.1 34.6 all-gather.8
  119.9 33.1 all-gather.10
  154.8 27.8 all-gather.12
  190.1 290.8 all-reduce.15
  482.6 53.3 all-gather.14
  538.0 54.3 all-gather.16
  639.5 290.8 all-reduce.19
  933.3 153.9 all-reduce.17
  1148.4 53.3 reduce-scatter.7
  1204.7 54.3 reduce-scatter.9
  1283.3 835.4 all-reduce.23
  2122.8 50.1 reduce-scatter.15
  2177.4 115.9 reduce-scatter.17
  2297.8 115.9 reduce-scatter.19
  2418.1 92.3 reduce-scatter.13
  2516.0 53.1 all-reduce.21
  2572.6 33.9 reduce-scatter.11
where the time goes:
time: 2630 us; the launch traced here: 2620 us
  waiting for transfers between devices  1740 us (66%)
  matrix products  445 us (17%)
  other arithmetic  272 us (10%)
  local copies, waits for them, and re-layouts  138 us (5%)
    psum x1, waiting for transfers between devices, shards(): lax.psum((col_product(grad_lin[0], qkv_again[0]), col_product(grad_lin[1]...  772 us
    psum x1, waiting for transfers between devices, shards(): hidden = combined[3] + (lax.psum(attn_part, 'tensor') + out_bias)  284 us
    psum x1, waiting for transfers between devices, shards(): grad_mlp_in = lax.psum(col_product(grad_up, up_again), 'tensor')  267 us
    psum x1, waiting for transfers between devices, shards(): lax.psum(down_part.astype(jnp.bfloat16), 'tensor').astype(jnp.float32)  149 us
    dot_general x1, matrix products, shards(): jnp.einsum('snd,jnd->nsj', grad_stack, layers_wide, precision=EXACT)  125 us
    dot_general x1, matrix products, shards(): jnp.einsum('nsj,snd->jnd', mix_weights, grad_stack, precision=EXACT)  88.2 us
    reduce_sum x6, other arithmetic, layer_norm(): centred = values - jnp.mean(values, axis=-1, keepdims=True)  69.8 us
    dot_general x7, matrix products, col_product(): lax.dot_general(left, right, (((1,), (1,)), ((), ())), preferred_element_...  60.2 us
  transfers between devices with their start and end apart: 18, of which 13 were waited for; matrix products, arithmetic and copies ran while one was open for 25% of the time, Pallas kernels for 0%

commit v1 on v0

v1 whole, which is shorter than its diff:
```python
import functools
import math

import jax
import jax.numpy as jnp
from jax import lax
from jax.experimental import pallas as pl
from jax.experimental.pallas import tpu as pltpu
from jax.sharding import PartitionSpec as P

HEAD_DIM = 128
ROT = 32
STREAMS = 4
EXACT = lax.Precision.HIGHEST
RMS_EPSILON = 1e-06
NORM_EPSILON = 1e-05
BF = jnp.bfloat16
F32 = jnp.float32
MESH = pl.DeviceIdType.MESH
ANY = pl.BlockSpec(memory_space=pl.ANY)
VMEM = pl.BlockSpec(memory_space=pltpu.VMEM)
RING = 4
NN = (((1,), (0,)), ((), ()))
NT = (((1,), (1,)), ((), ()))
TN = (((0,), (0,)), ((), ()))


def dot(left, right, dims=NN, precision=None):
    return lax.dot_general(left, right, dims, precision=precision, preferred_element_type=F32)


def normal_cdf(values):
    return 0.5 * (1.0 + lax.erf(values * math.sqrt(0.5)))


def gelu_slope(values, cdf):
    return cdf + values * (jnp.exp(-0.5 * values * values) * (1.0 / math.sqrt(2.0 * math.pi)))


def mean_last(values):
    return jnp.mean(values, axis=-1, keepdims=True)


def rows_loop(total, step, body):
    def one(index, carry):
        body(pl.ds(pl.multiple_of(index * step, step), step))
        return carry

    lax.fori_loop(0, total // step, one, 0)


def params(limit_mib, collective_id=None):
    if collective_id is None:
        return pltpu.CompilerParams(vmem_limit_bytes=limit_mib << 20)
    return pltpu.CompilerParams(
        vmem_limit_bytes=limit_mib << 20, collective_id=collective_id, has_side_effects=True
    )


def cost(micros):
    return pl.CostEstimate(flops=0, bytes_accessed=int(micros * 3.0e6), transcendentals=0)


def front_kernel(hist, gain, w1, w2, lg, lb, normed_out, resid_out, mix_out, pre_out, scratch):
    depth, rows, _ = hist.shape

    def rms(part):
        wide = hist[depth - 1, part, :].astype(F32)
        scale = lax.rsqrt(mean_last(wide * wide) + RMS_EPSILON)
        scratch[part, :] = (wide * scale * gain[...]).astype(BF)

    rows_loop(rows, 16, rms)
    pre = dot(scratch[...], w1[...])
    pre_out[...] = pre
    mix_out[...] = dot(pre * normal_cdf(pre), w2[...], precision=EXACT)

    def combine(part):
        layers = [hist[j, part, :].astype(F32) for j in range(depth)]
        mix = mix_out[part, :]
        for m in range(STREAMS):
            running = layers[depth - 1]
            for j in range(depth):
                running = running + mix[:, m * depth + j : m * depth + j + 1] * layers[j]
            if m == STREAMS - 1:
                resid_out[part, :] = running
            else:
                centred = running - mean_last(running)
                inverse = lax.rsqrt(mean_last(centred * centred) + NORM_EPSILON)
                normed = centred * inverse * lg[m : m + 1, :] + lb[m : m + 1, :]
                normed_out[m, part, :] = normed.astype(BF)

    rows_loop(rows, 16, combine)


def front(layers, gain, w1, w2, lg, lb):
    depth, rows, feats = layers.shape
    tile = min(128, rows)
    hidden = w1.shape[1]
    full = lambda shape: pl.BlockSpec(shape, lambda i: (0,) * len(shape))
    return pl.pallas_call(
        front_kernel,
        grid=(rows // tile,),
        in_specs=[
            pl.BlockSpec((depth, tile, feats), lambda i: (0, i, 0)),
            full((1, feats)),
            full(w1.shape),
            full(w2.shape),
            full(lg.shape),
            full(lb.shape),
        ],
        out_specs=[
            pl.BlockSpec((3, tile, feats), lambda i: (0, i, 0)),
            pl.BlockSpec((tile, feats), lambda i: (i, 0)),
            pl.BlockSpec((tile, STREAMS * depth), lambda i: (i, 0)),
            pl.BlockSpec((tile, hidden), lambda i: (i, 0)),
        ],
        out_shape=[
            jax.ShapeDtypeStruct((3, rows, feats), BF),
            jax.ShapeDtypeStruct((rows, feats), F32),
            jax.ShapeDtypeStruct((rows, STREAMS * depth), F32),
            jax.ShapeDtypeStruct((rows, hidden), F32),
        ],
        scratch_shapes=[pltpu.VMEM((tile, feats), BF)],
        compiler_params=params(40),
        cost_estimate=cost(20),
        name="front",
    )(layers, gain.reshape(1, feats), w1, w2, lg, lb)


def turn(values, tables, sign):
    cosines, low, high = tables
    return values * cosines + sign * (
        pltpu.roll(values, HEAD_DIM - ROT // 2, 1) * low + pltpu.roll(values, ROT // 2, 1) * high
    )


def rotary_tables(positions):
    exponents = jnp.arange(0, ROT, 2).astype(F32) / ROT
    inverse = jnp.power(10000.0, -exponents)
    phases = positions.astype(F32)[:, None] * inverse[None, :]
    cosines, sines = jnp.cos(phases), jnp.sin(phases)
    rows, half = phases.shape
    ones = jnp.ones((rows, HEAD_DIM - 2 * half), F32)
    none = jnp.zeros((rows, HEAD_DIM - 2 * half), F32)
    zero = jnp.zeros((rows, half), F32)
    return jnp.stack(
        [
            jnp.concatenate([cosines, cosines, ones], axis=1),
            jnp.concatenate([-sines, zero, none], axis=1),
            jnp.concatenate([zero, sines, none], axis=1),
        ]
    )


def proj_kernel(first, lhs, weight, bias, tables, out):
    branch = pl.program_id(0) + first
    value = dot(lhs[0], weight[...]) + bias[0]

    @pl.when(branch < 2)
    def _():
        tabs = (tables[0], tables[1], tables[2])
        for head in range(value.shape[1] // HEAD_DIM):
            cols = slice(head * HEAD_DIM, (head + 1) * HEAD_DIM)
            out[0, :, cols] = turn(value[:, cols], tabs, 1.0).astype(BF)

    @pl.when(branch >= 2)
    def _():
        out[0] = value.astype(BF)


def project(normed, weight, bias, tables, first):
    _, rows, feats = normed.shape
    count, width = bias.shape
    tile = min(256, rows)
    return pl.pallas_call(
        functools.partial(proj_kernel, first),
        grid=(count, rows // tile),
        in_specs=[
            pl.BlockSpec((1, tile, feats), lambda b, r: (b + first, r, 0)),
            pl.BlockSpec((feats, width), lambda b, r: (0, b)),
            pl.BlockSpec((1, 1, width), lambda b, r: (b, 0, 0)),
            pl.BlockSpec((3, tile, HEAD_DIM), lambda b, r: (0, r, 0)),
        ],
        out_specs=pl.BlockSpec((1, tile, width), lambda b, r: (b, r, 0)),
        out_shape=jax.ShapeDtypeStruct((count, rows, width), BF),
        compiler_params=params(40),
        cost_estimate=cost(4 * count),
        name="project",
    )(normed, weight, bias.reshape(count, 1, width), tables)


def attend_kernel(scalars, q, k, v, out):
    keys = k[...].reshape(-1, HEAD_DIM)
    values = v[...].reshape(-1, HEAD_DIM)
    length = scalars[pl.program_id(0)]
    offset = scalars[pl.num_programs(0)]
    scores = dot(q[0], keys, NT) * (1.0 / math.sqrt(HEAD_DIM))
    key_place = lax.broadcasted_iota(jnp.int32, scores.shape, 1)
    query_place = lax.broadcasted_iota(jnp.int32, scores.shape, 0) + offset
    scores = jnp.where((key_place <= query_place) & (key_place < length), scores, -1e30)
    weights = jnp.exp(scores - jnp.max(scores, axis=-1, keepdims=True))
    total = jnp.sum(weights, axis=-1, keepdims=True)
    probs = (weights * (1.0 / total)).astype(BF)
    out[0] = dot(probs, values).astype(BF)


def attend(scalars, q, kv, heads):
    seqs, _, slots, length, width = kv.shape
    block = (1, length, HEAD_DIM)
    return pl.pallas_call(
        attend_kernel,
        grid_spec=pltpu.PrefetchScalarGridSpec(
            num_scalar_prefetch=1,
            grid=(slots, heads),
            in_specs=[
                pl.BlockSpec(block, lambda s, h, _: (s, 0, h)),
                pl.BlockSpec((seqs, 1, 1, length, HEAD_DIM), lambda s, h, _: (0, 0, s, 0, h)),
                pl.BlockSpec((seqs, 1, 1, length, HEAD_DIM), lambda s, h, _: (0, 1, s, 0, h)),
            ],
            out_specs=pl.BlockSpec(block, lambda s, h, _: (s, 0, h)),
        ),
        out_shape=jax.ShapeDtypeStruct((slots, length, width), BF),
        compiler_params=params(40),
        cost_estimate=cost(15),
        name="attend",
    )(scalars, q.reshape(slots, length, width), kv, kv)


def attend_back_kernel(scalars, q, k, v, g, tables, dq_out, dkv_out):
    seqs = k.shape[0]
    scaling = 1.0 / math.sqrt(HEAD_DIM)
    keys = k[...].reshape(-1, HEAD_DIM)
    values = v[...].reshape(-1, HEAD_DIM)
    length = scalars[pl.program_id(0)]
    offset = scalars[pl.num_programs(0)]
    queries, grads = q[0], g[0]
    scores = dot(keys, queries, NT) * scaling
    key_place = lax.broadcasted_iota(jnp.int32, scores.shape, 0)
    query_place = lax.broadcasted_iota(jnp.int32, scores.shape, 1) + offset
    scores = jnp.where((key_place <= query_place) & (key_place < length), scores, -1e30)
    weights = jnp.exp(scores - jnp.max(scores, axis=0, keepdims=True))
    probs = weights * (1.0 / jnp.sum(weights, axis=0, keepdims=True))
    grad_probs = dot(values, grads, NT)
    mixed = jnp.sum(probs * grad_probs, axis=0, keepdims=True)
    grad_scores = (probs * (grad_probs - mixed)).astype(BF)
    grad_values = dot(probs.astype(BF), grads)
    grad_keys = dot(grad_scores, queries) * scaling
    shape = (seqs, -1, HEAD_DIM)
    dkv_out[:, 0, 0] = grad_keys.astype(BF).reshape(shape)
    dkv_out[:, 1, 0] = grad_values.astype(BF).reshape(shape)
    grad_queries = dot(grad_scores, keys, TN) * scaling
    tabs = (tables[0], tables[1], tables[2])
    dq_out[0] = turn(grad_queries, tabs, -1.0).astype(BF)


def attend_back(scalars, q, kv, g, tables, heads):
    seqs, _, slots, length, width = kv.shape
    block = (1, length, HEAD_DIM)
    own = pl.BlockSpec(block, lambda s, h, _: (s, 0, h))
    return pl.pallas_call(
        attend_back_kernel,
        grid_spec=pltpu.PrefetchScalarGridSpec(
            num_scalar_prefetch=1,
            grid=(slots, heads),
            in_specs=[
                own,
                pl.BlockSpec((seqs, 1, 1, length, HEAD_DIM), lambda s, h, _: (0, 0, s, 0, h)),
                pl.BlockSpec((seqs, 1, 1, length, HEAD_DIM), lambda s, h, _: (0, 1, s, 0, h)),
                own,
                pl.BlockSpec((3, length, HEAD_DIM), lambda s, h, _: (0, s, 0)),
            ],
            out_specs=[
                own,
                pl.BlockSpec((seqs, 2, 1, length, HEAD_DIM), lambda s, h, _: (0, 0, s, 0, h)),
            ],
        ),
        out_shape=[
            jax.ShapeDtypeStruct((slots, length, width), BF),
            jax.ShapeDtypeStruct((seqs, 2, slots, length, width), BF),
        ],
        compiler_params=params(48),
        cost_estimate=cost(25),
        name="attend_back",
    )(scalars, q.reshape(slots, length, width), kv, kv, g.reshape(slots, length, width), tables)


class Ring:
    def __init__(self, chunk):
        me = lax.axis_index("tensor")
        self.chunk, self.half = chunk, chunk // 2
        self.me = me
        self.right = lax.rem(me + 1, RING)
        self.left = lax.rem(me + RING - 1, RING)
        self.far = lax.rem(me + 2, RING)

    def at(self, index, shift=0):
        return pl.multiple_of(index * self.chunk + shift, self.half)

    def barrier(self):
        gate = pltpu.get_barrier_semaphore()
        for near in (self.left, self.right):
            pl.semaphore_signal(gate, inc=1, device_id={"tensor": near}, device_id_type=MESH)
        pl.semaphore_wait(gate, 2)


def remote(source, target, sems, index, device):
    return pltpu.make_async_remote_copy(
        src_ref=source,
        dst_ref=target,
        send_sem=sems.at[0, index],
        recv_sem=sems.at[1, index],
        device_id={"tensor": device},
        device_id_type=MESH,
    )


def product(lhs, rhs, start, count, write, step=512):
    total = rhs.shape[0]

    def one(cols):
        write(cols, dot(lhs[pl.ds(start, count), :], rhs[cols, :], NT))

    rows_loop(total, min(step, total), one)


class Scatter:
    def __init__(self, ring, lhs, rhs, far, near, far_in, near_in, sems):
        self.ring, self.lhs, self.rhs = ring, lhs, rhs
        self.far, self.near, self.far_in, self.near_in = far, near, far_in, near_in
        half = ring.half
        up, down = pl.ds(0, half), pl.ds(half, half)
        self.copies = [
            remote(far.at[0], far_in.at[0], sems, 0, ring.right),
            remote(far.at[1], far_in.at[1], sems, 1, ring.left),
            remote(near.at[0, down], near_in.at[0, down], sems, 2, ring.right),
            remote(near.at[1, up], near_in.at[1, up], sems, 3, ring.left),
            remote(near.at[0, up], near_in.at[0, up], sems, 4, ring.right),
            remote(near.at[1, down], near_in.at[1, down], sems, 5, ring.left),
        ]

    def begin(self):
        ring, half = self.ring, self.ring.half

        def far_half(which):
            def write(cols, value):
                self.far[which, :, cols] = value.astype(BF)

            product(self.lhs, self.rhs, ring.at(ring.far, which * half), half, write)
            self.copies[which].start()

        def near_half(which, device, part, copy):
            def write(cols, value):
                self.near[which, pl.ds(part * half, half), cols] = value.astype(BF)

            product(self.lhs, self.rhs, ring.at(device, part * half), half, write)
            self.copies[copy].start()

        far_half(0)
        far_half(1)
        near_half(0, ring.right, 1, 2)
        near_half(1, ring.left, 0, 3)

    def relay(self):
        ring, half = self.ring, self.ring.half

        def add_half(which, device, part, copy):
            self.copies[which].wait_recv()

            def write(cols, value):
                arrived = self.far_in[which, :, cols].astype(F32)
                self.near[which, pl.ds(part * half, half), cols] = (value + arrived).astype(BF)

            product(self.lhs, self.rhs, ring.at(device, part * half), half, write)
            self.copies[copy].start()

        add_half(0, ring.right, 0, 4)
        add_half(1, ring.left, 1, 5)

    def arrive(self):
        for copy in self.copies[2:]:
            copy.wait_recv()

    def finish(self):
        for copy in self.copies:
            copy.wait_send()


class Gather:
    def __init__(self, ring, own, out, sems, base, local_sem):
        half = ring.half

        def rows(index, shift=0, count=ring.chunk):
            return out.at[pl.ds(ring.at(index, shift), count), :]

        mine = rows(ring.me)
        self.local = pltpu.make_async_copy(own, mine, local_sem)
        self.first = [
            remote(own, mine, sems, base, ring.right),
            remote(own, mine, sems, base + 1, ring.left),
        ]
        up, down = rows(ring.left, 0, half), rows(ring.right, half, half)
        self.second = [
            remote(up, up, sems, base + 2, ring.right),
            remote(down, down, sems, base + 3, ring.left),
        ]

    def begin(self):
        for copy in self.first:
            copy.start()
        self.local.start()

    def relay(self):
        for arrived, onward in zip(self.first, self.second):
            arrived.wait_recv()
            onward.start()

    def finish(self):
        for copy in self.second:
            copy.wait_recv()
        for copy in self.first + self.second:
            copy.wait_send()
        self.local.wait()


def scatter_scratch(chunk, feats, count=1):
    half = chunk // 2
    lead = () if count == 1 else (count,)
    return [
        pltpu.VMEM(lead + (2, half, feats), BF),
        pltpu.VMEM(lead + (2, chunk, feats), BF),
        pltpu.VMEM(lead + (2, half, feats), BF),
        pltpu.VMEM(lead + (2, chunk, feats), BF),
    ]


def own_sum(scatter, total):
    ring = scatter.ring

    def write(cols, value):
        total[:, cols] = value

    product(scatter.lhs, scatter.rhs, ring.at(ring.me), ring.chunk, write)


def whole_sum(scatter, total, part):
    near = scatter.near_in
    return total[part, :] + near[0, part, :].astype(F32) + near[1, part, :].astype(F32)


def attn_out_kernel(
    lhs, rhs, resid, bias, lg, lb, hidden_out, mlp_out,
    far, near, far_in, near_in, total, base_rows, own, sems, local_sems,
):
    chunk, feats = total.shape
    ring = Ring(chunk)
    fetch = pltpu.make_async_copy(
        resid.at[pl.ds(ring.at(ring.me), chunk), :], base_rows, local_sems.at[0]
    )
    fetch.start()
    ring.barrier()
    scatter = Scatter(ring, lhs, rhs, far, near, far_in, near_in, sems)
    scatter.begin()
    scatter.relay()
    own_sum(scatter, total)
    fetch.wait()
    scatter.arrive()

    def norm(part):
        value = base_rows[part, :] + (whole_sum(scatter, total, part) + bias[...])
        hidden_out[part, :] = value
        centred = value - mean_last(value)
        inverse = lax.rsqrt(mean_last(centred * centred) + NORM_EPSILON)
        own[part, :] = (centred * inverse * lg[...] + lb[...]).astype(BF)

    rows_loop(chunk, 16, norm)
    gather = Gather(ring, own, mlp_out, sems, 6, local_sems.at[1])
    gather.begin()
    gather.relay()
    scatter.finish()
    gather.finish()


def attn_out(lhs, rhs, resid, bias, lg, lb):
    rows, feats = resid.shape
    chunk = rows // RING
    return pl.pallas_call(
        attn_out_kernel,
        in_specs=[VMEM, VMEM, ANY, VMEM, VMEM, VMEM],
        out_specs=[VMEM, ANY],
        out_shape=[
            jax.ShapeDtypeStruct((chunk, feats), F32),
            jax.ShapeDtypeStruct((rows, feats), BF),
        ],
        scratch_shapes=scatter_scratch(chunk, feats)
        + [
            pltpu.VMEM((chunk, feats), F32),
            pltpu.VMEM((chunk, feats), F32),
            pltpu.VMEM((chunk, feats), BF),
            pltpu.SemaphoreType.DMA((2, 10)),
            pltpu.SemaphoreType.DMA((2,)),
        ],
        compiler_params=params(48, 0),
        cost_estimate=cost(80),
        name="attn_out",
    )(lhs, rhs, resid, bias, lg, lb)


def norm_back(values, grads, gain):
    centred = values - mean_last(values)
    inverse = lax.rsqrt(mean_last(centred * centred) + NORM_EPSILON)
    normed = centred * inverse
    inner = grads * gain
    back = inverse * (inner - mean_last(inner) - normed * mean_last(inner * normed))
    return back, normed


def fold(values):
    rows, feats = values.shape
    return jnp.sum(values.reshape(rows // 8, 8, feats), axis=0)


def mlp_back_kernel(
    lhs, rhs, hidden, cot, lg, grad_out, small_out,
    far, near, far_in, near_in, total, cot_rows, own, sums, sems, local_sems,
):
    chunk, feats = total.shape
    ring = Ring(chunk)
    fetch = pltpu.make_async_copy(
        cot.at[pl.ds(ring.at(ring.me), chunk), :], cot_rows, local_sems.at[0]
    )
    fetch.start()
    ring.barrier()
    scatter = Scatter(ring, lhs, rhs, far, near, far_in, near_in, sems)
    scatter.begin()
    scatter.relay()
    own_sum(scatter, total)
    fetch.wait()
    sums[...] = jnp.zeros_like(sums)
    scatter.arrive()

    def back(part):
        grads = whole_sum(scatter, total, part)
        step, normed = norm_back(hidden[part, :], grads, lg[...])
        low = (cot_rows[part, :].astype(F32) + step).astype(BF)
        own[part, :] = low
        sums[0] += fold(grads * normed)
        sums[1] += fold(grads)
        sums[2] += fold(low.astype(F32))

    rows_loop(chunk, 16, back)
    gather = Gather(ring, own, grad_out, sems, 6, local_sems.at[1])
    gather.begin()
    for i in range(3):
        small_out[i : i + 1, :] = jnp.sum(sums[i], axis=0, keepdims=True)
    gather.relay()
    scatter.finish()
    gather.finish()


def mlp_back(lhs, rhs, hidden, cot, lg):
    rows, feats = cot.shape
    chunk = rows // RING
    return pl.pallas_call(
        mlp_back_kernel,
        in_specs=[VMEM, VMEM, VMEM, ANY, VMEM],
        out_specs=[ANY, VMEM],
        out_shape=[
            jax.ShapeDtypeStruct((rows, feats), BF),
            jax.ShapeDtypeStruct((3, feats), F32),
        ],
        scratch_shapes=scatter_scratch(chunk, feats)
        + [
            pltpu.VMEM((chunk, feats), F32),
            pltpu.VMEM((chunk, feats), BF),
            pltpu.VMEM((chunk, feats), BF),
            pltpu.VMEM((3, 8, feats), F32),
            pltpu.SemaphoreType.DMA((2, 10)),
            pltpu.SemaphoreType.DMA((2,)),
        ],
        compiler_params=params(52, 1),
        cost_estimate=cost(80),
        name="mlp_back",
    )(lhs, rhs, hidden, cot, lg)


def streams_back_kernel(
    lhs, rhs_q, rhs_kv, hist, mix, lg, grads_out, small_out,
    far, near, far_in, near_in, total, layers, mix_rows, own, sums, sems, local_sems,
):
    chunk, feats = total.shape
    depth = layers.shape[0]
    width = lhs.shape[2]
    ring = Ring(chunk)
    mine = pl.ds(ring.at(ring.me), chunk)
    fetch = pltpu.make_async_copy(hist.at[:, mine, :], layers, local_sems.at[0])
    fetch.start()
    fetch_mix = pltpu.make_async_copy(mix.at[mine, :], mix_rows, local_sems.at[1])
    fetch_mix.start()
    ring.barrier()
    weights = [
        rhs_q,
        rhs_kv.at[:, pl.ds(0, width)],
        rhs_kv.at[:, pl.ds(width, width)],
    ]
    scatters = [
        Scatter(
            ring, lhs.at[i], weights[i], far.at[i], near.at[i], far_in.at[i], near_in.at[i],
            sems.at[i],
        )
        for i in range(3)
    ]
    gathers = [
        Gather(ring, own.at[i], grads_out.at[i], sems.at[i], 6, local_sems.at[2 + i])
        for i in range(3)
    ]
    for scatter in scatters:
        scatter.begin()
    sums[...] = jnp.zeros_like(sums)
    fetch.wait()
    fetch_mix.wait()
    for i, scatter in enumerate(scatters):
        scatter.relay()
    for i, scatter in enumerate(scatters):
        own_sum(scatter, total)
        scatter.arrive()

        def back(part):
            grads = whole_sum(scatter, total, part)
            running = layers[depth - 1, part, :].astype(F32)
            weight = mix_rows[part, :]
            mixture = running
            for j in range(depth):
                at = i * depth + j
                mixture = mixture + weight[:, at : at + 1] * layers[j, part, :].astype(F32)
            step, normed = norm_back(mixture, grads, lg[i : i + 1, :])
            own[i, part, :] = step.astype(BF)
            sums[i, 0] += fold(grads * normed)
            sums[i, 1] += fold(grads)

        rows_loop(chunk, 16, back)
        gathers[i].begin()
        if i:
            gathers[i - 1].relay()
    for i in range(3):
        for j in range(2):
            small_out[j, i : i + 1, :] = jnp.sum(sums[i, j], axis=0, keepdims=True)
    gathers[2].relay()
    for scatter, gather in zip(scatters, gathers):
        scatter.finish()
        gather.finish()


def streams_back(lhs, rhs_q, rhs_kv, hist, mix, lg):
    depth, rows, feats = hist.shape
    chunk = rows // RING
    return pl.pallas_call(
        streams_back_kernel,
        in_specs=[VMEM, VMEM, VMEM, ANY, ANY, VMEM],
        out_specs=[ANY, VMEM],
        out_shape=[
            jax.ShapeDtypeStruct((3, rows, feats), BF),
            jax.ShapeDtypeStruct((2, 3, feats), F32),
        ],
        scratch_shapes=scatter_scratch(chunk, feats, 3)
        + [
            pltpu.VMEM((chunk, feats), F32),
            pltpu.VMEM((depth, chunk, feats), BF),
            pltpu.VMEM((chunk, mix.shape[1]), F32),
            pltpu.VMEM((3, chunk, feats), BF),
            pltpu.VMEM((3, 2, 8, feats), F32),
            pltpu.SemaphoreType.DMA((3, 2, 10)),
            pltpu.SemaphoreType.DMA((5,)),
        ],
        compiler_params=params(58, 2),
        cost_estimate=cost(220),
        name="streams_back",
    )(lhs, rhs_q, rhs_kv, hist, mix, lg)


def mlp_kernel(mlp_in, cot, up, down, bias, act_out, grad_out, sum_out):
    lin = dot(mlp_in[...], up[...]) + bias[...]
    grad_act = dot(cot[...], down[...])
    cdf = normal_cdf(lin)
    act_out[...] = (lin * cdf).astype(BF)
    grad = (grad_act * gelu_slope(lin, cdf)).astype(BF)
    grad_out[...] = grad

    @pl.when(pl.program_id(1) == 0)
    def _():
        sum_out[...] = jnp.zeros_like(sum_out)

    sum_out[...] += jnp.sum(grad.astype(F32), axis=0, keepdims=True)


def mlp(mlp_in, cot, up, down, bias):
    rows, feats = mlp_in.shape
    width = up.shape[1]
    tile, cols = min(256, rows), 512
    return pl.pallas_call(
        mlp_kernel,
        grid=(width // cols, rows // tile),
        in_specs=[
            pl.BlockSpec((tile, feats), lambda n, r: (r, 0)),
            pl.BlockSpec((tile, feats), lambda n, r: (r, 0)),
            pl.BlockSpec((feats, cols), lambda n, r: (0, n)),
            pl.BlockSpec((feats, cols), lambda n, r: (0, n)),
            pl.BlockSpec((1, cols), lambda n, r: (0, n)),
        ],
        out_specs=[
            pl.BlockSpec((tile, cols), lambda n, r: (r, n)),
            pl.BlockSpec((tile, cols), lambda n, r: (r, n)),
            pl.BlockSpec((1, cols), lambda n, r: (0, n)),
        ],
        out_shape=[
            jax.ShapeDtypeStruct((rows, width), BF),
            jax.ShapeDtypeStruct((rows, width), BF),
            jax.ShapeDtypeStruct((1, width), F32),
        ],
        compiler_params=params(48),
        cost_estimate=cost(25),
        name="mlp",
    )(mlp_in, cot, up, down, bias)


def turn_back_kernel(dkv, tables, dk_out, sum_out):
    tabs = (tables[0], tables[1], tables[2])
    for head in range(dk_out.shape[1] // HEAD_DIM):
        cols = slice(head * HEAD_DIM, (head + 1) * HEAD_DIM)
        dk_out[:, cols] = turn(dkv[0, :, cols].astype(F32), tabs, -1.0).astype(BF)


def last_kernel(
    hist, streams, attn, mix, pre, gain, w1, w2, grad_out, gain_out, w1_out, w2_out,
    normed, grad_mix, grad_normed, gain_sum,
):
    depth, rows, feats = hist.shape
    step_index = pl.program_id(0)

    @pl.when(step_index == 0)
    def _():
        gain_sum[...] = jnp.zeros_like(gain_sum)
        w1_out[...] = jnp.zeros_like(w1_out)
        w2_out[...] = jnp.zeros_like(w2_out)

    def reduce(part):
        layers = [hist[j, part, :].astype(F32) for j in range(depth)]
        latest = layers[depth - 1]
        scale = lax.rsqrt(mean_last(latest * latest) + RMS_EPSILON)
        normed[part, :] = (latest * scale * gain[...]).astype(BF)
        for m in range(STREAMS):
            grads = (attn[part, :] if m == STREAMS - 1 else streams[m, part, :]).astype(F32)
            for j in range(depth):
                at = m * depth + j
                grad_mix[part, at : at + 1] = jnp.sum(grads * layers[j], axis=-1, keepdims=True)

    rows_loop(rows, 16, reduce)
    pre_value = pre[...]
    cdf = normal_cdf(pre_value)
    grads = grad_mix[...]
    w2_out[...] += dot(pre_value * cdf, grads, TN, EXACT)
    grad_act = dot(grads, w2[...], NT, EXACT)
    grad_pre = (grad_act * gelu_slope(pre_value, cdf)).astype(BF)
    w1_out[...] += dot(grad_pre, normed[...], TN)
    grad_normed[...] = dot(grad_pre, w1[...], NT)

    def write(part):
        layers = [hist[depth - 1, part, :].astype(F32)]
        latest = layers[0]
        scale = lax.rsqrt(mean_last(latest * latest) + RMS_EPSILON)
        value = grad_normed[part, :]
        gain_sum[...] += fold(value * latest * scale)
        value = value * gain[...]
        back = scale * value - latest * (scale * scale * scale * mean_last(latest * value))
        weight = mix[part, :]
        grads = [streams[m, part, :].astype(F32) for m in range(STREAMS - 1)]
        grads.append(attn[part, :].astype(F32))
        for j in range(depth):
            total = weight[:, j : j + 1] * grads[0]
            for m in range(1, STREAMS):
                at = m * depth + j
                total = total + weight[:, at : at + 1] * grads[m]
            if j == depth - 1:
                total = total + (grads[0] + grads[1] + grads[2] + grads[3]) + back
            grad_out[j, part, :] = total

    rows_loop(rows, 16, write)

    @pl.when(step_index == pl.num_programs(0) - 1)
    def _():
        gain_out[...] = jnp.sum(gain_sum[...], axis=0, keepdims=True)


def last(hist, streams, attn, mix, pre, gain, w1, w2):
    depth, rows, feats = hist.shape
    hidden = w1.shape[1]
    tile = min(64, rows)
    full = lambda shape: pl.BlockSpec(shape, lambda i: (0,) * len(shape))
    return pl.pallas_call(
        last_kernel,
        grid=(rows // tile,),
        in_specs=[
            pl.BlockSpec((depth, tile, feats), lambda i: (0, i, 0)),
            pl.BlockSpec((3, tile, feats), lambda i: (0, i, 0)),
            pl.BlockSpec((tile, feats), lambda i: (i, 0)),
            pl.BlockSpec((tile, STREAMS * depth), lambda i: (i, 0)),
            pl.BlockSpec((tile, hidden), lambda i: (i, 0)),
            full((1, feats)),
            full(w1.shape),
            full(w2.shape),
        ],
        out_specs=[
            pl.BlockSpec((depth, tile, feats), lambda i: (0, i, 0)),
            full((1, feats)),
            full((hidden, feats)),
            full(w2.shape),
        ],
        out_shape=[
            jax.ShapeDtypeStruct((depth, rows, feats), F32),
            jax.ShapeDtypeStruct((1, feats), F32),
            jax.ShapeDtypeStruct((hidden, feats), F32),
            jax.ShapeDtypeStruct(w2.shape, F32),
        ],
        scratch_shapes=[
            pltpu.VMEM((tile, feats), BF),
            pltpu.VMEM((tile, STREAMS * depth), F32),
            pltpu.VMEM((tile, feats), F32),
            pltpu.VMEM((8, feats), F32),
        ],
        compiler_params=params(40),
        cost_estimate=cost(30),
        name="last",
    )(hist, streams, attn, mix, pre, gain.reshape(1, feats), w1, w2)


def turn_back(dkv, tables):
    _, rows, width = dkv.shape
    return pl.pallas_call(
        lambda d, t, o: turn_back_kernel(d, t, o, None),
        grid=(1,),
        in_specs=[
            pl.BlockSpec((1, rows, width), lambda i: (0, 0, 0)),
            pl.BlockSpec(tables.shape, lambda i: (0, 0, 0)),
        ],
        out_specs=pl.BlockSpec((rows, width), lambda i: (0, 0)),
        out_shape=jax.ShapeDtypeStruct((rows, width), BF),
        compiler_params=params(40),
        cost_estimate=cost(3),
        name="turn_back",
    )(dkv, tables)


def row_product(left, right):
    return dot(left, right, TN).astype(BF)


def shards(
    history,
    positions,
    lengths,
    cotangent,
    mix_gain,
    mix_w1,
    mix_w2,
    ln_gain,
    ln_bias,
    qkv_weight,
    qkv_bias,
    out_weight,
    out_bias,
    up_weight,
    up_bias,
    down_weight,
    down_bias,
):
    depth, slots, block_len, feats = history.shape
    rows = slots * block_len
    width = qkv_weight.shape[2]
    heads = width // HEAD_DIM
    owners = ("dp", "seq")
    layers = history.reshape(depth, rows, feats)

    w_mix = lax.all_gather(mix_w1, owners, axis=0, tiled=True)
    kv_shard = jnp.concatenate([qkv_weight[1], qkv_weight[2]], axis=1)
    w_kv = lax.all_gather(kv_shard, owners, axis=0, tiled=True)
    w_q = lax.all_gather(qkv_weight[0], owners, axis=0, tiled=True)
    w_out = lax.all_gather(out_weight, owners, axis=0, tiled=True)
    w_up = lax.all_gather(up_weight, owners, axis=0, tiled=True)
    w_down = lax.all_gather(down_weight, owners, axis=0, tiled=True)

    offset = lax.axis_index("seq") * block_len
    query_place = offset + jnp.arange(block_len, dtype=jnp.int32)
    valid = (query_place[None, :] < lengths[:, None]).reshape(rows, 1)
    cot = jnp.where(valid, cotangent.reshape(rows, feats), jnp.zeros((), BF))
    scalars = jnp.concatenate([lengths, offset[None].astype(jnp.int32)])
    tables = rotary_tables(positions.reshape(rows))

    normed, resid, mix, pre = front(layers, mix_gain, w_mix, mix_w2, ln_gain, ln_bias)
    kv = project(normed, w_kv, qkv_bias[1:], tables, 1)
    kv_all = lax.all_gather(kv.reshape(2, slots, block_len, width), "seq", axis=0)
    q = project(normed, w_q, qkv_bias[:1], tables, 0)[0]
    attn_vals = attend(scalars, q, kv_all, heads).reshape(rows, width)
    hidden, mlp_in = attn_out(
        attn_vals, w_out, resid, out_bias[None, :], ln_gain[3:4], ln_bias[3:4]
    )
    up_act, grad_up, grad_up_bias = mlp(mlp_in, cot, w_up, w_down, up_bias[None, :])

    mine = lax.psum_scatter(
        dot(up_act, w_down, NT).astype(BF), "tensor", scatter_dimension=0, tiled=True
    )
    out_rows = (hidden + (mine.astype(F32) + down_bias)).astype(BF)
    layer_out = lax.all_gather(out_rows, "tensor", axis=0, tiled=True)

    grad_attn, small_mlp = mlp_back(grad_up, w_up, hidden, cot, ln_gain[3:4])
    scatter = functools.partial(
        lax.psum_scatter, axis_name=owners, scatter_dimension=0, tiled=True
    )
    shard_down = scatter(row_product(cot, up_act)).astype(F32)
    shard_up = scatter(row_product(mlp_in, grad_up)).astype(F32)
    grad_vals = dot(grad_attn, w_out).astype(BF)
    dq, dkv = attend_back(scalars, q, kv_all, grad_vals, tables, heads)
    dkv_own = lax.psum_scatter(dkv, "seq", scatter_dimension=0).reshape(2, rows, width)
    shard_out = scatter(row_product(grad_attn, attn_vals)).astype(F32)
    grad_lin = jnp.stack([dq.reshape(rows, width), turn_back(dkv_own, tables), dkv_own[1]])
    grads, small_qkv = streams_back(grad_lin, w_q, w_kv, layers, mix, ln_gain)
    shard_qkv = jnp.stack(
        [scatter(row_product(normed[i], grad_lin[i])).astype(F32) for i in range(3)]
    )
    grad_layers, grad_gain, grad_w1, grad_w2 = last(
        layers, grads, grad_attn, mix, pre, mix_gain, w_mix, mix_w2
    )
    grad_history = grad_layers.reshape(depth, slots, block_len, feats)
    shard_w1 = lax.psum_scatter(grad_w1.T, owners, scatter_dimension=0, tiled=True)
    small_mlp, small_qkv = lax.psum((small_mlp, small_qkv), ("dp", "seq", "tensor"))
    grad_gain, grad_w2, grad_qkv_bias, grad_up_bias, grad_down_bias = lax.psum(
        (
            grad_gain[0],
            grad_w2,
            jnp.sum(grad_lin.astype(F32), axis=1),
            grad_up_bias[0],
            jnp.sum(cot.astype(F32), axis=0),
        ),
        owners,
    )
    return (
        layer_out.reshape(slots, block_len, feats),
        grad_history,
        grad_gain,
        shard_w1,
        grad_w2,
        jnp.concatenate([small_qkv[0], small_mlp[0:1]], axis=0),
        jnp.concatenate([small_qkv[1], small_mlp[1:2]], axis=0),
        shard_qkv,
        grad_qkv_bias,
        shard_out,
        small_mlp[2],
        shard_up,
        grad_up_bias,
        shard_down,
        grad_down_bias,
    )


def solution(mesh):
    in_specs = (
        P(None, "dp", "seq", None),
        P("dp", "seq"),
        P("dp"),
        P("dp", "seq", None),
        P(),
        P(("dp", "seq"), None),
        P(),
        P(),
        P(),
        P(None, ("dp", "seq"), "tensor"),
        P(None, "tensor"),
        P(("dp", "seq"), "tensor"),
        P(),
        P(("dp", "seq"), "tensor"),
        P("tensor"),
        P(("dp", "seq"), "tensor"),
        P(),
    )
    out_specs = (
        P("dp", "seq", None),
        P(None, "dp", "seq", None),
        P(),
        P(("dp", "seq"), None),
        P(),
        P(),
        P(),
        P(None, ("dp", "seq"), "tensor"),
        P(None, "tensor"),
        P(("dp", "seq"), "tensor"),
        P(),
        P(("dp", "seq"), "tensor"),
        P("tensor"),
        P(("dp", "seq"), "tensor"),
        P(),
    )
    return jax.shard_map(shards, mesh=mesh, in_specs=in_specs, out_specs=out_specs, check_vma=False)
```

time: 2630 us -> 1630 us (0.62)
  waiting for transfers between devices: 1740 us -> 469 us
  Pallas kernels: 0 us -> 956 us
  matrix products: 445 us -> 70.7 us
  other arithmetic: 272 us -> 28.9 us
  local copies, waits for them, and re-layouts: 138 us -> 41.1 us
  blocking collectives: 15 us -> 46.5 us
    psum x5 -> x1, waiting for transfers between devices: 1500 us -> 0.01 us  [shards(): lax.psum((small_mlp, small_qkv), ('dp', 'seq', 'tensor'))]
    pallas_call x0 -> x11, Pallas kernels: none -> 956 us  [the longest x1 477 us: streams_back(): pl.pallas_call(streams_back_kernel, in_specs=[VMEM, VMEM, VMEM, ANY, ANY,...]
    dot_general x32 -> x8, matrix products: 445 us -> 70.7 us  [dot(): lax.dot_general(left, right, dims, precision=precision, preferred_element...]
    reduce_scatter x7 -> x9, waiting for transfers between devices: 104 us -> 336 us  [the longest x3 123 us: shards(): scatter(row_product(normed[i], grad_lin[i])).astype(F32)]
    reduce_sum x21 -> x2, other arithmetic: 138 us -> 6.6 us  [the longest x1 3.46 us: shards(): jnp.sum(grad_lin.astype(F32), axis=1)]
    another operation x8 -> x4, other arithmetic: 47.7 us -> 3.02 us  [the longest x1 2.37 us: shards(): jnp.stack([scatter(row_product(normed[i], grad_lin[i])).astype(F32) for i...]
    dot_general x2 -> x0, local copies, waits for them, and re-layouts: 29.4 us -> none  [the longest x1 28.6 us: shards(): jnp.einsum('nsj,snd->jnd', mix_weights, grad_stack, precision=EXACT)]
    convert_element_type x7 -> x4, other arithmetic: 38.6 us -> 9.92 us  [the longest x1 2.79 us: shards(): shard_down = scatter(row_product(cot, up_act)).astype(F32)]
  transfers between devices with their start and end apart: 18 -> 17, of which waited for: 13 -> 10; matrix products, arithmetic and copies ran while one was open for 25% -> 6% of each run, Pallas kernels for 0% -> 46%
where the time goes in v1:
time: 1630 us
  Pallas kernels  956 us (59%)
  waiting for transfers between devices  469 us (29%)
  matrix products  70.7 us (4%)
  blocking collectives  46.5 us (3%)
  local copies, waits for them, and re-layouts  41.1 us (3%)
  other arithmetic  28.9 us (2%)
    pallas_call x1, Pallas kernels, streams_back(): pl.pallas_call(streams_back_kernel, in_specs=[VMEM, VMEM, VMEM, ANY, ANY,...  477 us
    pallas_call x1, Pallas kernels, mlp_back(): pl.pallas_call(mlp_back_kernel, in_specs=[VMEM, VMEM, VMEM, ANY, VMEM], o...  155 us
    pallas_call x1, Pallas kernels, attn_out(): pl.pallas_call(attn_out_kernel, in_specs=[VMEM, VMEM, ANY, VMEM, VMEM, VM...  147 us
    reduce_scatter x3, waiting for transfers between devices, shards(): scatter(row_product(normed[i], grad_lin[i])).astype(F32)  123 us
    all_gather x1, waiting for transfers between devices, shards(): layer_out = lax.all_gather(out_rows, 'tensor', axis=0, tiled=True)  80 us
    reduce_scatter x1, waiting for transfers between devices, shards(): shard_up = scatter(row_product(mlp_in, grad_up)).astype(F32)  72.2 us
    reduce_scatter x1, waiting for transfers between devices, shards(): shard_down = scatter(row_product(cot, up_act)).astype(F32)  72.2 us
    dot_general x8, matrix products, dot(): lax.dot_general(left, right, dims, precision=precision, preferred_element...  70.7 us
  transfers between devices with their start and end apart: 17, of which 10 were waited for; matrix products, arithmetic and copies ran while one was open for 6% of the time, Pallas kernels for 46%

profile of v1, /device:TPU:0, one launch (start us, length us, event | category | flops | bytes accessed | tf_op | source)
XLA Modules:
  0.0 1627.7 jit_solution(11411394124535948819)
XLA Ops:
  13.2 21.0 %all_gather.24.w1 = bf16[2048,16]{1,0:T(8,128)(2,1)S(1)} all-gather(bf16[256,16]{1,0:T(8,128)(2,1)S(1)} %copy.34), channel_id=1, replica_groups=mesh['dp'=4,'seq'=2,'tensor'=4] {'dp','seq'}, dimensions={0}, use_global_device_ids=true | all-gather | bytes 73728 | tf_op jit(solution)/shard_map/all_gather | solution.py:882
  37.1 41.9 %front.1 = (bf16[3,1024,2048]{2,1,0:T(8,128)(2,1)}, f32[1024,2048]{1,0:T(8,128)S(1)}, f32[1024,16]{1,0:T(8,128)S(1)}, f32[1024,16]{1,0:T(8,128)S(1)}) custom-call(bf16[4,1024,2048]{2,1,0:T(8,128)(2,1)} %bitcast.92, f32[1,2048]{1,0:T(1,128)S(1)} %bitcast.86, bf16[2048,16]{1,0:T(8,128)(2,1)S(1)} %all_gather.24.w1, f32[16,16]{1,0:T(8,128)S(1)} %copy-done.24, ...), custom_call_target="tpu_custom_call" | custom-call | bytes 60000000 | tf_op jit(solution)/shard_map/front/pallas_call | solution.py:100
  87.2 9.9 project.3
  103.1 5.1 bitcast_select_fusion.cot
  109.9 5.6 project.2
  115.5 39.6 %all-gather.11.cloned.1.call-done.k.v = bf16[2,2,2,512,512]{4,3,2,1,0:T(8,128)(2,1)} async-done(((bf16[1,2,2,512,512]{4,3,2,1,0:T(8,128)(2,1)}), bf16[2,2,2,512,512]{4,3,2,1,0:T(8,128)(2,1)}) %all-gather.11.cloned.1.call-update) | async-done | bytes 4194320 | tf_op jit(solution)/shard_map/all_gather | solution.py:899
  157.3 15.6 attend.1
  173.9 10.9 all-gather.13.cloned.1.call-done.rhs
  187.7 146.6 %attn_out.1 = (f32[256,2048]{1,0:T(8,128)S(1)}, bf16[1024,2048]{1,0:T(8,128)(2,1)}) custom-call(bf16[1024,512]{1,0:T(8,128)(2,1)S(1)} %bitcast.80, bf16[2048,512]{1,0:T(8,128)(2,1)S(1)} %copy-done.14, f32[1024,2048]{1,0:T(8,128)} %copy-done.5, f32[1,2048]{1,0:T(1,128)S(1)} %bitcast.88, f32[1,2048]{1,0:T(1,128)S(1)} %slice.57.lg, f32[1,2048]{1,0:T(1,128)S(1)} %slice.58.lb), custom_call_target="tpu_custom_call" | custom-call | bytes 240000000 | tf_op jit(solution)/shard_map/attn_out/pallas_call | solution.py:486
  335.5 31.4 %mlp.1 = (bf16[1024,2048]{1,0:T(8,128)(2,1)S(1)}, bf16[1024,2048]{1,0:T(8,128)(2,1)}, f32[1,2048]{1,0:T(1,128)S(1)}) custom-call(bf16[1024,2048]{1,0:T(8,128)(2,1)} %get-tuple-element.37.mlp_in, bf16[1024,2048]{1,0:T(8,128)(2,1)} %bitcast_select_fusion.cot, bf16[2048,2048]{1,0:T(8,128)(2,1)} %all-gather.15.cloned.1.call-done.up.rhs, ...), custom_call_target="tpu_custom_call" | custom-call | bytes 75000000 | tf_op jit(solution)/shard_map/mlp/pallas_call | solution.py:699
  368.9 154.6 %mlp_back.1 = (bf16[1024,2048]{1,0:T(8,128)(2,1)}, f32[3,2048]{1,0:T(4,128)}) custom-call(bf16[1024,2048]{1,0:T(8,128)(2,1)} %get-tuple-element.39.lhs, bf16[2048,2048]{1,0:T(8,128)(2,1)} %all-gather.15.cloned.1.call-done.up.rhs, f32[256,2048]{1,0:T(8,128)} %copy-done.3, bf16[1024,2048]{1,0:T(8,128)(2,1)} %bitcast_select_fusion.cot, f32[1,2048]{1,0:T(1,128)S(1)} %slice.57.lg), custom_call_target="tpu_custom_call" | custom-call | bytes 240000000 | tf_op jit(solution)/shard_map/mlp_back/pallas_call | solution.py:563
  523.5 4.5 convolution_convert_fusion.4
  528.0 23.7 %attend_back.1 = (bf16[2,512,512]{2,1,0:T(8,128)(2,1)S(1)}, bf16[2,2,2,512,512]{4,3,2,1,0:T(8,128)(2,1)}) custom-call(s32[3]{0:T(128)S(1)} %pad_add_fusion.scalars, bf16[2,512,512]{2,1,0:T(8,128)(2,1)S(1)} %bitcast.75, bf16[2,2,2,512,512]{4,3,2,1,0:T(8,128)(2,1)} %all-gather.11.cloned.1.call-done.k.v, ...), custom_call_target="tpu_custom_call" | custom-call | bytes 75000000 | tf_op jit(solution)/shard_map/attend_back/pallas_call | solution.py:260
  552.8 13.9 convolution_convert_fusion.2
  567.9 5.9 convolution_convert_fusion.3
  573.9 33.2 %reduce-scatter.12.cloned.1.call-done = bf16[1,2,2,512,512]{4,3,2,1,0:T(8,128)(2,1)} async-done(((bf16[2,2,2,512,512]{4,3,2,1,0:T(8,128)(2,1)}), bf16[1,2,2,512,512]{4,3,2,1,0:T(8,128)(2,1)}) %reduce-scatter.12.cloned.1.call-update) | async-done | bytes 2097168 | tf_op jit(solution)/shard_map/reduce_scatter | solution.py:921
  613.4 477.3 %streams_back.1 = (bf16[3,1024,2048]{2,1,0:T(8,128)(2,1)}, f32[2,3,2048]{2,1,0:T(4,128)}) custom-call(bf16[3,1024,512]{2,1,0:T(8,128)(2,1)} %get-tuple-element.61.lhs, bf16[2048,512]{1,0:T(8,128)(2,1)} %bitcast.76, bf16[2048,1024]{1,0:T(8,128)(2,1)} %all-gather.9.cloned.1.call-done.weight.rhs_kv, bf16[4,1024,2048]{2,1,0:T(8,128)(2,1)} %bitcast.93, ...), custom_call_target="tpu_custom_call" | custom-call | bytes 660000000 | tf_op jit(solution)/shard_map/streams_back/pallas_call | solution.py:656
  1090.8 5.9 fusion.9
  1096.7 6.2 fusion.15
  1103.0 5.9 fusion.12
  1109.0 14.3 convolution_convert_fusion
  1123.4 14.0 convolution_convert_fusion.1
  1148.8 48.0 %last.1 = (f32[4,1024,2048]{2,1,0:T(8,128)}, f32[1,2048]{1,0:T(1,128)S(1)}, f32[16,2048]{1,0:T(8,128)}, f32[16,16]{1,0:T(8,128)S(1)}) custom-call(bf16[4,1024,2048]{2,1,0:T(8,128)(2,1)} %bitcast.94, bf16[3,1024,2048]{2,1,0:T(8,128)(2,1)} %get-tuple-element.44.streams, bf16[1024,2048]{1,0:T(8,128)(2,1)S(1)} %copy-done.11, f32[1024,16]{1,0:T(8,128)S(1)} %copy-done.13, ...), custom_call_target="tpu_custom_call" | custom-call | bytes 90000000 | tf_op jit(solution)/shard_map/last/pallas_call | solution.py:798
  1196.9 25.5 %all-reduce.1 = (f32[2048]{0:T(1024)}, f32[16,16]{1,0:T(8,128)}, f32[3,512]{1,0:T(4,128)}, f32[2048]{0:T(1024)}, f32[2048]{0:T(1024)}) all-reduce(f32[2048]{0:T(1024)S(1)} %bitcast.91, f32[16,16]{1,0:T(8,128)S(1)} %get-tuple-element.49, f32[3,512]{1,0:T(4,128)S(1)} %get-tuple-element.60, ...), channel_id=1, replica_groups=mesh['dp'=4,'seq'=2,'tensor'=4] {'dp','seq'}, use_global_device_ids=true, to_apply=%region_2.3 | all-reduce | flops 7936 | bytes 63488 | tf_op jit(solution)/shard_map/psum | solution.py:934
  1225.3 33.0 %reduce-scatter.16.cloned.1.call-done = bf16[256,512]{1,0:T(8,128)(2,1)} async-done(((bf16[2048,512]{1,0:T(8,128)(2,1)}), bf16[256,512]{1,0:T(8,128)(2,1)}) %reduce-scatter.16.cloned.1.call-update) | async-done | bytes 262160 | tf_op jit(solution)/shard_map/reduce_scatter | solution.py:926
  1258.3 45.0 %reduce-scatter.20.cloned.1.call-done = bf16[256,512]{1,0:T(8,128)(2,1)} async-done(((bf16[2048,512]{1,0:T(8,128)(2,1)}), bf16[256,512]{1,0:T(8,128)(2,1)}) %reduce-scatter.20.cloned.1.call-update) | async-done | bytes 262160 | tf_op jit(solution)/shard_map/reduce_scatter | solution.py:926
  1303.3 44.9 %reduce-scatter.18.cloned.1.call-done = bf16[256,512]{1,0:T(8,128)(2,1)} async-done(((bf16[2048,512]{1,0:T(8,128)(2,1)}), bf16[256,512]{1,0:T(8,128)(2,1)}) %reduce-scatter.18.cloned.1.call-update) | async-done | bytes 262160 | tf_op jit(solution)/shard_map/reduce_scatter | solution.py:926
  1350.6 72.2 %reduce-scatter.26.cloned.1.call-done = bf16[256,2048]{1,0:T(8,128)(2,1)} async-done(((bf16[2048,2048]{1,0:T(8,128)(2,1)}), bf16[256,2048]{1,0:T(8,128)(2,1)}) %reduce-scatter.26.cloned.1.call-update) | async-done | bytes 1048592 | tf_op jit(solution)/shard_map/reduce_scatter | solution.py:917
  1425.6 72.2 %reduce-scatter.24.cloned.1.call-done = bf16[256,2048]{1,0:T(8,128)(2,1)} async-done(((bf16[2048,2048]{1,0:T(8,128)(2,1)}), bf16[256,2048]{1,0:T(8,128)(2,1)}) %reduce-scatter.24.cloned.1.call-update) | async-done | bytes 1048592 | tf_op jit(solution)/shard_map/reduce_scatter | solution.py:918
  1500.6 80.0 %all-gather.19.cloned.1.call-done = bf16[1024,2048]{1,0:T(8,128)(2,1)} async-done(((bf16[256,2048]{1,0:T(8,128)(2,1)}), bf16[1024,2048]{1,0:T(8,128)(2,1)}) %all-gather.19.cloned.1.call-update) | async-done | bytes 4194320 | tf_op jit(solution)/shard_map/all_gather | solution.py:911
  1580.6 35.3 %reduce-scatter.14.cloned.1.call-done = f32[256,16]{0,1:T(8,128)} async-done(((f32[2048,16]{0,1:T(8,128)}), f32[256,16]{0,1:T(8,128)}) %reduce-scatter.14.cloned.1.call-update) | async-done | bytes 16400 | tf_op jit(solution)/shard_map/reduce_scatter | solution.py:932
  1615.9 4.8 copy.40
  (141 shorter events, 65.0 us)
Async XLA Ops:
  7.2 77.8 %all-gather.9.cloned.1.call-start = ((), (), s32[]{:S(2)}) async-start(), calls=%async_computation.9 | async-start | bytes 4718592 | tf_op jit(solution)/shard_map/all_gather | solution.py:884
  10.0 98.2 %all-gather.21.cloned.1.call-start = ((), (), s32[]{:S(2)}) async-start(), calls=%async_computation.24 | async-start | bytes 2359296 | tf_op jit(solution)/shard_map/all_gather | solution.py:885
  10.7 144.4 %all-gather.11.cloned.1.call-start = ((), (), s32[]{:S(2)}) async-start(), calls=%async_computation.10 | async-start | bytes 6291456 | tf_op jit(solution)/shard_map/all_gather | solution.py:899
  79.0 3.3 copy-start.5
  82.3 2.5 copy-start.12
  82.3 2.5 copy-start.18
  85.0 2.2 copy-start.1
  98.4 3.9 copy-start.31
  98.4 86.4 %all-gather.13.cloned.1.call-start = ((), (), s32[]{:S(2)}) async-start(), calls=%async_computation.11 | async-start | bytes 2359296 | tf_op jit(solution)/shard_map/all_gather | solution.py:886
  99.0 236.6 %all-gather.15.cloned.1.call-start = ((), (), s32[]{:S(2)}) async-start(), calls=%async_computation.12 | async-start | bytes 9437184 | tf_op jit(solution)/shard_map/all_gather | solution.py:887
  99.6 236.0 %all-gather.17.cloned.1.call-start = ((), (), s32[]{:S(2)}) async-start(), calls=%async_computation.13 | async-start | bytes 9437184 | tf_op jit(solution)/shard_map/all_gather | solution.py:888
  100.1 507.0 %reduce-scatter.12.cloned.1.call-start = ((), (), s32[]{:S(2)}) async-start(), calls=%async_computation.16 | async-start | bytes 6291456 | tf_op jit(solution)/shard_map/reduce_scatter | solution.py:921
  157.3 27.5 %copy-start.26 = (f32[2048]{0:T(1024)S(1)}, f32[2048]{0:T(1024)}, u32[]{:S(2)}) copy-start(f32[2048]{0:T(1024)} %param.29) | copy-start | bytes 24580
  187.7 147.9 %copy-start.27 = (f32[2048]{0:T(1024)S(1)}, f32[2048]{0:T(1024)}, u32[]{:S(2)}) copy-start(f32[2048]{0:T(1024)} %param.31) | copy-start | bytes 24580
  368.9 154.6 %copy-start.15 = (bf16[2048,512]{1,0:T(8,128)(2,1)S(1)}, bf16[2048,512]{1,0:T(8,128)(2,1)}, u32[]{:S(2)}) copy-start(bf16[2048,512]{1,0:T(8,128)(2,1)} %all-gather.13.cloned.1.call-done.rhs) | copy-start | bytes 6291460
  552.7 584.9 %reduce-scatter.10.cloned.1.call-start = ((), (), s32[]{:S(2)}) async-start(), calls=%async_computation.14 | async-start | bytes 5242880 | tf_op jit(solution)/shard_map/reduce_scatter | solution.py:907
  566.7 578.1 %reduce-scatter.22.cloned.1.call-start = ((), (), s32[]{:S(2)}) async-start(), calls=%async_computation.21 | async-start | bytes 2359296 | tf_op jit(solution)/shard_map/reduce_scatter | solution.py:922
  573.9 648.5 %all-reduce.4.cloned.1.call-start = ((), (), s32[]{:S(2)}) async-start(), calls=%async_computation.25 | async-start | bytes 196608 | tf_op jit(solution)/shard_map/psum | solution.py:933
  609.9 3.5 copy-start.29
  613.4 477.4 %copy-start.17 = (bf16[2,512,512]{2,1,0:T(8,128)(2,1)S(1)}, bf16[2,512,512]{2,1,0:T(8,128)(2,1)}, u32[]{:S(2)}) copy-start(bf16[2,512,512]{2,1,0:T(8,128)(2,1)} %copy-done.16) | copy-start | bytes 3145732
  1090.7 167.6 %reduce-scatter.16.cloned.1.call-start = ((), (), s32[]{:S(2)}) async-start(), calls=%async_computation.18 | async-start | bytes 2359296 | tf_op jit(solution)/shard_map/reduce_scatter | solution.py:926
  1096.7 206.6 %reduce-scatter.20.cloned.1.call-start = ((), (), s32[]{:S(2)}) async-start(), calls=%async_computation.20 | async-start | bytes 2359296 | tf_op jit(solution)/shard_map/reduce_scatter | solution.py:926
  1103.0 245.2 %reduce-scatter.18.cloned.1.call-start = ((), (), s32[]{:S(2)}) async-start(), calls=%async_computation.19 | async-start | bytes 2359296 | tf_op jit(solution)/shard_map/reduce_scatter | solution.py:926
  1108.9 313.9 %reduce-scatter.26.cloned.1.call-start = ((), (), s32[]{:S(2)}) async-start(), calls=%async_computation.23 | async-start | bytes 9437184 | tf_op jit(solution)/shard_map/reduce_scatter | solution.py:917
  1123.3 374.5 %reduce-scatter.24.cloned.1.call-start = ((), (), s32[]{:S(2)}) async-start(), calls=%async_computation.22 | async-start | bytes 9437184 | tf_op jit(solution)/shard_map/reduce_scatter | solution.py:918
  1137.5 9.2 copy-start.13
  1137.5 9.2 copy-start.23
  1137.5 9.2 copy-start.25
  1137.5 443.1 %all-gather.19.cloned.1.call-start = ((), (), s32[]{:S(2)}) async-start(), calls=%async_computation.15 | async-start | bytes 5242880 | tf_op jit(solution)/shard_map/all_gather | solution.py:911
  1141.6 5.1 copy-start.19
  1141.6 474.3 %reduce-scatter.14.cloned.1.call-start = ((), (), s32[]{:S(2)}) async-start(), calls=%async_computation.17 | async-start | bytes 147456 | tf_op jit(solution)/shard_map/reduce_scatter | solution.py:932
  1146.7 2.2 copy-start.11
  (17 other events, 22.2 us)
Sparse Core Ops, SparseCore 0:
  10.5 41.9 all-gather.8
  54.9 27.9 all-gather.20
  98.5 56.5 all-gather.10
  156.9 27.9 all-gather.12
  186.6 54.3 all-gather.14
  242.7 54.3 all-gather.16
  552.8 54.2 reduce-scatter.11
  609.5 140.7 reduce-scatter.9
  753.6 42.1 reduce-scatter.21
  1090.8 121.6 all-reduce.3
  1216.1 42.1 reduce-scatter.15
  1262.0 41.2 reduce-scatter.19
  1306.9 41.2 reduce-scatter.17
  1351.5 71.2 reduce-scatter.25
  1426.5 71.2 reduce-scatter.23
  1499.8 80.7 all-gather.18
  1584.0 31.8 reduce-scatter.13

commit v2 on v1

--- a/solution.py
+++ b/solution.py
@@ -505,6 +505,88 @@
     )(lhs, rhs, resid, bias, lg, lb)
 
 
+def mlp_out_kernel(
+    lhs, rhs, hidden, bias, out,
+    far, near, far_in, near_in, total, own, sems, local_sems,
+):
+    chunk, feats = total.shape
+    ring = Ring(chunk)
+    ring.barrier()
+    scatter = Scatter(ring, lhs, rhs, far, near, far_in, near_in, sems)
+    scatter.begin()
+    scatter.relay()
+    own_sum(scatter, total)
+    scatter.arrive()
+
+    def add(part):
+        own[part, :] = (hidden[part, :] + (whole_sum(scatter, total, part) + bias[...])).astype(BF)
+
+    rows_loop(chunk, 16, add)
+    gather = Gather(ring, own, out, sems, 6, local_sems.at[0])
+    gather.begin()
+    gather.relay()
+    scatter.finish()
+    gather.finish()
+
+
+def mlp_out(lhs, rhs, hidden, bias):
+    rows = lhs.shape[0]
+    chunk, feats = hidden.shape
+    return pl.pallas_call(
+        mlp_out_kernel,
+        in_specs=[VMEM, VMEM, VMEM, VMEM],
+        out_specs=ANY,
+        out_shape=jax.ShapeDtypeStruct((rows, feats), BF),
+        scratch_shapes=scatter_scratch(chunk, feats)
+        + [
+            pltpu.VMEM((chunk, feats), F32),
+            pltpu.VMEM((chunk, feats), BF),
+            pltpu.SemaphoreType.DMA((2, 10)),
+            pltpu.SemaphoreType.DMA((1,)),
+        ],
+        compiler_params=params(52, 3),
+        cost_estimate=cost(140),
+        name="mlp_out",
+    )(lhs, rhs, hidden, bias)
+
+
+def weights_kernel(normed, grad_attn, grad_lin, attn_vals, out):
+    branch = pl.program_id(0)
+
+    @pl.when(branch < 3)
+    def _():
+        out[...] = dot(normed[0], grad_lin[0], TN).astype(BF)
+
+    @pl.when(branch == 3)
+    def _():
+        out[...] = dot(grad_attn[...], attn_vals[...], TN).astype(BF)
+
+
+def weight_grads(normed, grad_attn, grad_lin, attn_vals):
+    _, rows, feats = normed.shape
+    width = attn_vals.shape[1]
+    cols = 512
+    last_block = feats // cols - 1
+    return pl.pallas_call(
+        weights_kernel,
+        grid=(4, feats // cols),
+        in_specs=[
+            pl.BlockSpec(
+                (1, rows, cols),
+                lambda b, n: (jnp.minimum(b, 2), 0, jnp.where(b < 3, n, last_block)),
+            ),
+            pl.BlockSpec((rows, cols), lambda b, n: (0, jnp.where(b < 3, 0, n))),
+            pl.BlockSpec((1, rows, width), lambda b, n: (jnp.minimum(b, 2), 0, 0)),
+            pl.BlockSpec((rows, width), lambda b, n: (0, 0)),
+        ],
+        out_specs=pl.BlockSpec((cols, width), lambda b, n: (n, b)),
+        out_shape=jax.ShapeDtypeStruct((feats, 4 * width), BF),
+        compiler_params=params(40),
+        cost_estimate=cost(15),
+        name="weight_grads",
+    )(normed, grad_attn, grad_lin, attn_vals)
+
+
 def norm_back(values, grads, gain):
     centred = values - mean_last(values)
     inverse = lax.rsqrt(mean_last(centred * centred) + NORM_EPSILON)
@@ -583,98 +665,253 @@
     )(lhs, rhs, hidden, cot, lg)
 
 
+class Spread:
+    def __init__(self, ring, slots, sems, base):
+        half = slots.shape[1] // 2
+        mine = slots.at[ring.me]
+        self.first = [
+            remote(mine, mine, sems, base, ring.right),
+            remote(mine, mine, sems, base + 1, ring.left),
+        ]
+        up = slots.at[ring.left, pl.ds(0, half), :]
+        down = slots.at[ring.right, pl.ds(half, half), :]
+        self.second = [
+            remote(up, up, sems, base + 2, ring.right),
+            remote(down, down, sems, base + 3, ring.left),
+        ]
+
+    def begin(self):
+        for copy in self.first:
+            copy.start()
+
+    def relay(self):
+        for arrived, onward in zip(self.first, self.second):
+            arrived.wait_recv()
+            onward.start()
+
+    def arrive(self):
+        for copy in self.second:
+            copy.wait_recv()
+
+    def finish(self):
+        for copy in self.first + self.second:
+            copy.wait_send()
+
+
 def streams_back_kernel(
-    lhs, rhs_q, rhs_kv, hist, mix, lg, grads_out, small_out,
-    far, near, far_in, near_in, total, layers, mix_rows, own, sums, sems, local_sems,
+    lin, weight, hist, mix, lg, grads_out, small_out,
+    slots, weights, total, layers, stage, sums, sems, weight_sems, layer_sem, stage_sems, own_sems,
 ):
-    chunk, feats = total.shape
+    tile, feats = total.shape
     depth = layers.shape[0]
-    width = lhs.shape[2]
-    ring = Ring(chunk)
-    mine = pl.ds(ring.at(ring.me), chunk)
-    fetch = pltpu.make_async_copy(hist.at[:, mine, :], layers, local_sems.at[0])
-    fetch.start()
-    fetch_mix = pltpu.make_async_copy(mix.at[mine, :], mix_rows, local_sems.at[1])
-    fetch_mix.start()
+    rows, width = lin.shape[1], lin.shape[2]
+    tiles = rows // tile
+    ring = Ring(rows)
+
+    def fetch(stream):
+        return [
+            pltpu.make_async_copy(
+                weight.at[pl.ds(z * feats, feats), pl.ds(stream * width, width)],
+                weights.at[stream % 2, z],
+                weight_sems.at[stream % 2, z],
+            )
+            for z in range(RING)
+        ]
+
+    local = [
+        pltpu.make_async_copy(lin.at[i], slots.at[i, ring.me], own_sems.at[i]) for i in range(3)
+    ]
+    for copy in local:
+        copy.start()
+    for stream in range(2):
+        for copy in fetch(stream):
+            copy.start()
+    sums[...] = jnp.zeros_like(sums)
     ring.barrier()
-    weights = [
-        rhs_q,
-        rhs_kv.at[:, pl.ds(0, width)],
-        rhs_kv.at[:, pl.ds(width, width)],
-    ]
-    scatters = [
-        Scatter(
-            ring, lhs.at[i], weights[i], far.at[i], near.at[i], far_in.at[i], near_in.at[i],
-            sems.at[i],
+    spreads = [Spread(ring, slots.at[i], sems.at[i], 0) for i in range(3)]
+
+    def write_out(stream, index, slot):
+        part = pl.ds(pl.multiple_of(index * tile, tile), tile)
+        return pltpu.make_async_copy(
+            stage.at[slot], grads_out.at[stream, part, :], stage_sems.at[slot]
         )
-        for i in range(3)
-    ]
-    gathers = [
-        Gather(ring, own.at[i], grads_out.at[i], sems.at[i], 6, local_sems.at[2 + i])
-        for i in range(3)
-    ]
-    for scatter in scatters:
-        scatter.begin()
-    sums[...] = jnp.zeros_like(sums)
-    fetch.wait()
-    fetch_mix.wait()
-    for i, scatter in enumerate(scatters):
-        scatter.relay()
-    for i, scatter in enumerate(scatters):
-        own_sum(scatter, total)
-        scatter.arrive()
-
-        def back(part):
-            grads = whole_sum(scatter, total, part)
-            running = layers[depth - 1, part, :].astype(F32)
-            weight = mix_rows[part, :]
-            mixture = running
-            for j in range(depth):
-                at = i * depth + j
-                mixture = mixture + weight[:, at : at + 1] * layers[j, part, :].astype(F32)
-            step, normed = norm_back(mixture, grads, lg[i : i + 1, :])
-            own[i, part, :] = step.astype(BF)
-            sums[i, 0] += fold(grads * normed)
-            sums[i, 1] += fold(grads)
-
-        rows_loop(chunk, 16, back)
-        gathers[i].begin()
-        if i:
-            gathers[i - 1].relay()
+
+    def compute(stream):
+        for copy in fetch(stream):
+            copy.wait()
+
+        def one(index, carry):
+            part = pl.ds(pl.multiple_of(index * tile, tile), tile)
+            load = pltpu.make_async_copy(hist.at[:, part, :], layers, layer_sem)
+            load.start()
+            slot = lax.rem(index, 2)
+
+            def columns(cols):
+                value = dot(slots[stream, 0, part, :], weights[stream % 2, 0, cols, :], NT)
+                for z in range(1, RING):
+                    value += dot(slots[stream, z, part, :], weights[stream % 2, z, cols, :], NT)
+                total[:, cols] = value
+
+            rows_loop(feats, 512, columns)
+            load.wait()
+
+            @pl.when(index >= 2)
+            def _():
+                write_out(stream, index - 2, slot).wait()
+
+            def back(sub):
+                grads = total[sub, :]
+                latest = layers[depth - 1, sub, :].astype(F32)
+                at = pl.multiple_of(index * tile + sub.start, 16)
+                share = mix[pl.ds(at, 16), :]
+                mixture = latest
+                for j in range(depth):
+                    col = stream * depth + j
+                    mixture = mixture + share[:, col : col + 1] * layers[j, sub, :].astype(F32)
+                step, normed = norm_back(mixture, grads, lg[stream : stream + 1, :])
+                stage[slot, sub, :] = step.astype(BF)
+                sums[stream, 0] += fold(grads * normed)
+                sums[stream, 1] += fold(grads)
+
+            rows_loop(tile, 16, back)
+            write_out(stream, index, slot).start()
+            return carry
+
+        lax.fori_loop(0, tiles, one, 0)
+        for index in range(max(tiles - 2, 0), tiles):
+            write_out(stream, index, index % 2).wait()
+        if stream == 0:
+            for copy in fetch(2):
+                copy.start()
+
+    for copy in local:
+        copy.wait()
+    spreads[0].begin()
+    spreads[1].begin()
+    spreads[0].relay()
+    spreads[2].begin()
+    spreads[1].relay()
+    spreads[0].arrive()
+    compute(0)
+    spreads[2].relay()
+    spreads[1].arrive()
+    compute(1)
+    spreads[2].arrive()
+    compute(2)
     for i in range(3):
         for j in range(2):
             small_out[j, i : i + 1, :] = jnp.sum(sums[i, j], axis=0, keepdims=True)
-    gathers[2].relay()
-    for scatter, gather in zip(scatters, gathers):
-        scatter.finish()
-        gather.finish()
-
-
-def streams_back(lhs, rhs_q, rhs_kv, hist, mix, lg):
+    for spread in spreads:
+        spread.finish()
+
+
+def streams_back(lin, weight, hist, mix, lg):
     depth, rows, feats = hist.shape
-    chunk = rows // RING
+    width = lin.shape[2]
+    tile = min(256, rows)
     return pl.pallas_call(
         streams_back_kernel,
-        in_specs=[VMEM, VMEM, VMEM, ANY, ANY, VMEM],
+        in_specs=[VMEM, ANY, ANY, VMEM, VMEM],
         out_specs=[ANY, VMEM],
         out_shape=[
             jax.ShapeDtypeStruct((3, rows, feats), BF),
             jax.ShapeDtypeStruct((2, 3, feats), F32),
         ],
-        scratch_shapes=scatter_scratch(chunk, feats, 3)
-        + [
-            pltpu.VMEM((chunk, feats), F32),
-            pltpu.VMEM((depth, chunk, feats), BF),
-            pltpu.VMEM((chunk, mix.shape[1]), F32),
-            pltpu.VMEM((3, chunk, feats), BF),
+        scratch_shapes=[
+            pltpu.VMEM((3, RING, rows, width), BF),
+            pltpu.VMEM((2, RING, feats, width), BF),
+            pltpu.VMEM((tile, feats), F32),
+            pltpu.VMEM((depth, tile, feats), BF),
+            pltpu.VMEM((2, tile, feats), BF),
             pltpu.VMEM((3, 2, 8, feats), F32),
-            pltpu.SemaphoreType.DMA((3, 2, 10)),
-            pltpu.SemaphoreType.DMA((5,)),
+            pltpu.SemaphoreType.DMA((3, 2, 4)),
+            pltpu.SemaphoreType.DMA((2, RING)),
+            pltpu.SemaphoreType.DMA,
+            pltpu.SemaphoreType.DMA((2,)),
+            pltpu.SemaphoreType.DMA((3,)),
         ],
         compiler_params=params(58, 2),
-        cost_estimate=cost(220),
+        cost_estimate=cost(240),
         name="streams_back",
-    )(lhs, rhs_q, rhs_kv, hist, mix, lg)
+    )(lin, weight, hist, mix, lg)
+
+
+def small_kernel(seqs, owners, ours, share, out, share_out, near, all_ours, all_shares, near_sems, sems):
+    ring = Ring(2)
+    near_rows = near.shape[1]
+    rank = lax.axis_index("dp") * seqs + lax.axis_index("seq")
+    peers = [lax.rem(rank + k, owners) for k in range(1, owners)]
+    places = [{"dp": lax.div(p, seqs), "seq": lax.rem(p, seqs)} for p in peers]
+    mates = [ring.right, ring.far, ring.left]
+    gate = pltpu.get_barrier_semaphore()
+    for place in places + [{"tensor": z} for z in mates]:
+        pl.semaphore_signal(gate, inc=1, device_id=place, device_id_type=MESH)
+    pl.semaphore_wait(gate, len(places) + len(mates))
+
+    def send(source, target, pair, index, place):
+        return pltpu.make_async_remote_copy(
+            src_ref=source,
+            dst_ref=target,
+            send_sem=pair.at[0, index],
+            recv_sem=pair.at[1, index],
+            device_id=place,
+            device_id_type=MESH,
+        )
+
+    near[ring.me] = ours[0:near_rows, :]
+    shares = [
+        send(share.at[p], all_shares.at[rank], sems.at[0], k, place)
+        for k, (p, place) in enumerate(zip(peers, places))
+    ]
+    first = [
+        send(near.at[ring.me], near.at[ring.me], near_sems, k, {"tensor": z})
+        for k, z in enumerate(mates)
+    ]
+    for copy in first + shares:
+        copy.start()
+    for copy in first:
+        copy.wait()
+    all_ours[rank, 0:near_rows, :] = (near[0] + near[1]) + (near[2] + near[3])
+    all_ours[rank, near_rows:, :] = ours[near_rows:, :]
+    all_shares[rank] = share[rank]
+    second = [
+        send(all_ours.at[rank], all_ours.at[rank], sems.at[1], k, place)
+        for k, place in enumerate(places)
+    ]
+    for copy in second:
+        copy.start()
+    for copy in shares + second:
+        copy.wait()
+    total, part = all_ours[0], all_shares[0]
+    for index in range(1, owners):
+        total += all_ours[index]
+        part += all_shares[index]
+    out[...] = total
+    share_out[...] = part
+
+
+def small_sums(ours, share, seqs):
+    owners = share.shape[0]
+    rows, feats = ours.shape
+    return pl.pallas_call(
+        functools.partial(small_kernel, seqs, owners),
+        in_specs=[VMEM, VMEM],
+        out_specs=[VMEM, VMEM],
+        out_shape=[
+            jax.ShapeDtypeStruct(ours.shape, F32),
+            jax.ShapeDtypeStruct(share.shape[1:], F32),
+        ],
+        scratch_shapes=[
+            pltpu.VMEM((RING, 8, feats), F32),
+            pltpu.VMEM((owners,) + ours.shape, F32),
+            pltpu.VMEM(share.shape, F32),
+            pltpu.SemaphoreType.DMA((2, 3)),
+            pltpu.SemaphoreType.DMA((2, 2, owners - 1)),
+        ],
+        compiler_params=params(40, 4),
+        cost_estimate=cost(12),
+        name="small_sums",
+    )(ours, share)
 
 
 def mlp_kernel(mlp_in, cot, up, down, bias, act_out, grad_out, sum_out):
@@ -886,6 +1123,11 @@
     w_out = lax.all_gather(out_weight, owners, axis=0, tiled=True)
     w_up = lax.all_gather(up_weight, owners, axis=0, tiled=True)
     w_down = lax.all_gather(down_weight, owners, axis=0, tiled=True)
+    tie = lax.optimization_barrier
+    qkv_shard, w_down = tie(
+        (jnp.concatenate([qkv_weight[0], qkv_weight[1], qkv_weight[2]], axis=1), w_down)
+    )
+    w_qkv = lax.all_gather(qkv_shard, ("tensor",) + owners, axis=0, tiled=True)
 
     offset = lax.axis_index("seq") * block_len
     query_place = offset + jnp.arange(block_len, dtype=jnp.int32)
@@ -903,60 +1145,72 @@
         attn_vals, w_out, resid, out_bias[None, :], ln_gain[3:4], ln_bias[3:4]
     )
     up_act, grad_up, grad_up_bias = mlp(mlp_in, cot, w_up, w_down, up_bias[None, :])
-
-    mine = lax.psum_scatter(
-        dot(up_act, w_down, NT).astype(BF), "tensor", scatter_dimension=0, tiled=True
-    )
-    out_rows = (hidden + (mine.astype(F32) + down_bias)).astype(BF)
-    layer_out = lax.all_gather(out_rows, "tensor", axis=0, tiled=True)
-
-    grad_attn, small_mlp = mlp_back(grad_up, w_up, hidden, cot, ln_gain[3:4])
     scatter = functools.partial(
         lax.psum_scatter, axis_name=owners, scatter_dimension=0, tiled=True
     )
-    shard_down = scatter(row_product(cot, up_act)).astype(F32)
-    shard_up = scatter(row_product(mlp_in, grad_up)).astype(F32)
+    grad_down, grad_upw, grad_up = tie(
+        (row_product(cot, up_act), row_product(mlp_in, grad_up), grad_up)
+    )
+    grad_attn, small_mlp = mlp_back(grad_up, w_up, hidden, cot, ln_gain[3:4])
     grad_vals = dot(grad_attn, w_out).astype(BF)
     dq, dkv = attend_back(scalars, q, kv_all, grad_vals, tables, heads)
+    w_qkv, up_act, dkv = tie((w_qkv, up_act, dkv))
     dkv_own = lax.psum_scatter(dkv, "seq", scatter_dimension=0).reshape(2, rows, width)
-    shard_out = scatter(row_product(grad_attn, attn_vals)).astype(F32)
+    layer_out = mlp_out(up_act, w_down, hidden, down_bias[None, :])
+    layer_out, dkv_own, grad_down, grad_upw = tie((layer_out, dkv_own, grad_down, grad_upw))
+    shard_down, shard_up = scatter(grad_down), scatter(grad_upw)
     grad_lin = jnp.stack([dq.reshape(rows, width), turn_back(dkv_own, tables), dkv_own[1]])
-    grads, small_qkv = streams_back(grad_lin, w_q, w_kv, layers, mix, ln_gain)
-    shard_qkv = jnp.stack(
-        [scatter(row_product(normed[i], grad_lin[i])).astype(F32) for i in range(3)]
-    )
+    grad_owqkv, grad_lin = tie((weight_grads(normed, grad_attn, grad_lin, attn_vals), grad_lin))
+    shard_all = scatter(grad_owqkv)
+    grads, small_qkv = streams_back(grad_lin, w_qkv, layers, mix, ln_gain)
+    shard_down, shard_up, shard_all, grads = tie((shard_down, shard_up, shard_all, grads))
+    shard_down, shard_up, shard_all = (
+        shard_down.astype(F32), shard_up.astype(F32), shard_all.astype(F32)
+    )
+    shard_qkv = jnp.stack([shard_all[:, i * width : (i + 1) * width] for i in range(3)])
+    shard_out = shard_all[:, 3 * width :]
     grad_layers, grad_gain, grad_w1, grad_w2 = last(
         layers, grads, grad_attn, mix, pre, mix_gain, w_mix, mix_w2
     )
     grad_history = grad_layers.reshape(depth, slots, block_len, feats)
-    shard_w1 = lax.psum_scatter(grad_w1.T, owners, scatter_dimension=0, tiled=True)
-    small_mlp, small_qkv = lax.psum((small_mlp, small_qkv), ("dp", "seq", "tensor"))
-    grad_gain, grad_w2, grad_qkv_bias, grad_up_bias, grad_down_bias = lax.psum(
-        (
-            grad_gain[0],
-            grad_w2,
-            jnp.sum(grad_lin.astype(F32), axis=1),
-            grad_up_bias[0],
-            jnp.sum(cot.astype(F32), axis=0),
-        ),
-        owners,
-    )
+    seqs = lax.axis_size("seq")
+    count = lax.axis_size("dp") * seqs
+    hidden_count = mix_w1.shape[1]
+    share = grad_w1.reshape(hidden_count, count, feats // count).transpose(1, 0, 2)
+
+    def as_row(values):
+        flat = values.reshape(1, -1)
+        return jnp.pad(flat, ((0, 0), (0, feats - flat.shape[1])))
+
+    grad_qkv_bias = jnp.sum(grad_lin.astype(F32), axis=1)
+    ours = jnp.concatenate(
+        [small_mlp, jnp.zeros((5, feats), F32), small_qkv.reshape(6, feats)]
+        + [
+            as_row(values)
+            for values in (
+                grad_gain, grad_w2, grad_qkv_bias, grad_up_bias, jnp.sum(cot.astype(F32), axis=0)
+            )
+        ]
+        + [jnp.zeros((5, feats), F32)],
+        axis=0,
+    )
+    summed, shard_w1 = small_sums(ours, share.reshape(count, -1, 128), seqs)
     return (
         layer_out.reshape(slots, block_len, feats),
         grad_history,
-        grad_gain,
-        shard_w1,
-        grad_w2,
-        jnp.concatenate([small_qkv[0], small_mlp[0:1]], axis=0),
-        jnp.concatenate([small_qkv[1], small_mlp[1:2]], axis=0),
+        summed[14],
+        shard_w1.reshape(hidden_count, feats // count).T,
+        summed[15, : grad_w2.size].reshape(grad_w2.shape),
+        jnp.concatenate([summed[8:11], summed[0:1]], axis=0),
+        jnp.concatenate([summed[11:14], summed[1:2]], axis=0),
         shard_qkv,
-        grad_qkv_bias,
+        summed[16, : grad_qkv_bias.size].reshape(grad_qkv_bias.shape),
         shard_out,
-        small_mlp[2],
+        summed[2],
         shard_up,
-        grad_up_bias,
+        summed[17, : up_bias.size],
         shard_down,
-        grad_down_bias,
+        summed[18],
     )
 
 

time: 1630 us -> 1220 us (0.75)
  waiting for transfers between devices: 469 us -> 103 us
  matrix products: 70.7 us -> 32.2 us
  Pallas kernels: 956 us -> 989 us
  blocking collectives: 46.5 us -> 20.9 us
    reduce_scatter x8 -> x3, waiting for transfers between devices: 303 us -> 0.06 us  [the longest x2 0.04 us: shards(): shard_down, shard_up = (scatter(grad_down), scatter(grad_upw))]
    all_gather x1, waiting for transfers between devices: 80 us -> 0.01 us  [shards(): w_qkv = lax.all_gather(qkv_shard, ('tensor',) + owners, axis=0, tiled=True)]
    pallas_call x1, Pallas kernels: 147 us -> 192 us  [attn_out(): pl.pallas_call(attn_out_kernel, in_specs=[VMEM, VMEM, ANY, VMEM, VMEM, VM...]
    dot_general x8 -> x3, matrix products: 70.7 us -> 32.2 us  [dot(): lax.dot_general(left, right, dims, precision=precision, preferred_element...]
    reduce_scatter x1, waiting for transfers between devices: 33.2 us -> 0.02 us  [shards(): lax.psum_scatter(dkv, 'seq', scatter_dimension=0).reshape(2, rows, width)]
    psum x1 -> x0, blocking collectives: 25.5 us -> none  [shards(): lax.psum((grad_gain[0], grad_w2, jnp.sum(grad_lin.astype(F32), axis=1), g...]
    all_gather x1, waiting for transfers between devices: 0.01 us -> 25 us  [shards(): w_q = lax.all_gather(qkv_weight[0], owners, axis=0, tiled=True)]
    pallas_call x1 -> x4, Pallas kernels: 477 us -> 462 us  [the longest x1 266 us: streams_back(): pl.pallas_call(streams_back_kernel, in_specs=[VMEM, ANY, ANY, VMEM, VMEM]...]
  transfers between devices with their start and end apart: 17 -> 11, of which waited for: 10 -> 4; matrix products, arithmetic and copies ran while one was open for 6% -> 4% of each run, Pallas kernels for 46% -> 73%
where the time goes in v2:
time: 1220 us
  Pallas kernels  989 us (81%)
  waiting for transfers between devices  103 us (8%)
  local copies, waits for them, and re-layouts  38.3 us (3%)
  matrix products  32.2 us (3%)
  blocking collectives  20.9 us (2%)
  other arithmetic  19.6 us (2%)
  between operations  14.7 us (1%)
    pallas_call x1, Pallas kernels, streams_back(): pl.pallas_call(streams_back_kernel, in_specs=[VMEM, ANY, ANY, VMEM, VMEM]...  266 us
    pallas_call x1, Pallas kernels, attn_out(): pl.pallas_call(attn_out_kernel, in_specs=[VMEM, VMEM, ANY, VMEM, VMEM, VM...  192 us
    pallas_call x1, Pallas kernels, mlp_back(): pl.pallas_call(mlp_back_kernel, in_specs=[VMEM, VMEM, VMEM, ANY, VMEM], o...  157 us
    pallas_call x1, Pallas kernels, mlp_out(): pl.pallas_call(mlp_out_kernel, in_specs=[VMEM, VMEM, VMEM, VMEM], out_spe...  150 us
    all_gather x1, waiting for transfers between devices, shards(): lax.all_gather(kv.reshape(2, slots, block_len, width), 'seq', axis=0)  50.7 us
    pallas_call x1, Pallas kernels, last(): pl.pallas_call(last_kernel, grid=(rows // tile,), in_specs=[pl.BlockSpec(...  48 us
    pallas_call x1, Pallas kernels, front(): pl.pallas_call(front_kernel, grid=(rows // tile,), in_specs=[pl.BlockSpec...  41.9 us
    pallas_call x1, Pallas kernels, mlp(): pl.pallas_call(mlp_kernel, grid=(width // cols, rows // tile), in_specs=[...  32.9 us
  transfers between devices with their start and end apart: 11, of which 4 were waited for; matrix products, arithmetic and copies ran while one was open for 4% of the time, Pallas kernels for 73%

profile of v2, /device:TPU:0, one launch (start us, length us, event | category | flops | bytes accessed | tf_op | source)
XLA Modules:
  0.0 1218.1 jit_solution(15574190723970570437)
XLA Ops:
  7.3 1.9 fusion.1
  12.0 20.9 %all_gather.26.w1 = bf16[2048,16]{1,0:T(8,128)(2,1)S(1)} all-gather(bf16[256,16]{1,0:T(8,128)(2,1)S(1)} %copy.38), channel_id=1, replica_groups=mesh['dp'=4,'seq'=2,'tensor'=4] {'dp','seq'}, dimensions={0}, use_global_device_ids=true | all-gather | bytes 73728 | tf_op jit(solution)/shard_map/all_gather | solution.py:1119
  32.9 41.9 %front.1 = (bf16[3,1024,2048]{2,1,0:T(8,128)(2,1)}, f32[1024,2048]{1,0:T(8,128)S(1)}, f32[1024,16]{1,0:T(8,128)S(1)}, f32[1024,16]{1,0:T(8,128)S(1)}) custom-call(bf16[4,1024,2048]{2,1,0:T(8,128)(2,1)} %bitcast.80, f32[1,2048]{1,0:T(1,128)S(1)} %bitcast.75, bf16[2048,16]{1,0:T(8,128)(2,1)S(1)} %all_gather.26.w1, f32[16,16]{1,0:T(8,128)S(1)} %copy-done.31, ...), custom_call_target="tpu_custom_call" | custom-call | bytes 60000000 | tf_op jit(solution)/shard_map/front/pallas_call | solution.py:100
  74.9 3.3 copy-done.11
  78.2 1.9 multiply_cosine_fusion
  80.8 2.5 copy-done.17
  83.3 10.0 project.3
  96.9 12.3 %all-gather.9.cloned.1.call-done.down.rhs = bf16[2048,2048]{1,0:T(8,128)(2,1)} async-done(((bf16[256,2048]{1,0:T(8,128)(2,1)}), bf16[2048,2048]{1,0:T(8,128)(2,1)}) %all-gather.9.cloned.1.call-update) | async-done | bytes 8388624 | tf_op jit(solution)/shard_map/all_gather | solution.py:1125
  110.0 4.6 bitcast_select_fusion.cot
  114.6 25.0 %all-gather.21.cloned.1.call-done = bf16[1,2048,512]{2,1,0:T(8,128)(2,1)} async-done(((bf16[1,256,512]{2,1,0:T(8,128)(2,1)}), bf16[1,2048,512]{2,1,0:T(8,128)(2,1)}) %all-gather.21.cloned.1.call-update) | async-done | bytes 2097168 | tf_op jit(solution)/shard_map/all_gather | solution.py:1122
  141.1 5.5 project.2
  147.6 50.7 %all-gather.15.cloned.1.call-done.k.v = bf16[2,2,2,512,512]{4,3,2,1,0:T(8,128)(2,1)} async-done(((bf16[1,2,2,512,512]{4,3,2,1,0:T(8,128)(2,1)}), bf16[2,2,2,512,512]{4,3,2,1,0:T(8,128)(2,1)}) %all-gather.15.cloned.1.call-update) | async-done | bytes 4194320 | tf_op jit(solution)/shard_map/all_gather | solution.py:1141
  198.4 2.2 copy-done
  201.8 15.6 %attend.1 = bf16[2,512,512]{2,1,0:T(8,128)(2,1)S(1)} custom-call(s32[3]{0:T(128)S(1)} %pad_add_fusion.scalars, bf16[2,512,512]{2,1,0:T(8,128)(2,1)S(1)} %bitcast.65, bf16[2,2,2,512,512]{4,3,2,1,0:T(8,128)(2,1)S(1)} %copy-done, bf16[2,2,2,512,512]{4,3,2,1,0:T(8,128)(2,1)S(1)} %copy-done), custom_call_target="tpu_custom_call" | custom-call | bytes 45000000 | tf_op jit(solution)/shard_map/attend/pallas_call | solution.py:210
  217.4 10.7 all-gather.17.cloned.1.call-done.rhs
  229.6 191.6 %attn_out.1 = (f32[256,2048]{1,0:T(8,128)S(1)}, bf16[1024,2048]{1,0:T(8,128)(2,1)}) custom-call(bf16[1024,512]{1,0:T(8,128)(2,1)S(1)} %bitcast.63, bf16[2048,512]{1,0:T(8,128)(2,1)S(1)} %copy-done.22, f32[1024,2048]{1,0:T(8,128)} %copy-done.11, f32[1,2048]{1,0:T(1,128)S(1)} %bitcast.77, f32[1,2048]{1,0:T(1,128)S(1)} %slice.75.lg, f32[1,2048]{1,0:T(1,128)S(1)} %slice.76.lb), custom_call_target="tpu_custom_call" | custom-call | bytes 240000000 | tf_op jit(solution)/shard_map/attn_out/pallas_call | solution.py:486
  422.6 32.9 %mlp.1 = (bf16[1024,2048]{1,0:T(8,128)(2,1)S(1)}, bf16[1024,2048]{1,0:T(8,128)(2,1)}, f32[1,2048]{1,0:T(1,128)S(1)}) custom-call(bf16[1024,2048]{1,0:T(8,128)(2,1)} %get-tuple-element.57.mlp_in, bf16[1024,2048]{1,0:T(8,128)(2,1)} %bitcast_select_fusion.cot, bf16[2048,2048]{1,0:T(8,128)(2,1)} %all-gather.19.cloned.1.call-done.up.rhs, ...), custom_call_target="tpu_custom_call" | custom-call | bytes 75000000 | tf_op jit(solution)/shard_map/mlp/pallas_call | solution.py:936
  455.5 2.1 copy-done.18
  457.6 13.5 %convolution_convert_fusion = bf16[2048,2048]{1,0:T(8,128)(2,1)} fusion(bf16[1024,2048]{1,0:T(8,128)(2,1)S(1)} %copy-done.36, bf16[1024,2048]{1,0:T(8,128)(2,1)} %get-tuple-element.61.lhs), kind=kOutput, calls=%fused_computation.1 | convolution fusion | flops 8594128896 | bytes 16777216 | tf_op jit(solution)/shard_map/dot_general | solution.py:29
  471.0 14.2 %convolution_convert_fusion.1 = bf16[2048,2048]{1,0:T(8,128)(2,1)} fusion(bf16[1024,2048]{1,0:T(8,128)(2,1)} %bitcast_select_fusion.cot, bf16[1024,2048]{1,0:T(8,128)(2,1)} %copy-done.18), kind=kOutput, calls=%fused_computation.2 | convolution fusion | flops 8594128896 | bytes 16777216 | tf_op jit(solution)/shard_map/dot_general | solution.py:29
  485.2 156.9 %mlp_back.1 = (bf16[1024,2048]{1,0:T(8,128)(2,1)}, f32[3,2048]{1,0:T(4,128)S(1)}) custom-call(bf16[1024,2048]{1,0:T(8,128)(2,1)} %get-tuple-element.61.lhs, bf16[2048,2048]{1,0:T(8,128)(2,1)} %all-gather.19.cloned.1.call-done.up.rhs, f32[256,2048]{1,0:T(8,128)} %copy-done.10, bf16[1024,2048]{1,0:T(8,128)(2,1)} %bitcast_select_fusion.cot, f32[1,2048]{1,0:T(1,128)S(1)} %slice.75.lg), custom_call_target="tpu_custom_call" | custom-call | bytes 240000000 | tf_op jit(solution)/shard_map/mlp_back/pallas_call | solution.py:645
  642.1 4.6 convolution_convert_fusion.2
  646.7 23.7 %attend_back.1 = (bf16[2,512,512]{2,1,0:T(8,128)(2,1)S(1)}, bf16[2,2,2,512,512]{4,3,2,1,0:T(8,128)(2,1)}) custom-call(s32[3]{0:T(128)S(1)} %pad_add_fusion.scalars, bf16[2,512,512]{2,1,0:T(8,128)(2,1)S(1)} %bitcast.66, bf16[2,2,2,512,512]{4,3,2,1,0:T(8,128)(2,1)} %all-gather.15.cloned.1.call-done.k.v, ...), custom_call_target="tpu_custom_call" | custom-call | bytes 75000000 | tf_op jit(solution)/shard_map/attend_back/pallas_call | solution.py:260
  672.0 149.5 %mlp_out.1 = bf16[1024,2048]{1,0:T(8,128)(2,1)} custom-call(bf16[1024,2048]{1,0:T(8,128)(2,1)} %copy-done.18, bf16[2048,2048]{1,0:T(8,128)(2,1)} %all-gather.9.cloned.1.call-done.down.rhs, f32[256,2048]{1,0:T(8,128)} %copy-done.10, f32[1,2048]{1,0:T(1,128)S(1)} %bitcast.79), custom_call_target="tpu_custom_call" | custom-call | bytes 420000000 | tf_op jit(solution)/shard_map/mlp_out/pallas_call | solution.py:535
  827.3 19.0 %weight_grads.1 = bf16[2048,2048]{1,0:T(8,128)(2,1)} custom-call(bf16[3,1024,2048]{2,1,0:T(8,128)(2,1)} %get-tuple-element.55.lhs.normed, bf16[1024,2048]{1,0:T(8,128)(2,1)S(1)} %copy-done.3, bf16[3,1024,512]{2,1,0:T(8,128)(2,1)S(1)} %pad_maximum_fusion.grad_lin.lin, bf16[1024,512]{1,0:T(8,128)(2,1)S(1)} %bitcast.64), custom_call_target="tpu_custom_call" | custom-call | bytes 45000000 | tf_op jit(solution)/shard_map/weight_grads/pallas_call | solution.py:570
  847.7 3.1 convert_reduce_fusion
  850.8 265.5 %streams_back.1 = (bf16[3,1024,2048]{2,1,0:T(8,128)(2,1)}, f32[2,3,2048]{2,1,0:T(4,128)}) custom-call(bf16[3,1024,512]{2,1,0:T(8,128)(2,1)} %copy-done.1, bf16[8192,1536]{1,0:T(8,128)(2,1)} %all-gather.11.cloned.1.call-done.weight, bf16[4,1024,2048]{2,1,0:T(8,128)(2,1)} %bitcast.81, f32[1024,16]{1,0:T(8,128)} %copy-done.19, f32[4,2048]{1,0:T(4,128)} %lg.3), custom_call_target="tpu_custom_call" | custom-call | bytes 720000000 | tf_op jit(solution)/shard_map/streams_back/pallas_call | solution.py:812
  1117.8 2.2 copy-done.4
  1123.1 48.0 %last.1 = (f32[4,1024,2048]{2,1,0:T(8,128)}, f32[1,2048]{1,0:T(1,128)S(1)}, f32[16,2048]{1,0:T(8,128)S(1)}, f32[16,16]{1,0:T(8,128)S(1)}) custom-call(bf16[4,1024,2048]{2,1,0:T(8,128)(2,1)} %bitcast.82, bf16[3,1024,2048]{2,1,0:T(8,128)(2,1)} %get-tuple-element.79.streams, bf16[1024,2048]{1,0:T(8,128)(2,1)S(1)} %copy-done.4, f32[1024,16]{1,0:T(8,128)S(1)} %copy-done.20, ...), custom_call_target="tpu_custom_call" | custom-call | bytes 90000000 | tf_op jit(solution)/shard_map/last/pallas_call | solution.py:1035
  1171.3 27.7 %small_sums.1 = (f32[24,2048]{1,0:T(8,128)S(1)}, f32[32,128]{1,0:T(8,128)S(1)}) custom-call(f32[24,2048]{1,0:T(8,128)S(1)} %concatenate.33.ours, f32[8,32,128]{2,1,0:T(8,128)S(1)} %reshape.133.share), custom_call_target="tpu_custom_call" | custom-call | bytes 36000000 | tf_op jit(solution)/shard_map/small_sums/pallas_call | solution.py:896
  1202.9 2.9 convert_element_type.55
  1209.3 2.0 copy.47
  (159 shorter events, 35.2 us)
Async XLA Ops:
  7.2 4.4 copy-start.41
  7.2 4.6 copy-start.39
  7.2 4.7 copy-start.40
  7.2 25.7 %copy-start.30 = (f32[2048]{0:T(1024)S(1)}, f32[2048]{0:T(1024)}, u32[]{:S(2)}) copy-start(f32[2048]{0:T(1024)} %param.21) | copy-start | bytes 24580
  7.2 25.7 %copy-start.31 = (f32[16,16]{1,0:T(8,128)S(1)}, f32[16,16]{1,0:T(8,128)}, u32[]{:S(2)}) copy-start(f32[16,16]{1,0:T(8,128)} %w2.3) | copy-start | bytes 3076
  7.2 25.7 %copy-start.28 = (f32[4,2048]{1,0:T(4,128)S(1)}, f32[4,2048]{1,0:T(4,128)}, u32[]{:S(2)}) copy-start(f32[4,2048]{1,0:T(4,128)} %lg.3) | copy-start | bytes 98308
  7.2 25.7 %copy-start.29 = (f32[4,2048]{1,0:T(4,128)S(1)}, f32[4,2048]{1,0:T(4,128)}, u32[]{:S(2)}) copy-start(f32[4,2048]{1,0:T(4,128)} %lb.1) | copy-start | bytes 98308
  7.3 73.6 %all-gather.13.cloned.1.call-start = ((), (), s32[]{:S(2)}) async-start(), calls=%async_computation.6 | async-start | bytes 4718592 | tf_op jit(solution)/shard_map/all_gather | solution.py:1121
  10.1 99.1 %all-gather.9.cloned.1.call-start = ((), (), s32[]{:S(2)}) async-start(), calls=%async_computation.4 | async-start | bytes 9437184 | tf_op jit(solution)/shard_map/all_gather | solution.py:1125
  10.8 128.7 %all-gather.21.cloned.1.call-start = ((), (), s32[]{:S(2)}) async-start(), calls=%async_computation.14 | async-start | bytes 2359296 | tf_op jit(solution)/shard_map/all_gather | solution.py:1122
  11.6 186.8 %all-gather.15.cloned.1.call-start = ((), (), s32[]{:S(2)}) async-start(), calls=%async_computation.7 | async-start | bytes 6291456 | tf_op jit(solution)/shard_map/all_gather | solution.py:1141
  32.9 42.0 %copy-start.13 = (bf16[2048,16]{1,0:T(8,128)(2,1)}, bf16[2048,16]{1,0:T(8,128)(2,1)S(1)}, u32[]{:S(2)}) copy-start(bf16[2048,16]{1,0:T(8,128)(2,1)S(1)} %all_gather.26.w1) | copy-start | bytes 196612
  74.9 3.3 copy-start.11
  94.7 15.2 %copy-start.42 = (s32[2]{0:T(128)S(1)}, s32[2]{0:T(128)}, u32[]{:S(2)}) copy-start(s32[2]{0:T(128)} %param.19) | copy-start | bytes 28
  94.7 133.3 %all-gather.17.cloned.1.call-start = ((), (), s32[]{:S(2)}) async-start(), calls=%async_computation.8 | async-start | bytes 2359296 | tf_op jit(solution)/shard_map/all_gather | solution.py:1123
  95.3 327.3 %all-gather.19.cloned.1.call-start = ((), (), s32[]{:S(2)}) async-start(), calls=%async_computation.9 | async-start | bytes 9437184 | tf_op jit(solution)/shard_map/all_gather | solution.py:1124
  95.9 575.5 %all-gather.11.cloned.1.call-start = ((), (), s32[]{:S(2)}) async-start(), calls=%async_computation.5 | async-start | bytes 25952256 | tf_op jit(solution)/shard_map/all_gather | solution.py:1130
  109.2 712.4 %reduce-scatter.5.cloned.1.call-start = ((), (), s32[]{:S(2)}) async-start(), calls=%async_computation.10 | async-start | bytes 6291456 | tf_op jit(solution)/shard_map/reduce_scatter | solution.py:1158
  201.8 26.2 %copy-start.32 = (f32[2048]{0:T(1024)S(1)}, f32[2048]{0:T(1024)}, u32[]{:S(2)}) copy-start(f32[2048]{0:T(1024)} %param.29) | copy-start | bytes 24580
  217.4 203.9 %copy-start.5 = (bf16[2,512,512]{2,1,0:T(8,128)(2,1)}, bf16[2,512,512]{2,1,0:T(8,128)(2,1)S(1)}, u32[]{:S(2)}) copy-start(bf16[2,512,512]{2,1,0:T(8,128)(2,1)S(1)} %attend.1) | copy-start | bytes 3145732
  229.6 193.0 %copy-start.33 = (f32[2048]{0:T(1024)S(1)}, f32[2048]{0:T(1024)}, u32[]{:S(2)}) copy-start(f32[2048]{0:T(1024)} %param.31) | copy-start | bytes 24580
  422.6 35.0 %copy-start.36 = (bf16[1024,2048]{1,0:T(8,128)(2,1)S(1)}, bf16[1024,2048]{1,0:T(8,128)(2,1)}, u32[]{:S(2)}) copy-start(bf16[1024,2048]{1,0:T(8,128)(2,1)} %get-tuple-element.57.mlp_in) | copy-start | bytes 12582916
  485.2 156.9 %copy-start.23 = (bf16[2048,512]{1,0:T(8,128)(2,1)S(1)}, bf16[2048,512]{1,0:T(8,128)(2,1)}, u32[]{:S(2)}) copy-start(bf16[2048,512]{1,0:T(8,128)(2,1)} %all-gather.17.cloned.1.call-done.rhs) | copy-start | bytes 6291460
  642.1 4.6 copy-start.9
  671.4 446.3 %reduce-scatter.11.cloned.1.call-start = ((), (), s32[]{:S(2)}) async-start(), calls=%async_computation.13 | async-start | bytes 9437184 | tf_op jit(solution)/shard_map/reduce_scatter | solution.py:1164
  827.3 19.0 %copy-start.1 = (bf16[3,1024,512]{2,1,0:T(8,128)(2,1)}, bf16[3,1024,512]{2,1,0:T(8,128)(2,1)S(1)}, u32[]{:S(2)}) copy-start(bf16[3,1024,512]{2,1,0:T(8,128)(2,1)S(1)} %pad_maximum_fusion.grad_lin.lin) | copy-start | bytes 9437188
  846.3 271.4 %reduce-scatter.7.cloned.1.call-start = ((), (), s32[]{:S(2)}) async-start(), calls=%async_computation.11 | async-start | bytes 9437184 | tf_op jit(solution)/shard_map/reduce_scatter | solution.py:1161
  846.9 270.8 %reduce-scatter.9.cloned.1.call-start = ((), (), s32[]{:S(2)}) async-start(), calls=%async_computation.12 | async-start | bytes 9437184 | tf_op jit(solution)/shard_map/reduce_scatter | solution.py:1161
  850.8 266.4 %copy-start.2 = (bf16[3,1024,512]{2,1,0:T(8,128)(2,1)S(1)}, bf16[3,1024,512]{2,1,0:T(8,128)(2,1)}, u32[]{:S(2)}) copy-start(bf16[3,1024,512]{2,1,0:T(8,128)(2,1)} %copy-done.1) | copy-start | bytes 9437188
  1123.1 76.6 %copy-start.37 = (bf16[256,2048]{1,0:T(8,128)(2,1)S(1)}, bf16[256,2048]{1,0:T(8,128)(2,1)}, u32[]{:S(2)}) copy-start(bf16[256,2048]{1,0:T(8,128)(2,1)} %reduce-scatter.11.cloned.1.call-done) | copy-start | bytes 3145732
  1200.0 5.8 copy-start.38
  1202.9 6.4 copy-start.35
  (22 other events, 36.6 us)
Sparse Core Ops, SparseCore 0:
  10.5 42.2 all-gather.12
  54.7 54.3 all-gather.8
  111.6 27.8 all-gather.20
  141.5 56.8 all-gather.14
  200.1 27.8 all-gather.16
  229.8 54.3 all-gather.18
  287.1 216.9 all-gather.10
  671.5 53.6 reduce-scatter.4
  846.5 71.8 reduce-scatter.10
  921.7 71.2 reduce-scatter.6
  996.9 71.3 reduce-scatter.8

commit v3 on v2

--- a/solution.py
+++ b/solution.py
@@ -61,8 +61,68 @@
     return pl.CostEstimate(flops=0, bytes_accessed=int(micros * 3.0e6), transcendentals=0)
 
 
-def front_kernel(hist, gain, w1, w2, lg, lb, normed_out, resid_out, mix_out, pre_out, scratch):
+def owner_places(seqs, owners):
+    rank = lax.axis_index("dp") * seqs + lax.axis_index("seq")
+    peers = [lax.rem(rank + k, owners) for k in range(1, owners)]
+    return rank, peers, [{"dp": lax.div(p, seqs), "seq": lax.rem(p, seqs)} for p in peers]
+
+
+def push(source, target, sems, index, place):
+    return pltpu.make_async_remote_copy(
+        src_ref=source,
+        dst_ref=target,
+        send_sem=sems.at[0, index],
+        recv_sem=sems.at[1, index],
+        device_id=place,
+        device_id_type=MESH,
+    )
+
+
+def enter(places):
+    gate = pltpu.get_barrier_semaphore()
+    for place in places:
+        pl.semaphore_signal(gate, inc=1, device_id=place, device_id_type=MESH)
+    pl.semaphore_wait(gate, len(places))
+
+
+def front_kernel(
+    seqs, owners,
+    hist, gain, w1, w2, lg, lb, shard_out, shard_qkv,
+    normed_out, resid_out, mix_out, pre_out, w1_out, ring_out, ring_qkv,
+    scratch, w1_all, w1_sems, ring_sems, own_sems,
+):
     depth, rows, _ = hist.shape
+    index = pl.program_id(0)
+    ring = Ring(16)
+    rank, _, places = owner_places(seqs, owners)
+    w1_copies = [push(w1, w1_all.at[rank], w1_sems, k, p) for k, p in enumerate(places)]
+    spreads = [
+        Spread(ring, slots, ring_sems.at[i], 0, source)
+        for i, (slots, source) in enumerate(((ring_out, shard_out), (ring_qkv, shard_qkv)))
+    ]
+    local = [
+        pltpu.make_async_copy(shard_out, ring_out.at[ring.me], own_sems.at[0]),
+        pltpu.make_async_copy(shard_qkv, ring_qkv.at[ring.me], own_sems.at[1]),
+    ]
+
+    @pl.when(index == 0)
+    def _():
+        enter(places + [{"tensor": ring.left}, {"tensor": ring.right}])
+        for copy in w1_copies:
+            copy.start()
+        for copy in local:
+            copy.start()
+        for spread in spreads:
+            spread.begin()
+        w1_all[rank] = w1[...]
+        for copy in w1_copies:
+            copy.wait()
+        w1_out[...] = w1_all[...].reshape(w1_out.shape)
+
+    @pl.when(index == pl.num_programs(0) - 1)
+    def _():
+        for spread in spreads:
+            spread.relay()
 
     def rms(part):
         wide = hist[depth - 1, part, :].astype(F32)
@@ -70,7 +130,7 @@
         scratch[part, :] = (wide * scale * gain[...]).astype(BF)
 
     rows_loop(rows, 16, rms)
-    pre = dot(scratch[...], w1[...])
+    pre = dot(scratch[...], w1_out[...])
     pre_out[...] = pre
     mix_out[...] = dot(pre * normal_cdf(pre), w2[...], precision=EXACT)
 
@@ -91,14 +151,22 @@
 
     rows_loop(rows, 16, combine)
 
-
-def front(layers, gain, w1, w2, lg, lb):
+    @pl.when(index == pl.num_programs(0) - 1)
+    def _():
+        for spread in spreads:
+            spread.arrive()
+            spread.finish()
+        for copy in local:
+            copy.wait()
+
+
+def front(layers, gain, w1, w2, lg, lb, shard_out, shard_qkv, seqs, owners):
     depth, rows, feats = layers.shape
     tile = min(128, rows)
     hidden = w1.shape[1]
     full = lambda shape: pl.BlockSpec(shape, lambda i: (0,) * len(shape))
     return pl.pallas_call(
-        front_kernel,
+        functools.partial(front_kernel, seqs, owners),
         grid=(rows // tile,),
         in_specs=[
             pl.BlockSpec((depth, tile, feats), lambda i: (0, i, 0)),
@@ -107,24 +175,38 @@
             full(w2.shape),
             full(lg.shape),
             full(lb.shape),
+            ANY,
+            ANY,
         ],
         out_specs=[
             pl.BlockSpec((3, tile, feats), lambda i: (0, i, 0)),
             pl.BlockSpec((tile, feats), lambda i: (i, 0)),
             pl.BlockSpec((tile, STREAMS * depth), lambda i: (i, 0)),
             pl.BlockSpec((tile, hidden), lambda i: (i, 0)),
+            full((feats, hidden)),
+            ANY,
+            ANY,
         ],
         out_shape=[
             jax.ShapeDtypeStruct((3, rows, feats), BF),
             jax.ShapeDtypeStruct((rows, feats), F32),
             jax.ShapeDtypeStruct((rows, STREAMS * depth), F32),
             jax.ShapeDtypeStruct((rows, hidden), F32),
-        ],
-        scratch_shapes=[pltpu.VMEM((tile, feats), BF)],
-        compiler_params=params(40),
-        cost_estimate=cost(20),
+            jax.ShapeDtypeStruct((feats, hidden), BF),
+            jax.ShapeDtypeStruct((RING,) + shard_out.shape, BF),
+            jax.ShapeDtypeStruct((RING,) + shard_qkv.shape, BF),
+        ],
+        scratch_shapes=[
+            pltpu.VMEM((tile, feats), BF),
+            pltpu.VMEM((owners,) + w1.shape, BF),
+            pltpu.SemaphoreType.DMA((2, owners - 1)),
+            pltpu.SemaphoreType.DMA((2, 2, 4)),
+            pltpu.SemaphoreType.DMA((2,)),
+        ],
+        compiler_params=params(48, 5),
+        cost_estimate=cost(70),
         name="front",
-    )(layers, gain.reshape(1, feats), w1, w2, lg, lb)
+    )(layers, gain.reshape(1, feats), w1, w2, lg, lb, shard_out, shard_qkv)
 
 
 def turn(values, tables, sign):
@@ -187,6 +269,58 @@
         cost_estimate=cost(4 * count),
         name="project",
     )(normed, weight, bias.reshape(count, 1, width), tables)
+
+
+def share_kernel(lhs, weight, bias, tables, kv, q_out, kv_out, sems, own_sem):
+    seqs = kv_out.shape[0]
+    me = lax.axis_index("seq")
+    places = [{"seq": lax.rem(me + k, seqs)} for k in range(1, seqs)]
+    local = pltpu.make_async_copy(kv, kv_out.at[me], own_sem)
+    local.start()
+    enter(places)
+    copies = [push(kv, kv_out.at[me], sems, k, place) for k, place in enumerate(places)]
+    for copy in copies:
+        copy.start()
+
+    def rows(part):
+        value = dot(lhs[0, part, :], weight[...]) + bias[...]
+        tabs = (tables[0, part, :], tables[1, part, :], tables[2, part, :])
+        for head in range(value.shape[1] // HEAD_DIM):
+            cols = slice(head * HEAD_DIM, (head + 1) * HEAD_DIM)
+            q_out[part, cols] = turn(value[:, cols], tabs, 1.0).astype(BF)
+
+    rows_loop(lhs.shape[1], 256, rows)
+    for copy in copies:
+        copy.wait()
+    local.wait()
+
+
+def share(normed, weight, bias, tables, kv, seqs):
+    _, rows, feats = normed.shape
+    width = weight.shape[1]
+    return pl.pallas_call(
+        share_kernel,
+        grid=(1,),
+        in_specs=[
+            pl.BlockSpec((1, rows, feats), lambda i: (0, 0, 0)),
+            pl.BlockSpec(weight.shape, lambda i: (0, 0)),
+            pl.BlockSpec(bias.shape, lambda i: (0, 0)),
+            pl.BlockSpec(tables.shape, lambda i: (0, 0, 0)),
+            ANY,
+        ],
+        out_specs=[pl.BlockSpec((rows, width), lambda i: (0, 0)), ANY],
+        out_shape=[
+            jax.ShapeDtypeStruct((rows, width), BF),
+            jax.ShapeDtypeStruct((seqs,) + kv.shape, BF),
+        ],
+        scratch_shapes=[
+            pltpu.SemaphoreType.DMA((2, seqs - 1)),
+            pltpu.SemaphoreType.DMA,
+        ],
+        compiler_params=params(48, 6),
+        cost_estimate=cost(50),
+        name="share",
+    )(normed, weight, bias, tables, kv)
 
 
 def attend_kernel(scalars, q, k, v, out):
@@ -447,107 +581,145 @@
     return total[part, :] + near[0, part, :].astype(F32) + near[1, part, :].astype(F32)
 
 
+def weight_copies(weight, target, sems, index):
+    count = weight.shape[-2]
+
+    def one(owner):
+        source = weight.at[owner] if index is None else weight.at[owner, :, index]
+        return pltpu.make_async_copy(
+            source,
+            target.at[:, pl.ds(pl.multiple_of(owner * count, count), count), :],
+            sems.at[owner],
+        )
+
+    def every(act):
+        def step(owner, carry):
+            act(one(owner))
+            return carry
+
+        lax.fori_loop(0, weight.shape[0], step, 0)
+
+    return every
+
+
+def ring_product(slots, weight, part, total):
+    def columns(cols):
+        value = dot(slots[0, part, :], weight[0, cols, :], NT)
+        for z in range(1, RING):
+            value += dot(slots[z, part, :], weight[z, cols, :], NT)
+        total[:, cols] = value
+
+    rows_loop(total.shape[1], 512, columns)
+
+
 def attn_out_kernel(
-    lhs, rhs, resid, bias, lg, lb, hidden_out, mlp_out,
-    far, near, far_in, near_in, total, base_rows, own, sems, local_sems,
+    vals, weight, resid, bias, lg, lb, hidden_out, mlp_out,
+    slots, weights, total, base_rows, stage, sems, weight_sems, base_sem, stage_sems, own_sem,
 ):
     chunk, feats = total.shape
     ring = Ring(chunk)
-    fetch = pltpu.make_async_copy(
-        resid.at[pl.ds(ring.at(ring.me), chunk), :], base_rows, local_sems.at[0]
-    )
-    fetch.start()
+    load = weight_copies(weight, weights, weight_sems, None)
+    load(lambda copy: copy.start())
+    local = pltpu.make_async_copy(vals, slots.at[ring.me], own_sem)
+    local.start()
     ring.barrier()
-    scatter = Scatter(ring, lhs, rhs, far, near, far_in, near_in, sems)
-    scatter.begin()
-    scatter.relay()
-    own_sum(scatter, total)
-    fetch.wait()
-    scatter.arrive()
-
-    def norm(part):
-        value = base_rows[part, :] + (whole_sum(scatter, total, part) + bias[...])
-        hidden_out[part, :] = value
-        centred = value - mean_last(value)
-        inverse = lax.rsqrt(mean_last(centred * centred) + NORM_EPSILON)
-        own[part, :] = (centred * inverse * lg[...] + lb[...]).astype(BF)
-
-    rows_loop(chunk, 16, norm)
-    gather = Gather(ring, own, mlp_out, sems, 6, local_sems.at[1])
-    gather.begin()
-    gather.relay()
-    scatter.finish()
-    gather.finish()
-
-
-def attn_out(lhs, rhs, resid, bias, lg, lb):
+    spread = Spread(ring, slots, sems, 0, vals)
+    spread.begin()
+    spread.relay()
+    load(lambda copy: copy.wait())
+    local.wait()
+    spread.arrive()
+
+    def write_out(index, slot):
+        part = pl.ds(pl.multiple_of(index * chunk, chunk), chunk)
+        return pltpu.make_async_copy(stage.at[slot], mlp_out.at[part, :], stage_sems.at[slot])
+
+    def one(index, carry):
+        part = pl.ds(pl.multiple_of(index * chunk, chunk), chunk)
+        fetch = pltpu.make_async_copy(resid.at[part, :], base_rows, base_sem)
+        fetch.start()
+        slot = lax.rem(index, 2)
+        ring_product(slots, weights, part, total)
+        fetch.wait()
+
+        @pl.when(index >= 2)
+        def _():
+            write_out(index - 2, slot).wait()
+
+        def norm(sub):
+            value = base_rows[sub, :] + (total[sub, :] + bias[...])
+            total[sub, :] = value
+            centred = value - mean_last(value)
+            inverse = lax.rsqrt(mean_last(centred * centred) + NORM_EPSILON)
+            stage[slot, sub, :] = (centred * inverse * lg[...] + lb[...]).astype(BF)
+
+        rows_loop(chunk, 16, norm)
+        write_out(index, slot).start()
+
+        @pl.when(index == ring.me)
+        def _():
+            hidden_out[...] = total[...]
+
+        return carry
+
+    lax.fori_loop(0, RING, one, 0)
+    for index in range(RING - 2, RING):
+        write_out(index, index % 2).wait()
+    spread.finish()
+
+
+def attn_out(vals, weight, resid, bias, lg, lb):
     rows, feats = resid.shape
+    width = vals.shape[1]
     chunk = rows // RING
     return pl.pallas_call(
         attn_out_kernel,
-        in_specs=[VMEM, VMEM, ANY, VMEM, VMEM, VMEM],
+        in_specs=[VMEM, ANY, ANY, VMEM, VMEM, VMEM],
         out_specs=[VMEM, ANY],
         out_shape=[
             jax.ShapeDtypeStruct((chunk, feats), F32),
             jax.ShapeDtypeStruct((rows, feats), BF),
         ],
-        scratch_shapes=scatter_scratch(chunk, feats)
-        + [
+        scratch_shapes=[
+            pltpu.VMEM((RING, rows, width), BF),
+            pltpu.VMEM((RING, feats, width), BF),
             pltpu.VMEM((chunk, feats), F32),
             pltpu.VMEM((chunk, feats), F32),
-            pltpu.VMEM((chunk, feats), BF),
-            pltpu.SemaphoreType.DMA((2, 10)),
+            pltpu.VMEM((2, chunk, feats), BF),
+            pltpu.SemaphoreType.DMA((2, 4)),
+            pltpu.SemaphoreType.DMA((weight.shape[0],)),
+            pltpu.SemaphoreType.DMA,
             pltpu.SemaphoreType.DMA((2,)),
+            pltpu.SemaphoreType.DMA,
         ],
         compiler_params=params(48, 0),
-        cost_estimate=cost(80),
+        cost_estimate=cost(95),
         name="attn_out",
-    )(lhs, rhs, resid, bias, lg, lb)
-
-
-def mlp_out_kernel(
-    lhs, rhs, hidden, bias, out,
-    far, near, far_in, near_in, total, own, sems, local_sems,
-):
-    chunk, feats = total.shape
+    )(vals, weight, resid, bias, lg, lb)
+
+
+def layer_out_kernel(own, out, sems, own_sem):
+    chunk = own.shape[0]
     ring = Ring(chunk)
     ring.barrier()
-    scatter = Scatter(ring, lhs, rhs, far, near, far_in, near_in, sems)
-    scatter.begin()
-    scatter.relay()
-    own_sum(scatter, total)
-    scatter.arrive()
-
-    def add(part):
-        own[part, :] = (hidden[part, :] + (whole_sum(scatter, total, part) + bias[...])).astype(BF)
-
-    rows_loop(chunk, 16, add)
-    gather = Gather(ring, own, out, sems, 6, local_sems.at[0])
+    gather = Gather(ring, own, out, sems, 0, own_sem)
     gather.begin()
     gather.relay()
-    scatter.finish()
     gather.finish()
 
 
-def mlp_out(lhs, rhs, hidden, bias):
-    rows = lhs.shape[0]
-    chunk, feats = hidden.shape
+def spread_rows(own):
+    chunk, feats = own.shape
     return pl.pallas_call(
-        mlp_out_kernel,
-        in_specs=[VMEM, VMEM, VMEM, VMEM],
+        layer_out_kernel,
+        in_specs=[VMEM],
         out_specs=ANY,
-        out_shape=jax.ShapeDtypeStruct((rows, feats), BF),
-        scratch_shapes=scatter_scratch(chunk, feats)
-        + [
-            pltpu.VMEM((chunk, feats), F32),
-            pltpu.VMEM((chunk, feats), BF),
-            pltpu.SemaphoreType.DMA((2, 10)),
-            pltpu.SemaphoreType.DMA((1,)),
-        ],
-        compiler_params=params(52, 3),
-        cost_estimate=cost(140),
-        name="mlp_out",
-    )(lhs, rhs, hidden, bias)
+        out_shape=jax.ShapeDtypeStruct((RING * chunk, feats), BF),
+        scratch_shapes=[pltpu.SemaphoreType.DMA((2, 4)), pltpu.SemaphoreType.DMA],
+        compiler_params=params(32, 3),
+        cost_estimate=cost(72),
+        name="spread_rows",
+    )(own)
 
 
 def weights_kernel(normed, grad_attn, grad_lin, attn_vals, out):
@@ -601,27 +773,197 @@
     return jnp.sum(values.reshape(rows // 8, 8, feats), axis=0)
 
 
+def weight_product(source, rhs, out, blocks, stage, load_sems, store_sems):
+    width = blocks.shape[2]
+    count = source.shape[1] // width
+
+    def load(n, slot):
+        cols = pl.ds(pl.multiple_of(n * width, width), width)
+        return pltpu.make_async_copy(source.at[:, cols], blocks.at[slot], load_sems.at[slot])
+
+    def store(n, slot):
+        part = pl.ds(pl.multiple_of(n * width, width), width)
+        return pltpu.make_async_copy(stage.at[slot], out.at[part, :], store_sems.at[slot])
+
+    load(0, 0).start()
+
+    def one(n, carry):
+        slot = lax.rem(n, 2)
+
+        @pl.when(n + 1 < count)
+        def _():
+            load(n + 1, 1 - slot).start()
+
+        load(n, slot).wait()
+
+        @pl.when(n >= 2)
+        def _():
+            store(n - 2, slot).wait()
+
+        def columns(cols):
+            stage[slot, :, cols] = dot(blocks[slot], rhs[:, cols], TN).astype(BF)
+
+        rows_loop(rhs.shape[1], 512, columns)
+        store(n, slot).start()
+        return carry
+
+    lax.fori_loop(0, count, one, 0)
+    for n in range(count - 2, count):
+        store(n, n % 2).wait()
+
+
+class Line:
+    def __init__(self, chunk):
+        me = lax.axis_index("tensor")
+        self.me, self.chunk = me, chunk
+        self.low = me < 2
+        self.outer = (me == 0) | (me == RING - 1)
+        self.inner = (me == 1) | (me == RING - 2)
+        self.up = jnp.where(self.low, me + 1, me - 1)
+        self.down = jnp.where(self.low, lax.max(me - 1, 0), lax.min(me + 1, RING - 1))
+
+    def at(self, number):
+        index = jnp.where(self.low, number, RING - 1 - number)
+        return pl.ds(pl.multiple_of(index * self.chunk, self.chunk), self.chunk)
+
+    def barrier(self):
+        gate = pltpu.get_barrier_semaphore()
+        pl.semaphore_signal(gate, inc=1, device_id={"tensor": self.up}, device_id_type=MESH)
+
+        @pl.when(self.inner)
+        def _():
+            pl.semaphore_signal(
+                gate, inc=1, device_id={"tensor": self.down}, device_id_type=MESH
+            )
+            pl.semaphore_wait(gate, 2)
+
+        @pl.when(self.outer)
+        def _():
+            pl.semaphore_wait(gate, 1)
+
+
+class LineSum:
+    def __init__(self, line, lhs, rhs, outbound, inbound, sems, base):
+        self.line, self.lhs, self.rhs = line, lhs, rhs
+        self.outbound, self.inbound = outbound, inbound
+        copy = lambda slot, target, device: remote(
+            outbound.at[slot], inbound.at[target], sems, base + target, device
+        )
+        self.inward = [copy(i, i, line.up) for i in range(3)]
+        self.across = [copy(i, 3 + i, line.up) for i in range(2)]
+        self.outward = remote(outbound.at[2], inbound.at[5], sems, base + 5, line.down)
+
+    def partial(self, number, slot, arrived=None):
+        rows = self.line.at(number)
+
+        def write(cols, value):
+            if arrived is not None:
+                value = value + self.inbound[arrived, :, cols].astype(F32)
+            self.outbound[slot, :, cols] = value.astype(BF)
+
+        product(self.lhs, self.rhs, rows.start, self.line.chunk, write)
+
+    def own(self, total):
+        index = self.line.me * self.line.chunk
+
+        def write(cols, value):
+            total[:, cols] = value
+
+        product(
+            self.lhs, self.rhs, pl.multiple_of(index, self.line.chunk), self.line.chunk, write
+        )
+
+    def send_inward(self):
+        for slot, copy in enumerate(self.inward):
+            self.partial(3 - slot, slot)
+            copy.start()
+
+    def send_across(self, i):
+        self.inward[i].wait_recv()
+        self.partial(3 - i, i, i)
+        self.across[i].start()
+
+    def send_outward(self):
+        self.across[0].wait_recv()
+        self.partial(0, 2, 3)
+        self.outward.start()
+
+    def arrive(self):
+        line = self.line
+
+        @pl.when(line.inner)
+        def _():
+            self.inward[2].wait_recv()
+            self.across[1].wait_recv()
+
+        @pl.when(line.outer)
+        def _():
+            self.outward.wait_recv()
+
+    def sent(self):
+        line = self.line
+
+        @pl.when(line.inner)
+        def _():
+            for copy in self.across + [self.outward]:
+                copy.wait_send()
+
+        @pl.when(line.outer)
+        def _():
+            for copy in self.inward:
+                copy.wait_send()
+
+    def clear(self):
+        @pl.when(self.line.outer)
+        def _():
+            self.inbound[2] = jnp.zeros_like(self.inbound[2])
+
+    def whole(self, total, part):
+        last = jnp.where(self.line.outer, 5, 4)
+        return (
+            total[part, :]
+            + self.inbound[2, part, :].astype(F32)
+            + self.inbound[last, part, :].astype(F32)
+        )
+
+
 def mlp_back_kernel(
-    lhs, rhs, hidden, cot, lg, grad_out, small_out,
-    far, near, far_in, near_in, total, cot_rows, own, sums, sems, local_sems,
+    lhs, rhs, acts, down, hidden, cot, mlp_in, lg, down_bias,
+    grad_out, small_out, rows_out, grad_up, grad_down,
+    outbound, inbound, total, cot_rows, own, sums, blocks, stage,
+    sems, gather_sems, local_sems, load_sems, store_sems,
 ):
     chunk, feats = total.shape
-    ring = Ring(chunk)
-    fetch = pltpu.make_async_copy(
-        cot.at[pl.ds(ring.at(ring.me), chunk), :], cot_rows, local_sems.at[0]
-    )
+    line = Line(chunk)
+    mine = pl.ds(pl.multiple_of(line.me * chunk, chunk), chunk)
+    fetch = pltpu.make_async_copy(cot.at[mine, :], cot_rows, local_sems.at[0])
     fetch.start()
-    ring.barrier()
-    scatter = Scatter(ring, lhs, rhs, far, near, far_in, near_in, sems)
-    scatter.begin()
-    scatter.relay()
-    own_sum(scatter, total)
+    line.barrier()
+    first = LineSum(line, lhs, rhs, outbound, inbound.at[0], sems.at[0], 0)
+    second = LineSum(line, acts, down, outbound, inbound.at[1], sems.at[1], 0)
+    first.clear()
+    second.clear()
+
+    @pl.when(line.outer)
+    def _():
+        first.send_inward()
+
+    first.own(total)
+    sums[...] = jnp.zeros_like(sums)
+    weight_product(mlp_in, lhs, grad_up, blocks, stage, load_sems, store_sems)
+
+    @pl.when(line.inner)
+    def _():
+        first.send_across(0)
+        first.send_across(1)
+        first.send_outward()
+
+    weight_product(cot, acts, grad_down, blocks, stage, load_sems, store_sems)
     fetch.wait()
-    sums[...] = jnp.zeros_like(sums)
-    scatter.arrive()
+    first.arrive()
 
     def back(part):
-        grads = whole_sum(scatter, total, part)
+        grads = first.whole(total, part)
         step, normed = norm_back(hidden[part, :], grads, lg[...])
         low = (cot_rows[part, :].astype(F32) + step).astype(BF)
         own[part, :] = low
@@ -630,48 +972,102 @@
         sums[2] += fold(low.astype(F32))
 
     rows_loop(chunk, 16, back)
-    gather = Gather(ring, own, grad_out, sems, 6, local_sems.at[1])
-    gather.begin()
+    local = pltpu.make_async_copy(own, grad_out.at[mine, :], local_sems.at[1])
+    local.start()
+    first.sent()
+
+    def chunk_copy(number, index, device, source=None):
+        rows = grad_out.at[line.at(number), :]
+        return remote(rows if source is None else source, rows, gather_sems, index, device)
+
+    @pl.when(line.outer)
+    def _():
+        onward = chunk_copy(0, 0, line.up, own)
+        onward.start()
+        second.send_inward()
+        second.own(total)
+        for number in range(1, RING):
+            chunk_copy(number, 2 + number, line.up).wait_recv()
+        onward.wait_send()
+
+    @pl.when(line.inner)
+    def _():
+        inward = [chunk_copy(1, 1, line.up, own), chunk_copy(1, 3, line.down, own)]
+        for copy in inward:
+            copy.start()
+        second.own(total)
+        chunk_copy(0, 0, line.up).wait_recv()
+        relay = chunk_copy(0, 2, line.up)
+        relay.start()
+        chunk_copy(2, 1, line.up).wait_recv()
+        near = chunk_copy(2, 4, line.down)
+        near.start()
+        second.send_across(0)
+        chunk_copy(3, 2, line.up).wait_recv()
+        far = chunk_copy(3, 5, line.down)
+        far.start()
+        second.send_across(1)
+        second.send_outward()
+        for copy in inward + [relay, near, far]:
+            copy.wait_send()
+
     for i in range(3):
         small_out[i : i + 1, :] = jnp.sum(sums[i], axis=0, keepdims=True)
-    gather.relay()
-    scatter.finish()
-    gather.finish()
-
-
-def mlp_back(lhs, rhs, hidden, cot, lg):
+    second.arrive()
+
+    def add(part):
+        value = hidden[part, :] + (second.whole(total, part) + down_bias[...])
+        rows_out[part, :] = value.astype(BF)
+
+    rows_loop(chunk, 16, add)
+    second.sent()
+    local.wait()
+
+
+def mlp_back(lhs, rhs, acts, down, hidden, cot, mlp_in, lg, down_bias):
     rows, feats = cot.shape
+    width = lhs.shape[1]
     chunk = rows // RING
+    block = 256
     return pl.pallas_call(
         mlp_back_kernel,
-        in_specs=[VMEM, VMEM, VMEM, ANY, VMEM],
-        out_specs=[ANY, VMEM],
+        in_specs=[VMEM, VMEM, VMEM, VMEM, VMEM, ANY, ANY, VMEM, VMEM],
+        out_specs=[ANY, VMEM, VMEM, ANY, ANY],
         out_shape=[
             jax.ShapeDtypeStruct((rows, feats), BF),
             jax.ShapeDtypeStruct((3, feats), F32),
-        ],
-        scratch_shapes=scatter_scratch(chunk, feats)
-        + [
+            jax.ShapeDtypeStruct((chunk, feats), BF),
+            jax.ShapeDtypeStruct((feats, width), BF),
+            jax.ShapeDtypeStruct((feats, width), BF),
+        ],
+        scratch_shapes=[
+            pltpu.VMEM((3, chunk, feats), BF),
+            pltpu.VMEM((2, 6, chunk, feats), BF),
             pltpu.VMEM((chunk, feats), F32),
             pltpu.VMEM((chunk, feats), BF),
             pltpu.VMEM((chunk, feats), BF),
             pltpu.VMEM((3, 8, feats), F32),
-            pltpu.SemaphoreType.DMA((2, 10)),
+            pltpu.VMEM((2, rows, block), BF),
+            pltpu.VMEM((2, block, width), BF),
+            pltpu.SemaphoreType.DMA((2, 2, 6)),
+            pltpu.SemaphoreType.DMA((2, 6)),
             pltpu.SemaphoreType.DMA((2,)),
-        ],
-        compiler_params=params(52, 1),
-        cost_estimate=cost(80),
+            pltpu.SemaphoreType.DMA((2,)),
+            pltpu.SemaphoreType.DMA((2,)),
+        ],
+        compiler_params=params(60, 1),
+        cost_estimate=cost(175),
         name="mlp_back",
-    )(lhs, rhs, hidden, cot, lg)
+    )(lhs, rhs, acts, down, hidden, cot, mlp_in, lg, down_bias)
 
 
 class Spread:
-    def __init__(self, ring, slots, sems, base):
+    def __init__(self, ring, slots, sems, base, source):
         half = slots.shape[1] // 2
         mine = slots.at[ring.me]
         self.first = [
-            remote(mine, mine, sems, base, ring.right),
-            remote(mine, mine, sems, base + 1, ring.left),
+            remote(source, mine, sems, base, ring.right),
+            remote(source, mine, sems, base + 1, ring.left),
         ]
         up = slots.at[ring.left, pl.ds(0, half), :]
         down = slots.at[ring.right, pl.ds(half, half), :]
@@ -709,14 +1105,9 @@
     ring = Ring(rows)
 
     def fetch(stream):
-        return [
-            pltpu.make_async_copy(
-                weight.at[pl.ds(z * feats, feats), pl.ds(stream * width, width)],
-                weights.at[stream % 2, z],
-                weight_sems.at[stream % 2, z],
-            )
-            for z in range(RING)
-        ]
+        return weight_copies(
+            weight, weights.at[stream % 2], weight_sems.at[stream % 2], stream
+        )
 
     local = [
         pltpu.make_async_copy(lin.at[i], slots.at[i, ring.me], own_sems.at[i]) for i in range(3)
@@ -724,11 +1115,10 @@
     for copy in local:
         copy.start()
     for stream in range(2):
-        for copy in fetch(stream):
-            copy.start()
+        fetch(stream)(lambda copy: copy.start())
     sums[...] = jnp.zeros_like(sums)
     ring.barrier()
-    spreads = [Spread(ring, slots.at[i], sems.at[i], 0) for i in range(3)]
+    spreads = [Spread(ring, slots.at[i], sems.at[i], 0, lin.at[i]) for i in range(3)]
 
     def write_out(stream, index, slot):
         part = pl.ds(pl.multiple_of(index * tile, tile), tile)
@@ -737,8 +1127,7 @@
         )
 
     def compute(stream):
-        for copy in fetch(stream):
-            copy.wait()
+        fetch(stream)(lambda copy: copy.wait())
 
         def one(index, carry):
             part = pl.ds(pl.multiple_of(index * tile, tile), tile)
@@ -746,13 +1135,7 @@
             load.start()
             slot = lax.rem(index, 2)
 
-            def columns(cols):
-                value = dot(slots[stream, 0, part, :], weights[stream % 2, 0, cols, :], NT)
-                for z in range(1, RING):
-                    value += dot(slots[stream, z, part, :], weights[stream % 2, z, cols, :], NT)
-                total[:, cols] = value
-
-            rows_loop(feats, 512, columns)
+            ring_product(slots.at[stream], weights.at[stream % 2], part, total)
             load.wait()
 
             @pl.when(index >= 2)
@@ -781,8 +1164,7 @@
         for index in range(max(tiles - 2, 0), tiles):
             write_out(stream, index, index % 2).wait()
         if stream == 0:
-            for copy in fetch(2):
-                copy.start()
+            fetch(2)(lambda copy: copy.start())
 
     for copy in local:
         copy.wait()
@@ -825,7 +1207,7 @@
             pltpu.VMEM((2, tile, feats), BF),
             pltpu.VMEM((3, 2, 8, feats), F32),
             pltpu.SemaphoreType.DMA((3, 2, 4)),
-            pltpu.SemaphoreType.DMA((2, RING)),
+            pltpu.SemaphoreType.DMA((2, weight.shape[0])),
             pltpu.SemaphoreType.DMA,
             pltpu.SemaphoreType.DMA((2,)),
             pltpu.SemaphoreType.DMA((3,)),
@@ -839,32 +1221,17 @@
 def small_kernel(seqs, owners, ours, share, out, share_out, near, all_ours, all_shares, near_sems, sems):
     ring = Ring(2)
     near_rows = near.shape[1]
-    rank = lax.axis_index("dp") * seqs + lax.axis_index("seq")
-    peers = [lax.rem(rank + k, owners) for k in range(1, owners)]
-    places = [{"dp": lax.div(p, seqs), "seq": lax.rem(p, seqs)} for p in peers]
+    rank, peers, places = owner_places(seqs, owners)
     mates = [ring.right, ring.far, ring.left]
-    gate = pltpu.get_barrier_semaphore()
-    for place in places + [{"tensor": z} for z in mates]:
-        pl.semaphore_signal(gate, inc=1, device_id=place, device_id_type=MESH)
-    pl.semaphore_wait(gate, len(places) + len(mates))
-
-    def send(source, target, pair, index, place):
-        return pltpu.make_async_remote_copy(
-            src_ref=source,
-            dst_ref=target,
-            send_sem=pair.at[0, index],
-            recv_sem=pair.at[1, index],
-            device_id=place,
-            device_id_type=MESH,
-        )
+    enter(places + [{"tensor": z} for z in mates])
 
     near[ring.me] = ours[0:near_rows, :]
     shares = [
-        send(share.at[p], all_shares.at[rank], sems.at[0], k, place)
+        push(share.at[p], all_shares.at[rank], sems.at[0], k, place)
         for k, (p, place) in enumerate(zip(peers, places))
     ]
     first = [
-        send(near.at[ring.me], near.at[ring.me], near_sems, k, {"tensor": z})
+        push(near.at[ring.me], near.at[ring.me], near_sems, k, {"tensor": z})
         for k, z in enumerate(mates)
     ]
     for copy in first + shares:
@@ -875,7 +1242,7 @@
     all_ours[rank, near_rows:, :] = ours[near_rows:, :]
     all_shares[rank] = share[rank]
     second = [
-        send(all_ours.at[rank], all_ours.at[rank], sems.at[1], k, place)
+        push(all_ours.at[rank], all_ours.at[rank], sems.at[1], k, place)
         for k, place in enumerate(places)
     ]
     for copy in second:
@@ -1116,18 +1483,12 @@
     owners = ("dp", "seq")
     layers = history.reshape(depth, rows, feats)
 
-    w_mix = lax.all_gather(mix_w1, owners, axis=0, tiled=True)
-    kv_shard = jnp.concatenate([qkv_weight[1], qkv_weight[2]], axis=1)
-    w_kv = lax.all_gather(kv_shard, owners, axis=0, tiled=True)
-    w_q = lax.all_gather(qkv_weight[0], owners, axis=0, tiled=True)
-    w_out = lax.all_gather(out_weight, owners, axis=0, tiled=True)
-    w_up = lax.all_gather(up_weight, owners, axis=0, tiled=True)
-    w_down = lax.all_gather(down_weight, owners, axis=0, tiled=True)
+    seqs = lax.axis_size("seq")
+    count = lax.axis_size("dp") * seqs
     tie = lax.optimization_barrier
-    qkv_shard, w_down = tie(
-        (jnp.concatenate([qkv_weight[0], qkv_weight[1], qkv_weight[2]], axis=1), w_down)
-    )
-    w_qkv = lax.all_gather(qkv_shard, ("tensor",) + owners, axis=0, tiled=True)
+    gather = functools.partial(lax.all_gather, axis_name=owners, axis=0)
+    w_kv = gather(jnp.concatenate([qkv_weight[1], qkv_weight[2]], axis=1), tiled=True)
+    w_q = gather(qkv_weight[0], tiled=True)
 
     offset = lax.axis_index("seq") * block_len
     query_place = offset + jnp.arange(block_len, dtype=jnp.int32)
@@ -1136,27 +1497,37 @@
     scalars = jnp.concatenate([lengths, offset[None].astype(jnp.int32)])
     tables = rotary_tables(positions.reshape(rows))
 
-    normed, resid, mix, pre = front(layers, mix_gain, w_mix, mix_w2, ln_gain, ln_bias)
+    normed, resid, mix, pre, w_mix, ring_out, ring_qkv = front(
+        layers, mix_gain, mix_w1, mix_w2, ln_gain, ln_bias, out_weight,
+        qkv_weight.reshape(-1, width), seqs, count
+    )
+    w_out_all = gather(ring_out)
     kv = project(normed, w_kv, qkv_bias[1:], tables, 1)
-    kv_all = lax.all_gather(kv.reshape(2, slots, block_len, width), "seq", axis=0)
-    q = project(normed, w_q, qkv_bias[:1], tables, 0)[0]
+    kv, up_weight, down_weight = tie((kv, up_weight, down_weight))
+    w_up, w_down = gather(up_weight, tiled=True), gather(down_weight, tiled=True)
+    q, kv_all = share(normed, w_q, qkv_bias[:1], tables, kv, seqs)
+    kv_all = kv_all.reshape(seqs, 2, slots, block_len, width)
     attn_vals = attend(scalars, q, kv_all, heads).reshape(rows, width)
+    attn_vals, ring_qkv = tie((attn_vals, ring_qkv))
+    w_qkv = gather(ring_qkv.reshape((RING,) + qkv_weight.shape))
     hidden, mlp_in = attn_out(
-        attn_vals, w_out, resid, out_bias[None, :], ln_gain[3:4], ln_bias[3:4]
+        attn_vals, w_out_all, resid, out_bias[None, :], ln_gain[3:4], ln_bias[3:4]
     )
+    w_out = lax.dynamic_index_in_dim(
+        w_out_all, lax.axis_index("tensor"), 1, keepdims=False
+    ).reshape(feats, width)
     up_act, grad_up, grad_up_bias = mlp(mlp_in, cot, w_up, w_down, up_bias[None, :])
     scatter = functools.partial(
         lax.psum_scatter, axis_name=owners, scatter_dimension=0, tiled=True
     )
-    grad_down, grad_upw, grad_up = tie(
-        (row_product(cot, up_act), row_product(mlp_in, grad_up), grad_up)
+    grad_attn, small_mlp, out_rows, grad_upw, grad_down = mlp_back(
+        grad_up, w_up, up_act, w_down, hidden, cot, mlp_in, ln_gain[3:4], down_bias[None, :]
     )
-    grad_attn, small_mlp = mlp_back(grad_up, w_up, hidden, cot, ln_gain[3:4])
     grad_vals = dot(grad_attn, w_out).astype(BF)
     dq, dkv = attend_back(scalars, q, kv_all, grad_vals, tables, heads)
-    w_qkv, up_act, dkv = tie((w_qkv, up_act, dkv))
+    w_qkv, out_rows, dkv = tie((w_qkv, out_rows, dkv))
     dkv_own = lax.psum_scatter(dkv, "seq", scatter_dimension=0).reshape(2, rows, width)
-    layer_out = mlp_out(up_act, w_down, hidden, down_bias[None, :])
+    layer_out = spread_rows(out_rows)
     layer_out, dkv_own, grad_down, grad_upw = tie((layer_out, dkv_own, grad_down, grad_upw))
     shard_down, shard_up = scatter(grad_down), scatter(grad_upw)
     grad_lin = jnp.stack([dq.reshape(rows, width), turn_back(dkv_own, tables), dkv_own[1]])
@@ -1173,10 +1544,8 @@
         layers, grads, grad_attn, mix, pre, mix_gain, w_mix, mix_w2
     )
     grad_history = grad_layers.reshape(depth, slots, block_len, feats)
-    seqs = lax.axis_size("seq")
-    count = lax.axis_size("dp") * seqs
     hidden_count = mix_w1.shape[1]
-    share = grad_w1.reshape(hidden_count, count, feats // count).transpose(1, 0, 2)
+    w1_share = grad_w1.reshape(hidden_count, count, feats // count).transpose(1, 0, 2)
 
     def as_row(values):
         flat = values.reshape(1, -1)
@@ -1194,7 +1563,7 @@
         + [jnp.zeros((5, feats), F32)],
         axis=0,
     )
-    summed, shard_w1 = small_sums(ours, share.reshape(count, -1, 128), seqs)
+    summed, shard_w1 = small_sums(ours, w1_share.reshape(count, -1, 128), seqs)
     return (
         layer_out.reshape(slots, block_len, feats),
         grad_history,

time: 1220 us -> 1030 us (0.84)
  waiting for transfers between devices: 103 us -> 2.37 us
  Pallas kernels: 989 us -> 945 us
  matrix products: 32.2 us -> 5.26 us
  blocking collectives: 20.9 us -> 0 us
    all_gather x7 -> x6, waiting for transfers between devices: 98.7 us -> 0.03 us  [the longest x1 0.02 us: shards(): gather(jnp.concatenate([qkv_weight[1], qkv_weight[2]], axis=1), tiled=True)]
    pallas_call x4 -> x5, Pallas kernels: 540 us -> 503 us  [the longest x1 190 us: mlp_back(): pl.pallas_call(mlp_back_kernel, in_specs=[VMEM, VMEM, VMEM, VMEM, VMEM, A...]
    dot_general x3 -> x1, matrix products: 32.2 us -> 5.26 us  [dot(): lax.dot_general(left, right, dims, precision=precision, preferred_element...]
    all_gather x1 -> x0, blocking collectives: 20.9 us -> none  [shards(): w_mix = lax.all_gather(mix_w1, owners, axis=0, tiled=True)]
    unnamed x90 -> x88, local copies, waits for them, and re-layouts: 31.4 us -> 29 us
  transfers between devices with their start and end apart: 11 -> 10, of which waited for: 4 -> 0; matrix products, arithmetic and copies ran while one was open for 4% -> 2% of each run, Pallas kernels for 73% -> 83%
where the time goes in v3:
time: 1030 us
  Pallas kernels  945 us (92%)
  local copies, waits for them, and re-layouts  39 us (4%)
  other arithmetic  18.7 us (2%)
  between operations  14.8 us (1%)
    pallas_call x1, Pallas kernels, streams_back(): pl.pallas_call(streams_back_kernel, in_specs=[VMEM, ANY, ANY, VMEM, VMEM]...  264 us
    pallas_call x1, Pallas kernels, mlp_back(): pl.pallas_call(mlp_back_kernel, in_specs=[VMEM, VMEM, VMEM, VMEM, VMEM, A...  190 us
    pallas_call x1, Pallas kernels, attn_out(): pl.pallas_call(attn_out_kernel, in_specs=[VMEM, ANY, ANY, VMEM, VMEM, VME...  98.8 us
    pallas_call x1, Pallas kernels, front(): pl.pallas_call(functools.partial(front_kernel, seqs, owners), grid=(rows...  77.4 us
    pallas_call x1, Pallas kernels, share(): pl.pallas_call(share_kernel, grid=(1,), in_specs=[pl.BlockSpec((1, rows,...  73.5 us
    pallas_call x1, Pallas kernels, spread_rows(): pl.pallas_call(layer_out_kernel, in_specs=[VMEM], out_specs=ANY, out_shap...  63.3 us
    pallas_call x1, Pallas kernels, last(): pl.pallas_call(last_kernel, grid=(rows // tile,), in_specs=[pl.BlockSpec(...  48 us
    pallas_call x1, Pallas kernels, mlp(): pl.pallas_call(mlp_kernel, grid=(width // cols, rows // tile), in_specs=[...  32 us
  transfers between devices with their start and end apart: 10, of which 0 were waited for; matrix products, arithmetic and copies ran while one was open for 2% of the time, Pallas kernels for 83%

profile of v3, /device:TPU:0, one launch (start us, length us, event | category | flops | bytes accessed | tf_op | source)
XLA Modules:
  0.0 1026.2 jit_solution(9908228739257753122)
XLA Ops:
  7.3 1.9 slice_bitcast_fusion.4
  11.1 77.4 %front.1 = (bf16[3,1024,2048]{2,1,0:T(8,128)(2,1)}, f32[1024,2048]{1,0:T(8,128)}, f32[1024,16]{1,0:T(8,128)S(1)}, f32[1024,16]{1,0:T(8,128)S(1)}, bf16[2048,16]{...) custom-call(bf16[4,1024,2048]{2,1,0:T(8,128)(2,1)} %bitcast.80, ...), custom_call_target="tpu_custom_call" | custom-call | bytes 210000000 | tf_op jit(solution)/shard_map/front/pallas_call | solution.py:168
  91.3 1.9 multiply_cosine_fusion
  94.0 2.2 copy-done.11
  96.1 10.0 project.1.kv
  106.2 1.3 copy-done.9
  108.3 1.6 copy-done.18
  109.9 73.5 %share.1 = (bf16[1024,512]{1,0:T(8,128)(2,1)S(1)}, bf16[2,2,1024,512]{3,2,1,0:T(8,128)(2,1)}) custom-call(bf16[3,1024,2048]{2,1,0:T(8,128)(2,1)} %get-tuple-element.62.lhs.normed, bf16[2048,512]{1,0:T(8,128)(2,1)S(1)} %bitcast.72, f32[1,512]{1,0:T(1,128)S(1)} %slice.68.bias, f32[3,1024,128]{2,1,0:T(8,128)S(1)} %pad_maximum_fusion.1.tables.t, ...), custom_call_target="tpu_custom_call" | custom-call | bytes 150000000 | tf_op jit(solution)/shard_map/share/pallas_call | solution.py:301
  183.4 2.6 copy-done
  186.0 15.6 %attend.1 = bf16[2,512,512]{2,1,0:T(8,128)(2,1)S(1)} custom-call(s32[3]{0:T(128)S(1)} %pad_add_fusion.scalars, bf16[2,512,512]{2,1,0:T(8,128)(2,1)S(1)} %bitcast.68, bf16[2,2,2,512,512]{4,3,2,1,0:T(8,128)(2,1)S(1)} %bitcast.61, bf16[2,2,2,512,512]{4,3,2,1,0:T(8,128)(2,1)S(1)} %bitcast.62), custom_call_target="tpu_custom_call" | custom-call | bytes 45000000 | tf_op jit(solution)/shard_map/attend/pallas_call | solution.py:344
  201.8 4.7 bitcast_select_fusion.cot
  206.5 98.8 %attn_out.1 = (f32[256,2048]{1,0:T(8,128)S(1)}, bf16[1024,2048]{1,0:T(8,128)(2,1)}) custom-call(bf16[1024,512]{1,0:T(8,128)(2,1)S(1)} %bitcast.64, bf16[8,4,256,512]{3,2,1,0:T(8,128)(2,1)} %bitcast.83, f32[1024,2048]{1,0:T(8,128)} %get-tuple-element.70.resid, f32[1,2048]{1,0:T(1,128)S(1)} %bitcast.78, f32[1,2048]{1,0:T(1,128)S(1)} %slice.72.lg, ...), custom_call_target="tpu_custom_call" | custom-call | bytes 285000000 | tf_op jit(solution)/shard_map/attn_out/pallas_call | solution.py:675
  305.3 1.3 copy-done.19
  306.6 3.1 constant_dynamic-slice_fusion
  309.7 32.0 %mlp.1 = (bf16[1024,2048]{1,0:T(8,128)(2,1)S(1)}, bf16[1024,2048]{1,0:T(8,128)(2,1)}, f32[1,2048]{1,0:T(1,128)S(1)}) custom-call(bf16[1024,2048]{1,0:T(8,128)(2,1)} %get-tuple-element.71.mlp_in, bf16[1024,2048]{1,0:T(8,128)(2,1)} %bitcast_select_fusion.cot, bf16[2048,2048]{1,0:T(8,128)(2,1)} %all-gather.13.cloned.1.call-done.up.rhs, ...), custom_call_target="tpu_custom_call" | custom-call | bytes 75000000 | tf_op jit(solution)/shard_map/mlp/pallas_call | solution.py:1303
  341.7 2.0 copy-done.14
  343.7 189.7 %mlp_back.1 = (bf16[1024,2048]{1,0:T(8,128)(2,1)}, f32[3,2048]{1,0:T(4,128)}, bf16[256,2048]{1,0:T(8,128)(2,1)}, bf16[2048,2048]{1,0:T(8,128)(2,1)}, bf16[2048,2048]{1,0:T(8,128)(2,1)}) custom-call(bf16[1024,2048]{1,0:T(8,128)(2,1)} %get-tuple-element.74.lhs, bf16[2048,2048]{1,0:T(8,128)(2,1)} %all-gather.13.cloned.1.call-done.up.rhs, ...), custom_call_target="tpu_custom_call" | custom-call | bytes 525000000 | tf_op jit(solution)/shard_map/mlp_back/pallas_call | solution.py:1032
  533.5 5.3 convolution_convert_fusion
  538.7 23.5 %attend_back.1 = (bf16[2,512,512]{2,1,0:T(8,128)(2,1)S(1)}, bf16[2,2,2,512,512]{4,3,2,1,0:T(8,128)(2,1)}) custom-call(s32[3]{0:T(128)S(1)} %pad_add_fusion.scalars, bf16[2,512,512]{2,1,0:T(8,128)(2,1)S(1)} %bitcast.69, bf16[2,2,2,512,512]{4,3,2,1,0:T(8,128)(2,1)} %bitcast.59, bf16[2,2,2,512,512]{4,3,2,1,0:T(8,128)(2,1)} %bitcast.60, ...), custom_call_target="tpu_custom_call" | custom-call | bytes 75000000 | tf_op jit(solution)/shard_map/attend_back/pallas_call | solution.py:394
  564.4 63.3 %spread_rows.1 = bf16[1024,2048]{1,0:T(8,128)(2,1)S(1)} custom-call(bf16[256,2048]{1,0:T(8,128)(2,1)S(1)} %copy-done.20), custom_call_target="tpu_custom_call" | custom-call | bytes 216000000 | tf_op jit(solution)/shard_map/spread_rows/pallas_call | solution.py:713
  627.7 2.0 copy-done.3
  629.7 1.6 copy-done.10
  632.9 1.8 copy-done.5
  635.0 18.9 %weight_grads.1 = bf16[2048,2048]{1,0:T(8,128)(2,1)} custom-call(bf16[3,1024,2048]{2,1,0:T(8,128)(2,1)} %get-tuple-element.62.lhs.normed, bf16[1024,2048]{1,0:T(8,128)(2,1)S(1)} %copy-done.5, bf16[3,1024,512]{2,1,0:T(8,128)(2,1)S(1)} %pad_maximum_fusion.grad_lin.lin, bf16[1024,512]{1,0:T(8,128)(2,1)S(1)} %bitcast.65), custom_call_target="tpu_custom_call" | custom-call | bytes 45000000 | tf_op jit(solution)/shard_map/weight_grads/pallas_call | solution.py:742
  655.3 3.1 convert_reduce_fusion
  658.4 263.8 %streams_back.1 = (bf16[3,1024,2048]{2,1,0:T(8,128)(2,1)}, f32[2,3,2048]{2,1,0:T(4,128)}) custom-call(bf16[3,1024,512]{2,1,0:T(8,128)(2,1)} %copy-done.1, bf16[8,4,3,256,512]{4,3,2,1,0:T(8,128)(2,1)} %all-gather.11.cloned.1.call-done.weight, bf16[4,1024,2048]{2,1,0:T(8,128)(2,1)} %bitcast.81, f32[1024,16]{1,0:T(8,128)} %copy-done.16, f32[4,2048]{1,0:T(4,128)} %lg.3), custom_call_target="tpu_custom_call" | custom-call | bytes 720000000 | tf_op jit(solution)/shard_map/streams_back/pallas_call | solution.py:1194
  923.7 2.2 copy-done.6
  929.0 48.0 %last.1 = (f32[4,1024,2048]{2,1,0:T(8,128)}, f32[1,2048]{1,0:T(1,128)S(1)}, f32[16,2048]{1,0:T(8,128)S(1)}, f32[16,16]{1,0:T(8,128)S(1)}) custom-call(bf16[4,1024,2048]{2,1,0:T(8,128)(2,1)} %bitcast.82, bf16[3,1024,2048]{2,1,0:T(8,128)(2,1)} %get-tuple-element.94.streams, bf16[1024,2048]{1,0:T(8,128)(2,1)S(1)} %copy-done.6, f32[1024,16]{1,0:T(8,128)S(1)} %copy-done.17, ...), custom_call_target="tpu_custom_call" | custom-call | bytes 90000000 | tf_op jit(solution)/shard_map/last/pallas_call | solution.py:1402
  977.3 29.9 %small_sums.1 = (f32[24,2048]{1,0:T(8,128)S(1)}, f32[32,128]{1,0:T(8,128)S(1)}) custom-call(f32[24,2048]{1,0:T(8,128)S(1)} %concatenate.29.ours, f32[8,32,128]{2,1,0:T(8,128)S(1)} %reshape.147.share), custom_call_target="tpu_custom_call" | custom-call | bytes 36000000 | tf_op jit(solution)/shard_map/small_sums/pallas_call | solution.py:1263
  1011.0 2.8 convert_element_type.47
  1013.8 1.6 convert_element_type.48
  1017.3 2.0 copy.47
  (151 shorter events, 22.1 us)
Async XLA Ops:
  7.2 3.9 copy-start.15
  7.2 3.7 copy-start.38
  7.2 3.9 copy-start.31
  7.2 3.9 copy-start.32
  7.2 3.9 copy-start.28
  7.2 3.9 copy-start.30
  7.2 3.9 copy-start.27
  7.3 86.7 %all-gather.9.cloned.1.call-start = ((), (), s32[]{:S(2)}) async-start(), calls=%async_computation.4 | async-start | bytes 4718592 | tf_op jit(solution)/shard_map/all_gather | solution.py:1490
  10.1 98.1 %all-gather.17.cloned.1.call-start = ((), (), s32[]{:S(2)}) async-start(), calls=%async_computation.12 | async-start | bytes 2359296 | tf_op jit(solution)/shard_map/all_gather | solution.py:1491
  10.9 195.6 %all-gather.19.cloned.1.call-start = ((), (), s32[]{:S(2)}) async-start(), calls=%async_computation.13 | async-start | bytes 9437184 | tf_op jit(solution)/shard_map/all_gather | solution.py:1504
  11.1 80.0 %copy-start.40 = (s32[2,512]{1,0:T(2,128)S(1)}, s32[2,512]{1,0:T(2,128)}, u32[]{:S(2)}) copy-start(s32[2,512]{1,0:T(2,128)} %param.18) | copy-start | bytes 12292
  11.1 80.2 %copy-start.39 = (f32[3,512]{1,0:T(4,128)S(1)}, f32[3,512]{1,0:T(4,128)}, u32[]{:S(2)}) copy-start(f32[3,512]{1,0:T(4,128)} %param.27) | copy-start | bytes 18436
  91.0 218.6 %all-gather.13.cloned.1.call-start = ((), (), s32[]{:S(2)}) async-start(), calls=%async_computation.6 | async-start | bytes 9437184 | tf_op jit(solution)/shard_map/all_gather | solution.py:1507
  96.1 12.0 %copy-start.41 = (s32[2]{0:T(128)S(1)}, s32[2]{0:T(128)}, u32[]{:S(2)}) copy-start(s32[2]{0:T(128)} %param.19) | copy-start | bytes 28
  107.5 202.2 %all-gather.15.cloned.1.call-start = ((), (), s32[]{:S(2)}) async-start(), calls=%async_computation.7 | async-start | bytes 9437184 | tf_op jit(solution)/shard_map/all_gather | solution.py:1507
  108.1 455.1 %all-gather.11.cloned.1.call-start = ((), (), s32[]{:S(2)}) async-start(), calls=%async_computation.5 | async-start | bytes 28311552 | tf_op jit(solution)/shard_map/all_gather | solution.py:1512
  183.4 18.2 %copy-start.12 = (bf16[1024,512]{1,0:T(8,128)(2,1)}, bf16[1024,512]{1,0:T(8,128)(2,1)S(1)}, u32[]{:S(2)}) copy-start(bf16[1024,512]{1,0:T(8,128)(2,1)S(1)} %get-tuple-element.64) | copy-start | bytes 3145732
  201.5 5.0 copy-start.7
  201.6 428.2 %reduce-scatter.5.cloned.1.call-start = ((), (), s32[]{:S(2)}) async-start(), calls=%async_computation.8 | async-start | bytes 6291456 | tf_op jit(solution)/shard_map/reduce_scatter | solution.py:1529
  201.6 4.9 copy-start.29
  201.8 4.7 copy-start.33
  306.6 3.1 copy-start.34
  533.5 5.3 copy-start.13
  563.2 360.4 %reduce-scatter.11.cloned.1.call-start = ((), (), s32[]{:S(2)}) async-start(), calls=%async_computation.11 | async-start | bytes 9437184 | tf_op jit(solution)/shard_map/reduce_scatter | solution.py:1535
  635.0 18.9 %copy-start.1 = (bf16[3,1024,512]{2,1,0:T(8,128)(2,1)}, bf16[3,1024,512]{2,1,0:T(8,128)(2,1)S(1)}, u32[]{:S(2)}) copy-start(bf16[3,1024,512]{2,1,0:T(8,128)(2,1)S(1)} %pad_maximum_fusion.grad_lin.lin) | copy-start | bytes 9437188
  654.0 269.7 %reduce-scatter.7.cloned.1.call-start = ((), (), s32[]{:S(2)}) async-start(), calls=%async_computation.9 | async-start | bytes 9437184 | tf_op jit(solution)/shard_map/reduce_scatter | solution.py:1532
  654.7 269.0 %reduce-scatter.9.cloned.1.call-start = ((), (), s32[]{:S(2)}) async-start(), calls=%async_computation.10 | async-start | bytes 9437184 | tf_op jit(solution)/shard_map/reduce_scatter | solution.py:1532
  658.4 264.7 %copy-start.2 = (bf16[3,1024,512]{2,1,0:T(8,128)(2,1)S(1)}, bf16[3,1024,512]{2,1,0:T(8,128)(2,1)}, u32[]{:S(2)}) copy-start(bf16[3,1024,512]{2,1,0:T(8,128)(2,1)} %copy-done.1) | copy-start | bytes 9437188
  929.0 48.1 %copy-start.37 = (f32[3,2048]{1,0:T(4,128)S(1)}, f32[3,2048]{1,0:T(4,128)}, u32[]{:S(2)}) copy-start(f32[3,2048]{1,0:T(4,128)} %get-tuple-element.98) | copy-start | bytes 73732
  929.0 78.8 %copy-start.35 = (bf16[256,2048]{1,0:T(8,128)(2,1)S(1)}, bf16[256,2048]{1,0:T(8,128)(2,1)}, u32[]{:S(2)}) copy-start(bf16[256,2048]{1,0:T(8,128)(2,1)} %reduce-scatter.11.cloned.1.call-done) | copy-start | bytes 3145732
  1009.0 4.8 copy-start.36
  1013.8 3.5 copy-start.4
  (20 other events, 30.5 us)
Sparse Core Ops, SparseCore 0:
  10.5 40.5 all-gather.8
  53.6 27.8 all-gather.16
  91.1 77.2 all-gather.18
  170.2 55.8 all-gather.12
  227.8 54.4 all-gather.14
  284.0 125.3 all-gather.10
  563.3 54.1 reduce-scatter.4
  654.1 72.9 reduce-scatter.10
  730.5 71.3 reduce-scatter.6
  805.7 71.3 reduce-scatter.8

commit v4 on v3

--- a/solution.py
+++ b/solution.py
@@ -87,42 +87,23 @@
 
 def front_kernel(
     seqs, owners,
-    hist, gain, w1, w2, lg, lb, shard_out, shard_qkv,
-    normed_out, resid_out, mix_out, pre_out, w1_out, ring_out, ring_qkv,
-    scratch, w1_all, w1_sems, ring_sems, own_sems,
+    hist, gain, w1, w2, lg, lb, normed_out, resid_out, mix_out, pre_out, w1_out,
+    scratch, w1_all, w1_sems,
 ):
     depth, rows, _ = hist.shape
     index = pl.program_id(0)
-    ring = Ring(16)
     rank, _, places = owner_places(seqs, owners)
     w1_copies = [push(w1, w1_all.at[rank], w1_sems, k, p) for k, p in enumerate(places)]
-    spreads = [
-        Spread(ring, slots, ring_sems.at[i], 0, source)
-        for i, (slots, source) in enumerate(((ring_out, shard_out), (ring_qkv, shard_qkv)))
-    ]
-    local = [
-        pltpu.make_async_copy(shard_out, ring_out.at[ring.me], own_sems.at[0]),
-        pltpu.make_async_copy(shard_qkv, ring_qkv.at[ring.me], own_sems.at[1]),
-    ]
 
     @pl.when(index == 0)
     def _():
-        enter(places + [{"tensor": ring.left}, {"tensor": ring.right}])
+        enter(places)
         for copy in w1_copies:
             copy.start()
-        for copy in local:
-            copy.start()
-        for spread in spreads:
-            spread.begin()
         w1_all[rank] = w1[...]
         for copy in w1_copies:
             copy.wait()
         w1_out[...] = w1_all[...].reshape(w1_out.shape)
-
-    @pl.when(index == pl.num_programs(0) - 1)
-    def _():
-        for spread in spreads:
-            spread.relay()
 
     def rms(part):
         wide = hist[depth - 1, part, :].astype(F32)
@@ -151,16 +132,8 @@
 
     rows_loop(rows, 16, combine)
 
-    @pl.when(index == pl.num_programs(0) - 1)
-    def _():
-        for spread in spreads:
-            spread.arrive()
-            spread.finish()
-        for copy in local:
-            copy.wait()
-
-
-def front(layers, gain, w1, w2, lg, lb, shard_out, shard_qkv, seqs, owners):
+
+def front(layers, gain, w1, w2, lg, lb, seqs, owners):
     depth, rows, feats = layers.shape
     tile = min(128, rows)
     hidden = w1.shape[1]
@@ -175,8 +148,6 @@
             full(w2.shape),
             full(lg.shape),
             full(lb.shape),
-            ANY,
-            ANY,
         ],
         out_specs=[
             pl.BlockSpec((3, tile, feats), lambda i: (0, i, 0)),
@@ -184,8 +155,6 @@
             pl.BlockSpec((tile, STREAMS * depth), lambda i: (i, 0)),
             pl.BlockSpec((tile, hidden), lambda i: (i, 0)),
             full((feats, hidden)),
-            ANY,
-            ANY,
         ],
         out_shape=[
             jax.ShapeDtypeStruct((3, rows, feats), BF),
@@ -193,20 +162,16 @@
             jax.ShapeDtypeStruct((rows, STREAMS * depth), F32),
             jax.ShapeDtypeStruct((rows, hidden), F32),
             jax.ShapeDtypeStruct((feats, hidden), BF),
-            jax.ShapeDtypeStruct((RING,) + shard_out.shape, BF),
-            jax.ShapeDtypeStruct((RING,) + shard_qkv.shape, BF),
         ],
         scratch_shapes=[
             pltpu.VMEM((tile, feats), BF),
             pltpu.VMEM((owners,) + w1.shape, BF),
             pltpu.SemaphoreType.DMA((2, owners - 1)),
-            pltpu.SemaphoreType.DMA((2, 2, 4)),
-            pltpu.SemaphoreType.DMA((2,)),
         ],
         compiler_params=params(48, 5),
-        cost_estimate=cost(70),
+        cost_estimate=cost(45),
         name="front",
-    )(layers, gain.reshape(1, feats), w1, w2, lg, lb, shard_out, shard_qkv)
+    )(layers, gain.reshape(1, feats), w1, w2, lg, lb)
 
 
 def turn(values, tables, sign):
@@ -271,56 +236,61 @@
     )(normed, weight, bias.reshape(count, 1, width), tables)
 
 
-def share_kernel(lhs, weight, bias, tables, kv, q_out, kv_out, sems, own_sem):
+def share_kernel(
+    kv, shard_out, shard_qkv, kv_out, ring_out, ring_qkv, sems, ring_sems, own_sems
+):
     seqs = kv_out.shape[0]
     me = lax.axis_index("seq")
+    ring = Ring(16)
     places = [{"seq": lax.rem(me + k, seqs)} for k in range(1, seqs)]
-    local = pltpu.make_async_copy(kv, kv_out.at[me], own_sem)
-    local.start()
-    enter(places)
+    local = [
+        pltpu.make_async_copy(kv, kv_out.at[me], own_sems.at[0]),
+        pltpu.make_async_copy(shard_out, ring_out.at[ring.me], own_sems.at[1]),
+        pltpu.make_async_copy(shard_qkv, ring_qkv.at[ring.me], own_sems.at[2]),
+    ]
+    for copy in local:
+        copy.start()
+    enter(places + [{"tensor": ring.left}, {"tensor": ring.right}])
     copies = [push(kv, kv_out.at[me], sems, k, place) for k, place in enumerate(places)]
+    spreads = [
+        Spread(ring, slots, ring_sems.at[i], 0, source)
+        for i, (slots, source) in enumerate(((ring_out, shard_out), (ring_qkv, shard_qkv)))
+    ]
     for copy in copies:
         copy.start()
-
-    def rows(part):
-        value = dot(lhs[0, part, :], weight[...]) + bias[...]
-        tabs = (tables[0, part, :], tables[1, part, :], tables[2, part, :])
-        for head in range(value.shape[1] // HEAD_DIM):
-            cols = slice(head * HEAD_DIM, (head + 1) * HEAD_DIM)
-            q_out[part, cols] = turn(value[:, cols], tabs, 1.0).astype(BF)
-
-    rows_loop(lhs.shape[1], 256, rows)
+    for spread in spreads:
+        spread.begin()
+
+    for spread in spreads:
+        spread.relay()
     for copy in copies:
         copy.wait()
-    local.wait()
-
-
-def share(normed, weight, bias, tables, kv, seqs):
-    _, rows, feats = normed.shape
-    width = weight.shape[1]
+    for spread in spreads:
+        spread.arrive()
+        spread.finish()
+    for copy in local:
+        copy.wait()
+
+
+def share(kv, shard_out, shard_qkv, seqs):
     return pl.pallas_call(
         share_kernel,
-        grid=(1,),
-        in_specs=[
-            pl.BlockSpec((1, rows, feats), lambda i: (0, 0, 0)),
-            pl.BlockSpec(weight.shape, lambda i: (0, 0)),
-            pl.BlockSpec(bias.shape, lambda i: (0, 0)),
-            pl.BlockSpec(tables.shape, lambda i: (0, 0, 0)),
-            ANY,
-        ],
-        out_specs=[pl.BlockSpec((rows, width), lambda i: (0, 0)), ANY],
+        in_specs=[ANY, ANY, ANY],
+        out_specs=[ANY, ANY, ANY],
         out_shape=[
-            jax.ShapeDtypeStruct((rows, width), BF),
             jax.ShapeDtypeStruct((seqs,) + kv.shape, BF),
+            jax.ShapeDtypeStruct((RING,) + shard_out.shape, BF),
+            jax.ShapeDtypeStruct((RING,) + shard_qkv.shape, BF),
         ],
         scratch_shapes=[
             pltpu.SemaphoreType.DMA((2, seqs - 1)),
-            pltpu.SemaphoreType.DMA,
+            pltpu.SemaphoreType.DMA((2, 2, 4)),
+            pltpu.SemaphoreType.DMA((3,)),
         ],
         compiler_params=params(48, 6),
-        cost_estimate=cost(50),
+        cost_estimate=cost(72),
         name="share",
-    )(normed, weight, bias, tables, kv)
+    )(kv, shard_out, shard_qkv)
 
 
 def attend_kernel(scalars, q, k, v, out):
@@ -612,23 +582,41 @@
     rows_loop(total.shape[1], 512, columns)
 
 
+def spread_kernel(vals, out, sems, own_sem):
+    ring = Ring(16)
+    local = pltpu.make_async_copy(vals, out.at[ring.me], own_sem)
+    local.start()
+    ring.barrier()
+    spread = Spread(ring, out, sems, 0, vals)
+    spread.begin()
+    spread.relay()
+    spread.arrive()
+    spread.finish()
+    local.wait()
+
+
+def spread_vals(vals):
+    return pl.pallas_call(
+        spread_kernel,
+        in_specs=[ANY],
+        out_specs=ANY,
+        out_shape=jax.ShapeDtypeStruct((RING,) + vals.shape, BF),
+        scratch_shapes=[pltpu.SemaphoreType.DMA((2, 4)), pltpu.SemaphoreType.DMA],
+        compiler_params=params(32, 0),
+        cost_estimate=cost(70),
+        name="spread_vals",
+    )(vals)
+
+
 def attn_out_kernel(
-    vals, weight, resid, bias, lg, lb, hidden_out, mlp_out,
-    slots, weights, total, base_rows, stage, sems, weight_sems, base_sem, stage_sems, own_sem,
+    slots, weight, resid, bias, lg, lb, hidden_out, mlp_out,
+    weights, total, base_rows, stage, weight_sems, base_sem, stage_sems,
 ):
     chunk, feats = total.shape
-    ring = Ring(chunk)
+    me = lax.axis_index("tensor")
     load = weight_copies(weight, weights, weight_sems, None)
     load(lambda copy: copy.start())
-    local = pltpu.make_async_copy(vals, slots.at[ring.me], own_sem)
-    local.start()
-    ring.barrier()
-    spread = Spread(ring, slots, sems, 0, vals)
-    spread.begin()
-    spread.relay()
     load(lambda copy: copy.wait())
-    local.wait()
-    spread.arrive()
 
     def write_out(index, slot):
         part = pl.ds(pl.multiple_of(index * chunk, chunk), chunk)
@@ -656,7 +644,7 @@
         rows_loop(chunk, 16, norm)
         write_out(index, slot).start()
 
-        @pl.when(index == ring.me)
+        @pl.when(index == me)
         def _():
             hidden_out[...] = total[...]
 
@@ -665,12 +653,11 @@
     lax.fori_loop(0, RING, one, 0)
     for index in range(RING - 2, RING):
         write_out(index, index % 2).wait()
-    spread.finish()
-
-
-def attn_out(vals, weight, resid, bias, lg, lb):
+
+
+def attn_out(slots, weight, resid, bias, lg, lb):
     rows, feats = resid.shape
-    width = vals.shape[1]
+    width = slots.shape[2]
     chunk = rows // RING
     return pl.pallas_call(
         attn_out_kernel,
@@ -681,82 +668,18 @@
             jax.ShapeDtypeStruct((rows, feats), BF),
         ],
         scratch_shapes=[
-            pltpu.VMEM((RING, rows, width), BF),
             pltpu.VMEM((RING, feats, width), BF),
             pltpu.VMEM((chunk, feats), F32),
             pltpu.VMEM((chunk, feats), F32),
             pltpu.VMEM((2, chunk, feats), BF),
-            pltpu.SemaphoreType.DMA((2, 4)),
             pltpu.SemaphoreType.DMA((weight.shape[0],)),
             pltpu.SemaphoreType.DMA,
             pltpu.SemaphoreType.DMA((2,)),
-            pltpu.SemaphoreType.DMA,
-        ],
-        compiler_params=params(48, 0),
-        cost_estimate=cost(95),
+        ],
+        compiler_params=params(48),
+        cost_estimate=cost(30),
         name="attn_out",
-    )(vals, weight, resid, bias, lg, lb)
-
-
-def layer_out_kernel(own, out, sems, own_sem):
-    chunk = own.shape[0]
-    ring = Ring(chunk)
-    ring.barrier()
-    gather = Gather(ring, own, out, sems, 0, own_sem)
-    gather.begin()
-    gather.relay()
-    gather.finish()
-
-
-def spread_rows(own):
-    chunk, feats = own.shape
-    return pl.pallas_call(
-        layer_out_kernel,
-        in_specs=[VMEM],
-        out_specs=ANY,
-        out_shape=jax.ShapeDtypeStruct((RING * chunk, feats), BF),
-        scratch_shapes=[pltpu.SemaphoreType.DMA((2, 4)), pltpu.SemaphoreType.DMA],
-        compiler_params=params(32, 3),
-        cost_estimate=cost(72),
-        name="spread_rows",
-    )(own)
-
-
-def weights_kernel(normed, grad_attn, grad_lin, attn_vals, out):
-    branch = pl.program_id(0)
-
-    @pl.when(branch < 3)
-    def _():
-        out[...] = dot(normed[0], grad_lin[0], TN).astype(BF)
-
-    @pl.when(branch == 3)
-    def _():
-        out[...] = dot(grad_attn[...], attn_vals[...], TN).astype(BF)
-
-
-def weight_grads(normed, grad_attn, grad_lin, attn_vals):
-    _, rows, feats = normed.shape
-    width = attn_vals.shape[1]
-    cols = 512
-    last_block = feats // cols - 1
-    return pl.pallas_call(
-        weights_kernel,
-        grid=(4, feats // cols),
-        in_specs=[
-            pl.BlockSpec(
-                (1, rows, cols),
-                lambda b, n: (jnp.minimum(b, 2), 0, jnp.where(b < 3, n, last_block)),
-            ),
-            pl.BlockSpec((rows, cols), lambda b, n: (0, jnp.where(b < 3, 0, n))),
-            pl.BlockSpec((1, rows, width), lambda b, n: (jnp.minimum(b, 2), 0, 0)),
-            pl.BlockSpec((rows, width), lambda b, n: (0, 0)),
-        ],
-        out_specs=pl.BlockSpec((cols, width), lambda b, n: (n, b)),
-        out_shape=jax.ShapeDtypeStruct((feats, 4 * width), BF),
-        compiler_params=params(40),
-        cost_estimate=cost(15),
-        name="weight_grads",
-    )(normed, grad_attn, grad_lin, attn_vals)
+    )(slots, weight, resid, bias, lg, lb)
 
 
 def norm_back(values, grads, gain):
@@ -810,6 +733,51 @@
     lax.fori_loop(0, count, one, 0)
     for n in range(count - 2, count):
         store(n, n % 2).wait()
+
+
+def spread_dq_kernel(
+    lin, normed, grad_attn, vals, out, products,
+    blocks, tiles_out, sems, own_sem, load_sems, store_sems,
+):
+    ring = Ring(16)
+    width = lin.shape[1]
+    local = pltpu.make_async_copy(lin, out.at[ring.me], own_sem)
+    local.start()
+    ring.barrier()
+    spread = Spread(ring, out, sems, 0, lin)
+    spread.begin()
+    for i, (source, rhs) in enumerate(((normed.at[0], lin), (grad_attn, vals))):
+        target = products.at[:, pl.ds(i * width, width)]
+        weight_product(source, rhs, target, blocks, tiles_out, load_sems, store_sems)
+    spread.relay()
+    spread.arrive()
+    spread.finish()
+    local.wait()
+
+
+def spread_dq(lin, normed, grad_attn, vals):
+    rows, width = lin.shape
+    feats = grad_attn.shape[1]
+    return pl.pallas_call(
+        spread_dq_kernel,
+        in_specs=[VMEM, ANY, ANY, VMEM],
+        out_specs=[ANY, ANY],
+        out_shape=[
+            jax.ShapeDtypeStruct((RING, rows, width), BF),
+            jax.ShapeDtypeStruct((feats, 2 * width), BF),
+        ],
+        scratch_shapes=[
+            pltpu.VMEM((2, rows, 256), BF),
+            pltpu.VMEM((2, 256, width), BF),
+            pltpu.SemaphoreType.DMA((2, 4)),
+            pltpu.SemaphoreType.DMA,
+            pltpu.SemaphoreType.DMA((2,)),
+            pltpu.SemaphoreType.DMA((2,)),
+        ],
+        compiler_params=params(40, 3),
+        cost_estimate=cost(70),
+        name="spread_dq",
+    )(lin, normed, grad_attn, vals)
 
 
 class Line:
@@ -1095,8 +1063,10 @@
 
 
 def streams_back_kernel(
-    lin, weight, hist, mix, lg, grads_out, small_out,
-    slots, weights, total, layers, stage, sums, sems, weight_sems, layer_sem, stage_sems, own_sems,
+    first, lin, weight, hist, mix, lg, normed_in, own_rows,
+    grads_out, small_out, products, rows_out,
+    slots, weights, total, layers, stage, sums, blocks, tiles_out,
+    sems, weight_sems, layer_sem, stage_sems, own_sems, load_sems, store_sems,
 ):
     tile, feats = total.shape
     depth = layers.shape[0]
@@ -1110,15 +1080,20 @@
         )
 
     local = [
-        pltpu.make_async_copy(lin.at[i], slots.at[i, ring.me], own_sems.at[i]) for i in range(3)
+        pltpu.make_async_copy(lin.at[i], slots.at[i, ring.me], own_sems.at[i])
+        for i in range(2)
     ]
+    local.append(
+        pltpu.make_async_copy(own_rows, rows_out.at[ring.me], own_sems.at[2])
+    )
     for copy in local:
         copy.start()
     for stream in range(2):
         fetch(stream)(lambda copy: copy.start())
     sums[...] = jnp.zeros_like(sums)
     ring.barrier()
-    spreads = [Spread(ring, slots.at[i], sems.at[i], 0, lin.at[i]) for i in range(3)]
+    spreads = [Spread(ring, slots.at[i], sems.at[i], 0, lin.at[i]) for i in range(2)]
+    spreads.append(Spread(ring, rows_out, sems.at[2], 0, own_rows))
 
     def write_out(stream, index, slot):
         part = pl.ds(pl.multiple_of(index * tile, tile), tile)
@@ -1135,7 +1110,8 @@
             load.start()
             slot = lax.rem(index, 2)
 
-            ring_product(slots.at[stream], weights.at[stream % 2], part, total)
+            gathered = first if stream == 0 else slots.at[stream - 1]
+            ring_product(gathered, weights.at[stream % 2], part, total)
             load.wait()
 
             @pl.when(index >= 2)
@@ -1169,17 +1145,20 @@
     for copy in local:
         copy.wait()
     spreads[0].begin()
+    compute(0)
+    spreads[0].relay()
+    for i in range(2):
+        source, target = normed_in.at[i + 1], products.at[:, pl.ds(i * width, width)]
+        weight_product(source, lin.at[i], target, blocks, tiles_out, load_sems, store_sems)
+    spreads[0].arrive()
     spreads[1].begin()
-    spreads[0].relay()
+    compute(1)
+    spreads[1].relay()
+    spreads[1].arrive()
     spreads[2].begin()
-    spreads[1].relay()
-    spreads[0].arrive()
-    compute(0)
+    compute(2)
     spreads[2].relay()
-    spreads[1].arrive()
-    compute(1)
     spreads[2].arrive()
-    compute(2)
     for i in range(3):
         for j in range(2):
             small_out[j, i : i + 1, :] = jnp.sum(sums[i, j], axis=0, keepdims=True)
@@ -1187,35 +1166,41 @@
         spread.finish()
 
 
-def streams_back(lin, weight, hist, mix, lg):
+def streams_back(first, lin, weight, hist, mix, lg, normed, own_rows):
     depth, rows, feats = hist.shape
     width = lin.shape[2]
     tile = min(256, rows)
     return pl.pallas_call(
         streams_back_kernel,
-        in_specs=[VMEM, ANY, ANY, VMEM, VMEM],
-        out_specs=[ANY, VMEM],
+        in_specs=[VMEM, VMEM, ANY, ANY, VMEM, VMEM, ANY, ANY],
+        out_specs=[ANY, VMEM, ANY, ANY],
         out_shape=[
             jax.ShapeDtypeStruct((3, rows, feats), BF),
             jax.ShapeDtypeStruct((2, 3, feats), F32),
+            jax.ShapeDtypeStruct((feats, 2 * width), BF),
+            jax.ShapeDtypeStruct((RING,) + own_rows.shape, BF),
         ],
         scratch_shapes=[
-            pltpu.VMEM((3, RING, rows, width), BF),
+            pltpu.VMEM((2, RING, rows, width), BF),
             pltpu.VMEM((2, RING, feats, width), BF),
             pltpu.VMEM((tile, feats), F32),
             pltpu.VMEM((depth, tile, feats), BF),
             pltpu.VMEM((2, tile, feats), BF),
             pltpu.VMEM((3, 2, 8, feats), F32),
+            pltpu.VMEM((2, rows, 256), BF),
+            pltpu.VMEM((2, 256, width), BF),
             pltpu.SemaphoreType.DMA((3, 2, 4)),
             pltpu.SemaphoreType.DMA((2, weight.shape[0])),
             pltpu.SemaphoreType.DMA,
             pltpu.SemaphoreType.DMA((2,)),
             pltpu.SemaphoreType.DMA((3,)),
-        ],
-        compiler_params=params(58, 2),
+            pltpu.SemaphoreType.DMA((2,)),
+            pltpu.SemaphoreType.DMA((2,)),
+        ],
+        compiler_params=params(60, 2),
         cost_estimate=cost(240),
         name="streams_back",
-    )(lin, weight, hist, mix, lg)
+    )(first, lin, weight, hist, mix, lg, normed, own_rows)
 
 
 def small_kernel(seqs, owners, ours, share, out, share_out, near, all_ours, all_shares, near_sems, sems):
@@ -1497,21 +1482,25 @@
     scalars = jnp.concatenate([lengths, offset[None].astype(jnp.int32)])
     tables = rotary_tables(positions.reshape(rows))
 
-    normed, resid, mix, pre, w_mix, ring_out, ring_qkv = front(
-        layers, mix_gain, mix_w1, mix_w2, ln_gain, ln_bias, out_weight,
-        qkv_weight.reshape(-1, width), seqs, count
-    )
+    normed, resid, mix, pre, w_mix = front(
+        layers, mix_gain, mix_w1, mix_w2, ln_gain, ln_bias, seqs, count
+    )
+    w_up = gather(up_weight, tiled=True)
+    kv = project(normed, w_kv, qkv_bias[1:], tables, 1)
+    kv_all, ring_out, ring_qkv = share(kv, out_weight, qkv_weight.reshape(-1, width), seqs)
+    kv_all, w_up = tie((kv_all, w_up))
+    kv_all, w_q = tie((kv_all, w_q))
+    q = project(normed, w_q, qkv_bias[:1], tables, 0)[0]
     w_out_all = gather(ring_out)
-    kv = project(normed, w_kv, qkv_bias[1:], tables, 1)
-    kv, up_weight, down_weight = tie((kv, up_weight, down_weight))
-    w_up, w_down = gather(up_weight, tiled=True), gather(down_weight, tiled=True)
-    q, kv_all = share(normed, w_q, qkv_bias[:1], tables, kv, seqs)
     kv_all = kv_all.reshape(seqs, 2, slots, block_len, width)
     attn_vals = attend(scalars, q, kv_all, heads).reshape(rows, width)
-    attn_vals, ring_qkv = tie((attn_vals, ring_qkv))
+    attn_vals, down_weight = tie((attn_vals, down_weight))
+    w_down = gather(down_weight, tiled=True)
+    vals_all = spread_vals(attn_vals)
+    vals_all, ring_qkv = tie((vals_all, ring_qkv))
     w_qkv = gather(ring_qkv.reshape((RING,) + qkv_weight.shape))
     hidden, mlp_in = attn_out(
-        attn_vals, w_out_all, resid, out_bias[None, :], ln_gain[3:4], ln_bias[3:4]
+        vals_all, w_out_all, resid, out_bias[None, :], ln_gain[3:4], ln_bias[3:4]
     )
     w_out = lax.dynamic_index_in_dim(
         w_out_all, lax.axis_index("tensor"), 1, keepdims=False
@@ -1525,21 +1514,25 @@
     )
     grad_vals = dot(grad_attn, w_out).astype(BF)
     dq, dkv = attend_back(scalars, q, kv_all, grad_vals, tables, heads)
-    w_qkv, out_rows, dkv = tie((w_qkv, out_rows, dkv))
+    w_qkv, dq, dkv = tie((w_qkv, dq, dkv))
     dkv_own = lax.psum_scatter(dkv, "seq", scatter_dimension=0).reshape(2, rows, width)
-    layer_out = spread_rows(out_rows)
-    layer_out, dkv_own, grad_down, grad_upw = tie((layer_out, dkv_own, grad_down, grad_upw))
-    shard_down, shard_up = scatter(grad_down), scatter(grad_upw)
-    grad_lin = jnp.stack([dq.reshape(rows, width), turn_back(dkv_own, tables), dkv_own[1]])
-    grad_owqkv, grad_lin = tie((weight_grads(normed, grad_attn, grad_lin, attn_vals), grad_lin))
-    shard_all = scatter(grad_owqkv)
-    grads, small_qkv = streams_back(grad_lin, w_qkv, layers, mix, ln_gain)
-    shard_down, shard_up, shard_all, grads = tie((shard_down, shard_up, shard_all, grads))
-    shard_down, shard_up, shard_all = (
-        shard_down.astype(F32), shard_up.astype(F32), shard_all.astype(F32)
-    )
-    shard_qkv = jnp.stack([shard_all[:, i * width : (i + 1) * width] for i in range(3)])
-    shard_out = shard_all[:, 3 * width :]
+    dq = dq.reshape(rows, width)
+    dq_all, grad_qo = spread_dq(dq, normed, grad_attn, attn_vals)
+    dq_all, dkv_own, grad_down, grad_upw, grad_qo = tie(
+        (dq_all, dkv_own, grad_down, grad_upw, grad_qo)
+    )
+    shard_down, shard_up, shard_qo = scatter(grad_down), scatter(grad_upw), scatter(grad_qo)
+    lin_kv = jnp.stack([turn_back(dkv_own, tables), dkv_own[1]])
+    grads, small_qkv, grad_kv, layer_out = streams_back(
+        dq_all, lin_kv, w_qkv, layers, mix, ln_gain, normed, out_rows
+    )
+    shard_down, shard_up, shard_qo, grads, grad_kv = tie(
+        (shard_down, shard_up, shard_qo, grads, grad_kv)
+    )
+    shard_kv = scatter(grad_kv)
+    shard_down, shard_up = shard_down.astype(F32), shard_up.astype(F32)
+    shard_qkv = jnp.stack([shard_qo[:, :width], shard_kv[:, :width], shard_kv[:, width:]])
+    shard_qkv, shard_out = shard_qkv.astype(F32), shard_qo[:, width:].astype(F32)
     grad_layers, grad_gain, grad_w1, grad_w2 = last(
         layers, grads, grad_attn, mix, pre, mix_gain, w_mix, mix_w2
     )
@@ -1551,7 +1544,9 @@
         flat = values.reshape(1, -1)
         return jnp.pad(flat, ((0, 0), (0, feats - flat.shape[1])))
 
-    grad_qkv_bias = jnp.sum(grad_lin.astype(F32), axis=1)
+    grad_qkv_bias = jnp.concatenate(
+        [jnp.sum(dq.astype(F32), axis=0)[None], jnp.sum(lin_kv.astype(F32), axis=1)]
+    )
     ours = jnp.concatenate(
         [small_mlp, jnp.zeros((5, feats), F32), small_qkv.reshape(6, feats)]
         + [

time: 1030 us -> 984 us (0.955)
  Pallas kernels: 945 us -> 895 us
    pallas_call x1, Pallas kernels: 98.8 us -> 33.3 us  [attn_out(): pl.pallas_call(attn_out_kernel, in_specs=[VMEM, ANY, ANY, VMEM, VMEM, VME...]
    pallas_call x4, Pallas kernels: 420 us -> 448 us  [the longest x1 240 us: streams_back(): pl.pallas_call(streams_back_kernel, in_specs=[VMEM, VMEM, ANY, ANY, VMEM,...]
    pallas_call x1, Pallas kernels: 77.4 us -> 55.4 us  [front(): pl.pallas_call(functools.partial(front_kernel, seqs, owners), grid=(rows...]
    unnamed x88 -> x80, local copies, waits for them, and re-layouts: 29 us -> 26 us
  transfers between devices with their start and end apart: 10 -> 11, of which waited for: 0 -> 1; matrix products, arithmetic and copies ran while one was open for 2% -> 3% of each run, Pallas kernels for 83% -> 91%
where the time goes in v4:
time: 984 us; the launch traced here: 982 us
  Pallas kernels  895 us (91%)
  local copies, waits for them, and re-layouts  35.1 us (4%)
  other arithmetic  20.6 us (2%)
  between operations  14.6 us (1%)
  waiting for transfers between devices  11.4 us (1%)
    pallas_call x1, Pallas kernels, streams_back(): pl.pallas_call(streams_back_kernel, in_specs=[VMEM, VMEM, ANY, ANY, VMEM,...  240 us
    pallas_call x1, Pallas kernels, mlp_back(): pl.pallas_call(mlp_back_kernel, in_specs=[VMEM, VMEM, VMEM, VMEM, VMEM, A...  190 us
    pallas_call x1, Pallas kernels, spread_vals(): pl.pallas_call(spread_kernel, in_specs=[ANY], out_specs=ANY, out_shape=ja...  72.5 us
    pallas_call x1, Pallas kernels, share(): pl.pallas_call(share_kernel, in_specs=[ANY, ANY, ANY], out_specs=[ANY, AN...  71.3 us
    pallas_call x1, Pallas kernels, spread_dq(): pl.pallas_call(spread_dq_kernel, in_specs=[VMEM, ANY, ANY, VMEM], out_spe...  63.6 us
    pallas_call x1, Pallas kernels, front(): pl.pallas_call(functools.partial(front_kernel, seqs, owners), grid=(rows...  55.4 us
    pallas_call x1, Pallas kernels, last(): pl.pallas_call(last_kernel, grid=(rows // tile,), in_specs=[pl.BlockSpec(...  48 us
    pallas_call x1, Pallas kernels, attn_out(): pl.pallas_call(attn_out_kernel, in_specs=[VMEM, ANY, ANY, VMEM, VMEM, VME...  33.3 us
  transfers between devices with their start and end apart: 11, of which 1 were waited for; matrix products, arithmetic and copies ran while one was open for 3% of the time, Pallas kernels for 91%

profile of v4, /device:TPU:0, one launch (start us, length us, event | category | flops | bytes accessed | tf_op | source)
XLA Modules:
  0.0 982.2 jit_solution(18088733178806223268)
XLA Ops:
  7.3 1.9 fusion.1
  12.0 55.4 %front.1 = (bf16[3,1024,2048]{2,1,0:T(8,128)(2,1)}, f32[1024,2048]{1,0:T(8,128)}, f32[1024,16]{1,0:T(8,128)S(1)}, f32[1024,16]{1,0:T(8,128)S(1)}, bf16[2048,16]{1,0:T(8,128)(2,1)S(1)}) custom-call(bf16[4,1024,2048]{2,1,0:T(8,128)(2,1)} %bitcast.84, f32[1,2048]{1,0:T(1,128)S(1)} %bitcast.80, bf16[256,16]{1,0:T(8,128)(2,1)S(1)} %copy.38.w1, ...), custom_call_target="tpu_custom_call" | custom-call | bytes 135000000 | tf_op jit(solution)/shard_map/front/pallas_call | solution.py:141
  67.4 1.9 multiply_cosine_fusion
  70.1 2.2 copy-done.11
  72.3 10.0 %project.2.kv = bf16[2,1024,512]{2,1,0:T(8,128)(2,1)S(1)} custom-call(bf16[3,1024,2048]{2,1,0:T(8,128)(2,1)} %get-tuple-element.68.lhs.normed.normed_in, bf16[2048,1024]{1,0:T(8,128)(2,1)S(1)} %copy-done.11, f32[2,1,512]{2,1,0:T(1,128)S(1)} %reshape.134.bias, f32[3,1024,128]{2,1,0:T(8,128)S(1)} %pad_maximum_fusion.1.tables.t), custom_call_target="tpu_custom_call" | custom-call | bytes 24000000 | tf_op jit(solution)/shard_map/project/pallas_call | solution.py:222
  82.3 71.3 %share.1 = (bf16[2,2,1024,512]{3,2,1,0:T(8,128)(2,1)}, bf16[4,256,512]{2,1,0:T(8,128)(2,1)}, bf16[4,768,512]{2,1,0:T(8,128)(2,1)}) custom-call(bf16[2,1024,512]{2,1,0:T(8,128)(2,1)S(1)} %project.2.kv, bf16[256,512]{1,0:T(8,128)(2,1)S(1)} %copy-done.20, bf16[768,512]{1,0:T(8,128)(2,1)S(1)} %bitcast.76), custom_call_target="tpu_custom_call" | custom-call | bytes 216000000 | tf_op jit(solution)/shard_map/share/pallas_call | solution.py:276
  153.8 8.6 all-gather.17.cloned.1.call-done
  162.4 1.6 copy-done.16
  164.0 5.7 project.3
  169.6 15.6 %attend.1 = bf16[2,512,512]{2,1,0:T(8,128)(2,1)S(1)} custom-call(s32[3]{0:T(128)S(1)} %pad_add_fusion.scalars, bf16[2,512,512]{2,1,0:T(8,128)(2,1)S(1)} %bitcast.69, bf16[2,2,2,512,512]{4,3,2,1,0:T(8,128)(2,1)S(1)} %bitcast.65, bf16[2,2,2,512,512]{4,3,2,1,0:T(8,128)(2,1)S(1)} %bitcast.66), custom_call_target="tpu_custom_call" | custom-call | bytes 45000000 | tf_op jit(solution)/shard_map/attend/pallas_call | solution.py:314
  185.3 72.5 %spread_vals.1.slots = bf16[4,1024,512]{2,1,0:T(8,128)(2,1)S(1)} custom-call(bf16[1024,512]{1,0:T(8,128)(2,1)S(1)} %bitcast.67), custom_call_target="tpu_custom_call" | custom-call | bytes 210000000 | tf_op jit(solution)/shard_map/spread_vals/pallas_call | solution.py:599
  257.8 2.0 copy-done.1
  260.1 4.6 bitcast_select_fusion.cot
  264.6 33.3 %attn_out.1 = (f32[256,2048]{1,0:T(8,128)S(1)}, bf16[1024,2048]{1,0:T(8,128)(2,1)}) custom-call(bf16[4,1024,512]{2,1,0:T(8,128)(2,1)} %copy-done.1, bf16[8,4,256,512]{3,2,1,0:T(8,128)(2,1)} %bitcast.87, f32[1024,2048]{1,0:T(8,128)} %get-tuple-element.78.resid, f32[1,2048]{1,0:T(1,128)S(1)} %bitcast.82, f32[1,2048]{1,0:T(1,128)S(1)} %slice.72.lg, ...), custom_call_target="tpu_custom_call" | custom-call | bytes 90000000 | tf_op jit(solution)/shard_map/attn_out/pallas_call | solution.py:662
  299.3 3.1 constant_dynamic-slice_fusion
  302.4 32.0 %mlp.1 = (bf16[1024,2048]{1,0:T(8,128)(2,1)S(1)}, bf16[1024,2048]{1,0:T(8,128)(2,1)}, f32[1,2048]{1,0:T(1,128)S(1)}) custom-call(bf16[1024,2048]{1,0:T(8,128)(2,1)} %get-tuple-element.79.mlp_in, bf16[1024,2048]{1,0:T(8,128)(2,1)} %bitcast_select_fusion.cot, bf16[2048,2048]{1,0:T(8,128)(2,1)} %all-gather.11.cloned.1.call-done.up.rhs, ...), custom_call_target="tpu_custom_call" | custom-call | bytes 75000000 | tf_op jit(solution)/shard_map/mlp/pallas_call | solution.py:1288
  334.4 1.9 copy-done.12
  336.3 190.3 %mlp_back.1 = (bf16[1024,2048]{1,0:T(8,128)(2,1)}, f32[3,2048]{1,0:T(4,128)}, bf16[256,2048]{1,0:T(8,128)(2,1)}, bf16[2048,2048]{1,0:T(8,128)(2,1)}, bf16[2048,2048]{1,0:T(8,128)(2,1)}) custom-call(bf16[1024,2048]{1,0:T(8,128)(2,1)} %get-tuple-element.82.lhs, bf16[2048,2048]{1,0:T(8,128)(2,1)} %all-gather.11.cloned.1.call-done.up.rhs, ...), custom_call_target="tpu_custom_call" | custom-call | bytes 525000000 | tf_op jit(solution)/shard_map/mlp_back/pallas_call | solution.py:1000
  526.7 5.3 convolution_convert_fusion
  532.0 23.5 %attend_back.1 = (bf16[2,512,512]{2,1,0:T(8,128)(2,1)S(1)}, bf16[2,2,2,512,512]{4,3,2,1,0:T(8,128)(2,1)}) custom-call(s32[3]{0:T(128)S(1)} %pad_add_fusion.scalars, bf16[2,512,512]{2,1,0:T(8,128)(2,1)S(1)} %bitcast.70, bf16[2,2,2,512,512]{4,3,2,1,0:T(8,128)(2,1)} %bitcast.63, bf16[2,2,2,512,512]{4,3,2,1,0:T(8,128)(2,1)} %bitcast.64, ...), custom_call_target="tpu_custom_call" | custom-call | bytes 75000000 | tf_op jit(solution)/shard_map/attend_back/pallas_call | solution.py:364
  557.7 63.6 %spread_dq.1 = (bf16[4,1024,512]{2,1,0:T(8,128)(2,1)S(1)}, bf16[2048,1024]{1,0:T(8,128)(2,1)S(1)}) custom-call(bf16[1024,512]{1,0:T(8,128)(2,1)S(1)} %bitcast.75, bf16[3,1024,2048]{2,1,0:T(8,128)(2,1)} %get-tuple-element.68.lhs.normed.normed_in, bf16[1024,2048]{1,0:T(8,128)(2,1)} %get-tuple-element.85.grad_attn.attn, bf16[1024,512]{1,0:T(8,128)(2,1)S(1)} %bitcast.68), custom_call_target="tpu_custom_call" | custom-call | bytes 210000000 | tf_op jit(solution)/shard_map/spread_dq/pallas_call | solution.py:761
  621.3 2.0 copy-done.6
  623.3 1.9 copy-done.10
  626.7 1.6 copy-done.5
  631.8 240.2 %streams_back.1 = (bf16[3,1024,2048]{2,1,0:T(8,128)(2,1)}, f32[2,3,2048]{2,1,0:T(4,128)}, bf16[2048,1024]{1,0:T(8,128)(2,1)}, bf16[4,256,2048]{2,1,0:T(8,128)(2,1)}) custom-call(bf16[4,1024,512]{2,1,0:T(8,128)(2,1)} %copy-done.6, bf16[2,1024,512]{2,1,0:T(8,128)(2,1)} %pad_maximum_fusion.lin, ...), custom_call_target="tpu_custom_call" | custom-call | bytes 720000000 | tf_op jit(solution)/shard_map/streams_back/pallas_call | solution.py:1173
  872.2 3.2 convert_reduce_fusion
  876.1 2.2 copy-done.2
  879.4 48.0 %last.1 = (f32[4,1024,2048]{2,1,0:T(8,128)}, f32[1,2048]{1,0:T(1,128)S(1)}, f32[16,2048]{1,0:T(8,128)S(1)}, f32[16,16]{1,0:T(8,128)S(1)}) custom-call(bf16[4,1024,2048]{2,1,0:T(8,128)(2,1)} %bitcast.86, bf16[3,1024,2048]{2,1,0:T(8,128)(2,1)} %get-tuple-element.105.streams, bf16[1024,2048]{1,0:T(8,128)(2,1)S(1)} %copy-done.2, f32[1024,16]{1,0:T(8,128)S(1)} %copy-done.15, ...), custom_call_target="tpu_custom_call" | custom-call | bytes 90000000 | tf_op jit(solution)/shard_map/last/pallas_call | solution.py:1387
  927.7 32.4 %small_sums.1 = (f32[24,2048]{1,0:T(8,128)S(1)}, f32[32,128]{1,0:T(8,128)S(1)}) custom-call(f32[24,2048]{1,0:T(8,128)S(1)} %concatenate.33.ours, f32[8,32,128]{2,1,0:T(8,128)S(1)} %reshape.150.share), custom_call_target="tpu_custom_call" | custom-call | bytes 36000000 | tf_op jit(solution)/shard_map/small_sums/pallas_call | solution.py:1248
  962.0 2.8 convert_element_type.56
  964.8 1.6 convert_element_type.57
  970.9 4.8 copy.47
  (148 shorter events, 20.8 us)
Async XLA Ops:
  7.2 4.4 copy-start.36
  7.2 4.6 copy-start.34
  7.2 4.7 copy-start.35
  7.2 4.7 copy-start.24
  7.2 4.7 copy-start.25
  7.2 4.7 copy-start.21
  7.2 4.7 copy-start.23
  7.3 62.8 %all-gather.9.cloned.1.call-start = ((), (), s32[]{:S(2)}) async-start(), calls=%async_computation.5 | async-start | bytes 4718592 | tf_op jit(solution)/shard_map/all_gather | solution.py:1475
  10.1 143.7 %all-gather.11.cloned.1.call-start = ((), (), s32[]{:S(2)}) async-start(), calls=%async_computation.6 | async-start | bytes 9437184 | tf_op jit(solution)/shard_map/all_gather | solution.py:1488
  10.8 151.5 %all-gather.17.cloned.1.call-start = ((), (), s32[]{:S(2)}) async-start(), calls=%async_computation.14 | async-start | bytes 2359296 | tf_op jit(solution)/shard_map/all_gather | solution.py:1476
  11.5 253.1 %all-gather.19.cloned.1.call-start = ((), (), s32[]{:S(2)}) async-start(), calls=%async_computation.15 | async-start | bytes 9437184 | tf_op jit(solution)/shard_map/all_gather | solution.py:1494
  72.3 10.0 %copy-start.13 = (bf16[3,256,512]{2,1,0:T(8,128)(2,1)S(1)}, bf16[3,256,512]{2,1,0:T(8,128)(2,1)}, u32[]{:S(2)}) copy-start(bf16[3,256,512]{2,1,0:T(8,128)(2,1)} %param.26) | copy-start | bytes 2359300
  72.3 10.0 %copy-start.20 = (bf16[256,512]{1,0:T(8,128)(2,1)S(1)}, bf16[256,512]{1,0:T(8,128)(2,1)}, u32[]{:S(2)}) copy-start(bf16[256,512]{1,0:T(8,128)(2,1)} %shard_out.1) | copy-start | bytes 786436
  82.3 71.4 %copy-start.37 = (s32[2]{0:T(128)S(1)}, s32[2]{0:T(128)}, u32[]{:S(2)}) copy-start(s32[2]{0:T(128)} %param.19) | copy-start | bytes 28
  153.6 148.8 %all-gather.15.cloned.1.call-start = ((), (), s32[]{:S(2)}) async-start(), calls=%async_computation.8 | async-start | bytes 9437184 | tf_op jit(solution)/shard_map/all_gather | solution.py:1498
  163.9 5.7 copy-start
  169.6 15.6 %copy-start.3 = (bf16[1,1024,512]{2,1,0:T(8,128)(2,1)}, bf16[1,1024,512]{2,1,0:T(8,128)(2,1)S(1)}, u32[]{:S(2)}) copy-start(bf16[1,1024,512]{2,1,0:T(8,128)(2,1)S(1)} %project.3) | copy-start | bytes 3145732
  185.3 371.2 %all-gather.13.cloned.1.call-start = ((), (), s32[]{:S(2)}) async-start(), calls=%async_computation.7 | async-start | bytes 28311552 | tf_op jit(solution)/shard_map/all_gather | solution.py:1501
  259.8 365.4 %reduce-scatter.6.cloned.1.call-start = ((), (), s32[]{:S(2)}) async-start(), calls=%async_computation.9 | async-start | bytes 6291456 | tf_op jit(solution)/shard_map/reduce_scatter | solution.py:1518
  259.9 4.7 copy-start.22
  260.0 4.6 copy-start.26
  526.7 5.3 copy-start.4
  556.4 315.7 %reduce-scatter.12.cloned.1.call-start = ((), (), s32[]{:S(2)}) async-start(), calls=%async_computation.12 | async-start | bytes 4718592 | tf_op jit(solution)/shard_map/reduce_scatter | solution.py:1524
  625.3 246.8 %reduce-scatter.10.cloned.1.call-start = ((), (), s32[]{:S(2)}) async-start(), calls=%async_computation.11 | async-start | bytes 9437184 | tf_op jit(solution)/shard_map/reduce_scatter | solution.py:1524
  626.0 246.1 %reduce-scatter.8.cloned.1.call-start = ((), (), s32[]{:S(2)}) async-start(), calls=%async_computation.10 | async-start | bytes 9437184 | tf_op jit(solution)/shard_map/reduce_scatter | solution.py:1524
  626.6 341.9 %reduce-scatter.14.cloned.1.call-start = ((), (), s32[]{:S(2)}) async-start(), calls=%async_computation.13 | async-start | bytes 4718592 | tf_op jit(solution)/shard_map/reduce_scatter | solution.py:1532
  872.2 3.5 copy-start.29
  872.2 3.9 copy-start.32
  872.2 3.9 copy-start.15
  879.4 48.2 %copy-start.33 = (f32[3,2048]{1,0:T(4,128)S(1)}, f32[3,2048]{1,0:T(4,128)}, u32[]{:S(2)}) copy-start(f32[3,2048]{1,0:T(4,128)} %get-tuple-element.109) | copy-start | bytes 73732
  927.4 37.4 %copy-start.30 = (bf16[256,2048]{1,0:T(8,128)(2,1)S(1)}, bf16[256,2048]{1,0:T(8,128)(2,1)}, u32[]{:S(2)}) copy-start(bf16[256,2048]{1,0:T(8,128)(2,1)} %reduce-scatter.8.cloned.1.call-done) | copy-start | bytes 3145732
  927.4 40.3 %copy-start.31 = (bf16[256,1024]{1,0:T(8,128)(2,1)S(1)}, bf16[256,1024]{1,0:T(8,128)(2,1)}, u32[]{:S(2)}) copy-start(bf16[256,1024]{1,0:T(8,128)(2,1)} %reduce-scatter.12.cloned.1.call-done) | copy-start | bytes 1572868
  (17 other events, 32.5 us)
Sparse Core Ops, SparseCore 0:
  10.5 40.8 all-gather.8
  53.3 73.0 all-gather.10
  128.9 33.4 all-gather.16
  164.1 54.3 all-gather.18
  220.3 54.4 all-gather.14
  276.4 125.4 all-gather.12
  556.6 53.4 reduce-scatter.5
  625.4 52.4 reduce-scatter.11
  681.4 71.3 reduce-scatter.9
  756.5 71.4 reduce-scatter.7
  872.3 55.0 reduce-scatter.13

commit v5 on v4

--- a/solution.py
+++ b/solution.py
@@ -110,7 +110,7 @@
         scale = lax.rsqrt(mean_last(wide * wide) + RMS_EPSILON)
         scratch[part, :] = (wide * scale * gain[...]).astype(BF)
 
-    rows_loop(rows, 16, rms)
+    rows_loop(rows, 64, rms)
     pre = dot(scratch[...], w1_out[...])
     pre_out[...] = pre
     mix_out[...] = dot(pre * normal_cdf(pre), w2[...], precision=EXACT)
@@ -130,7 +130,7 @@
                 normed = centred * inverse * lg[m : m + 1, :] + lb[m : m + 1, :]
                 normed_out[m, part, :] = normed.astype(BF)
 
-    rows_loop(rows, 16, combine)
+    rows_loop(rows, 64, combine)
 
 
 def front(layers, gain, w1, w2, lg, lb, seqs, owners):
@@ -641,7 +641,7 @@
             inverse = lax.rsqrt(mean_last(centred * centred) + NORM_EPSILON)
             stage[slot, sub, :] = (centred * inverse * lg[...] + lb[...]).astype(BF)
 
-        rows_loop(chunk, 16, norm)
+        rows_loop(chunk, 64, norm)
         write_out(index, slot).start()
 
         @pl.when(index == me)
@@ -939,7 +939,7 @@
         sums[1] += fold(grads)
         sums[2] += fold(low.astype(F32))
 
-    rows_loop(chunk, 16, back)
+    rows_loop(chunk, 64, back)
     local = pltpu.make_async_copy(own, grad_out.at[mine, :], local_sems.at[1])
     local.start()
     first.sent()
@@ -987,7 +987,7 @@
         value = hidden[part, :] + (second.whole(total, part) + down_bias[...])
         rows_out[part, :] = value.astype(BF)
 
-    rows_loop(chunk, 16, add)
+    rows_loop(chunk, 64, add)
     second.sent()
     local.wait()
 
@@ -1070,6 +1070,8 @@
 ):
     tile, feats = total.shape
     depth = layers.shape[0]
+    whole_load = pltpu.make_async_copy(hist, layers, layer_sem)
+    whole_load.start()
     rows, width = lin.shape[1], lin.shape[2]
     tiles = rows // tile
     ring = Ring(rows)
@@ -1101,44 +1103,41 @@
             stage.at[slot], grads_out.at[stream, part, :], stage_sems.at[slot]
         )
 
+    def flush(stream):
+        for index in range(tiles):
+            write_out(stream, index, index).wait()
+
     def compute(stream):
         fetch(stream)(lambda copy: copy.wait())
+        if stream == 0:
+            whole_load.wait()
+        else:
+            flush(stream - 1)
 
         def one(index, carry):
             part = pl.ds(pl.multiple_of(index * tile, tile), tile)
-            load = pltpu.make_async_copy(hist.at[:, part, :], layers, layer_sem)
-            load.start()
-            slot = lax.rem(index, 2)
 
             gathered = first if stream == 0 else slots.at[stream - 1]
             ring_product(gathered, weights.at[stream % 2], part, total)
-            load.wait()
-
-            @pl.when(index >= 2)
-            def _():
-                write_out(stream, index - 2, slot).wait()
-
             def back(sub):
                 grads = total[sub, :]
-                latest = layers[depth - 1, sub, :].astype(F32)
-                at = pl.multiple_of(index * tile + sub.start, 16)
-                share = mix[pl.ds(at, 16), :]
+                here = pl.ds(pl.multiple_of(index * tile + sub.start, 64), 64)
+                latest = layers[depth - 1, here, :].astype(F32)
+                share = mix[here, :]
                 mixture = latest
                 for j in range(depth):
                     col = stream * depth + j
-                    mixture = mixture + share[:, col : col + 1] * layers[j, sub, :].astype(F32)
+                    mixture = mixture + share[:, col : col + 1] * layers[j, here, :].astype(F32)
                 step, normed = norm_back(mixture, grads, lg[stream : stream + 1, :])
-                stage[slot, sub, :] = step.astype(BF)
+                stage[index, sub, :] = step.astype(BF)
                 sums[stream, 0] += fold(grads * normed)
                 sums[stream, 1] += fold(grads)
 
-            rows_loop(tile, 16, back)
-            write_out(stream, index, slot).start()
+            rows_loop(tile, 64, back)
+            write_out(stream, index, index).start()
             return carry
 
         lax.fori_loop(0, tiles, one, 0)
-        for index in range(max(tiles - 2, 0), tiles):
-            write_out(stream, index, index % 2).wait()
         if stream == 0:
             fetch(2)(lambda copy: copy.start())
 
@@ -1159,6 +1158,7 @@
     compute(2)
     spreads[2].relay()
     spreads[2].arrive()
+    flush(2)
     for i in range(3):
         for j in range(2):
             small_out[j, i : i + 1, :] = jnp.sum(sums[i, j], axis=0, keepdims=True)
@@ -1184,15 +1184,15 @@
             pltpu.VMEM((2, RING, rows, width), BF),
             pltpu.VMEM((2, RING, feats, width), BF),
             pltpu.VMEM((tile, feats), F32),
-            pltpu.VMEM((depth, tile, feats), BF),
-            pltpu.VMEM((2, tile, feats), BF),
+            pltpu.VMEM((depth, rows, feats), BF),
+            pltpu.VMEM((rows // tile, tile, feats), BF),
             pltpu.VMEM((3, 2, 8, feats), F32),
             pltpu.VMEM((2, rows, 256), BF),
             pltpu.VMEM((2, 256, width), BF),
             pltpu.SemaphoreType.DMA((3, 2, 4)),
             pltpu.SemaphoreType.DMA((2, weight.shape[0])),
             pltpu.SemaphoreType.DMA,
-            pltpu.SemaphoreType.DMA((2,)),
+            pltpu.SemaphoreType.DMA((rows // tile,)),
             pltpu.SemaphoreType.DMA((3,)),
             pltpu.SemaphoreType.DMA((2,)),
             pltpu.SemaphoreType.DMA((2,)),
@@ -1342,7 +1342,7 @@
                 at = m * depth + j
                 grad_mix[part, at : at + 1] = jnp.sum(grads * layers[j], axis=-1, keepdims=True)
 
-    rows_loop(rows, 16, reduce)
+    rows_loop(rows, 64, reduce)
     pre_value = pre[...]
     cdf = normal_cdf(pre_value)
     grads = grad_mix[...]
@@ -1372,7 +1372,7 @@
                 total = total + (grads[0] + grads[1] + grads[2] + grads[3]) + back
             grad_out[j, part, :] = total
 
-    rows_loop(rows, 16, write)
+    rows_loop(rows, 64, write)
 
     @pl.when(step_index == pl.num_programs(0) - 1)
     def _():
@@ -1488,13 +1488,11 @@
     w_up = gather(up_weight, tiled=True)
     kv = project(normed, w_kv, qkv_bias[1:], tables, 1)
     kv_all, ring_out, ring_qkv = share(kv, out_weight, qkv_weight.reshape(-1, width), seqs)
-    kv_all, w_up = tie((kv_all, w_up))
-    kv_all, w_q = tie((kv_all, w_q))
     q = project(normed, w_q, qkv_bias[:1], tables, 0)[0]
     w_out_all = gather(ring_out)
     kv_all = kv_all.reshape(seqs, 2, slots, block_len, width)
     attn_vals = attend(scalars, q, kv_all, heads).reshape(rows, width)
-    attn_vals, down_weight = tie((attn_vals, down_weight))
+    attn_vals, w_up, down_weight = tie((attn_vals, w_up, down_weight))
     w_down = gather(down_weight, tiled=True)
     vals_all = spread_vals(attn_vals)
     vals_all, ring_qkv = tie((vals_all, ring_qkv))

time: 984 us -> 959 us (0.975); the launches traced: 982 us -> 944 us
  Pallas kernels: 895 us -> 863 us
    pallas_call x1, Pallas kernels: 55.4 us -> 44.8 us  [front(): pl.pallas_call(functools.partial(front_kernel, seqs, owners), grid=(rows...]
  transfers between devices with their start and end apart: 11 -> 11, of which waited for: 1 -> 0; matrix products, arithmetic and copies ran while one was open for 3% -> 3% of each run, Pallas kernels for 91% -> 91%
where the time goes in v5:
time: 959 us; the launch traced here: 944 us
  Pallas kernels  863 us (90%)
  local copies, waits for them, and re-layouts  36.3 us (4%)
  other arithmetic  20.6 us (2%)
  between operations  14.7 us (2%)
    pallas_call x1, Pallas kernels, streams_back(): pl.pallas_call(streams_back_kernel, in_specs=[VMEM, VMEM, ANY, ANY, VMEM,...  239 us
    pallas_call x1, Pallas kernels, mlp_back(): pl.pallas_call(mlp_back_kernel, in_specs=[VMEM, VMEM, VMEM, VMEM, VMEM, A...  188 us
    pallas_call x1, Pallas kernels, spread_vals(): pl.pallas_call(spread_kernel, in_specs=[ANY], out_specs=ANY, out_shape=ja...  71.7 us
    pallas_call x1, Pallas kernels, share(): pl.pallas_call(share_kernel, in_specs=[ANY, ANY, ANY], out_specs=[ANY, AN...  71.2 us
    pallas_call x1, Pallas kernels, spread_dq(): pl.pallas_call(spread_dq_kernel, in_specs=[VMEM, ANY, ANY, VMEM], out_spe...  63.8 us
    pallas_call x1, Pallas kernels, front(): pl.pallas_call(functools.partial(front_kernel, seqs, owners), grid=(rows...  44.8 us
    pallas_call x1, Pallas kernels, last(): pl.pallas_call(last_kernel, grid=(rows // tile,), in_specs=[pl.BlockSpec(...  38.7 us
    pallas_call x1, Pallas kernels, small_sums(): pl.pallas_call(functools.partial(small_kernel, seqs, owners), in_specs=[V...  33.9 us
  transfers between devices with their start and end apart: 11, of which 0 were waited for; matrix products, arithmetic and copies ran while one was open for 3% of the time, Pallas kernels for 91%

profile of v5, /device:TPU:0, one launch (start us, length us, event | category | flops | bytes accessed | tf_op | source)
XLA Modules:
  0.0 943.8 jit_solution(9931270541694584571)
XLA Ops:
  7.3 1.9 slice_bitcast_fusion.4
  12.0 44.8 %front.1 = (bf16[3,1024,2048]{2,1,0:T(8,128)(2,1)}, f32[1024,2048]{1,0:T(8,128)}, f32[1024,16]{1,0:T(8,128)S(1)}, f32[1024,16]{1,0:T(8,128)S(1)}, bf16[2048,16]{1,0:T(8,128)(2,1)S(1)}) custom-call(bf16[4,1024,2048]{2,1,0:T(8,128)(2,1)} %bitcast.84, f32[1,2048]{1,0:T(1,128)S(1)} %bitcast.80, bf16[256,16]{1,0:T(8,128)(2,1)S(1)} %copy.38.w1, ...), custom_call_target="tpu_custom_call" | custom-call | bytes 135000000 | tf_op jit(solution)/shard_map/front/pallas_call | solution.py:141
  56.8 1.9 multiply_cosine_fusion
  59.5 2.3 copy-done.11
  61.8 10.0 %project.3.kv = bf16[2,1024,512]{2,1,0:T(8,128)(2,1)S(1)} custom-call(bf16[3,1024,2048]{2,1,0:T(8,128)(2,1)} %get-tuple-element.65.lhs.normed.normed_in, bf16[2048,1024]{1,0:T(8,128)(2,1)S(1)} %copy-done.11, f32[2,1,512]{2,1,0:T(1,128)S(1)} %reshape.135.bias, f32[3,1024,128]{2,1,0:T(8,128)S(1)} %pad_maximum_fusion.1.tables.t), custom_call_target="tpu_custom_call" | custom-call | bytes 24000000 | tf_op jit(solution)/shard_map/project/pallas_call | solution.py:222
  71.8 71.2 %share.1 = (bf16[2,2,1024,512]{3,2,1,0:T(8,128)(2,1)}, bf16[4,256,512]{2,1,0:T(8,128)(2,1)}, bf16[4,768,512]{2,1,0:T(8,128)(2,1)}) custom-call(bf16[2,1024,512]{2,1,0:T(8,128)(2,1)S(1)} %project.3.kv, bf16[256,512]{1,0:T(8,128)(2,1)S(1)} %copy-done.20, bf16[768,512]{1,0:T(8,128)(2,1)S(1)} %bitcast.76), custom_call_target="tpu_custom_call" | custom-call | bytes 216000000 | tf_op jit(solution)/shard_map/share/pallas_call | solution.py:276
  143.2 1.6 copy-done.16
  144.8 5.7 project.2
  150.5 15.6 %attend.1 = bf16[2,512,512]{2,1,0:T(8,128)(2,1)S(1)} custom-call(s32[3]{0:T(128)S(1)} %pad_add_fusion.scalars, bf16[2,512,512]{2,1,0:T(8,128)(2,1)S(1)} %bitcast.69, bf16[2,2,2,512,512]{4,3,2,1,0:T(8,128)(2,1)S(1)} %bitcast.65, bf16[2,2,2,512,512]{4,3,2,1,0:T(8,128)(2,1)S(1)} %bitcast.66), custom_call_target="tpu_custom_call" | custom-call | bytes 45000000 | tf_op jit(solution)/shard_map/attend/pallas_call | solution.py:314
  167.2 71.7 %spread_vals.1.slots = bf16[4,1024,512]{2,1,0:T(8,128)(2,1)S(1)} custom-call(bf16[1024,512]{1,0:T(8,128)(2,1)S(1)} %bitcast.67), custom_call_target="tpu_custom_call" | custom-call | bytes 210000000 | tf_op jit(solution)/shard_map/spread_vals/pallas_call | solution.py:599
  238.9 2.0 copy-done.1
  241.1 4.6 bitcast_select_fusion.cot
  245.7 24.2 %attn_out.1 = (f32[256,2048]{1,0:T(8,128)S(1)}, bf16[1024,2048]{1,0:T(8,128)(2,1)}) custom-call(bf16[4,1024,512]{2,1,0:T(8,128)(2,1)} %copy-done.1, bf16[8,4,256,512]{3,2,1,0:T(8,128)(2,1)} %bitcast.87, f32[1024,2048]{1,0:T(8,128)} %get-tuple-element.72.resid, f32[1,2048]{1,0:T(1,128)S(1)} %bitcast.82, f32[1,2048]{1,0:T(1,128)S(1)} %slice.72.lg, ...), custom_call_target="tpu_custom_call" | custom-call | bytes 90000000 | tf_op jit(solution)/shard_map/attn_out/pallas_call | solution.py:662
  271.2 3.1 constant_dynamic-slice_fusion
  274.3 32.8 %mlp.1 = (bf16[1024,2048]{1,0:T(8,128)(2,1)S(1)}, bf16[1024,2048]{1,0:T(8,128)(2,1)}, f32[1,2048]{1,0:T(1,128)S(1)}) custom-call(bf16[1024,2048]{1,0:T(8,128)(2,1)} %get-tuple-element.73.mlp_in, bf16[1024,2048]{1,0:T(8,128)(2,1)} %bitcast_select_fusion.cot, bf16[2048,2048]{1,0:T(8,128)(2,1)} %all-gather.11.cloned.1.call-done.up.rhs, ...), custom_call_target="tpu_custom_call" | custom-call | bytes 75000000 | tf_op jit(solution)/shard_map/mlp/pallas_call | solution.py:1288
  307.1 1.9 copy-done.12
  309.1 188.0 %mlp_back.1 = (bf16[1024,2048]{1,0:T(8,128)(2,1)}, f32[3,2048]{1,0:T(4,128)}, bf16[256,2048]{1,0:T(8,128)(2,1)}, bf16[2048,2048]{1,0:T(8,128)(2,1)}, bf16[2048,2048]{1,0:T(8,128)(2,1)}) custom-call(bf16[1024,2048]{1,0:T(8,128)(2,1)} %get-tuple-element.76.lhs, bf16[2048,2048]{1,0:T(8,128)(2,1)} %all-gather.11.cloned.1.call-done.up.rhs, ...), custom_call_target="tpu_custom_call" | custom-call | bytes 525000000 | tf_op jit(solution)/shard_map/mlp_back/pallas_call | solution.py:1000
  497.1 5.3 convolution_convert_fusion
  502.4 23.5 %attend_back.1 = (bf16[2,512,512]{2,1,0:T(8,128)(2,1)S(1)}, bf16[2,2,2,512,512]{4,3,2,1,0:T(8,128)(2,1)}) custom-call(s32[3]{0:T(128)S(1)} %pad_add_fusion.scalars, bf16[2,512,512]{2,1,0:T(8,128)(2,1)S(1)} %bitcast.70, bf16[2,2,2,512,512]{4,3,2,1,0:T(8,128)(2,1)} %bitcast.63, bf16[2,2,2,512,512]{4,3,2,1,0:T(8,128)(2,1)} %bitcast.64, ...), custom_call_target="tpu_custom_call" | custom-call | bytes 75000000 | tf_op jit(solution)/shard_map/attend_back/pallas_call | solution.py:364
  528.1 63.8 %spread_dq.1 = (bf16[4,1024,512]{2,1,0:T(8,128)(2,1)S(1)}, bf16[2048,1024]{1,0:T(8,128)(2,1)S(1)}) custom-call(bf16[1024,512]{1,0:T(8,128)(2,1)S(1)} %bitcast.75, bf16[3,1024,2048]{2,1,0:T(8,128)(2,1)} %get-tuple-element.65.lhs.normed.normed_in, bf16[1024,2048]{1,0:T(8,128)(2,1)} %get-tuple-element.79.grad_attn.attn, bf16[1024,512]{1,0:T(8,128)(2,1)S(1)} %bitcast.68), custom_call_target="tpu_custom_call" | custom-call | bytes 210000000 | tf_op jit(solution)/shard_map/spread_dq/pallas_call | solution.py:761
  592.0 2.0 copy-done.6
  594.0 1.9 copy-done.10
  597.5 1.6 copy-done.5
  601.1 1.5 pad_maximum_fusion.lin
  602.6 238.5 %streams_back.1 = (bf16[3,1024,2048]{2,1,0:T(8,128)(2,1)}, f32[2,3,2048]{2,1,0:T(4,128)}, bf16[2048,1024]{1,0:T(8,128)(2,1)}, bf16[4,256,2048]{2,1,0:T(8,128)(2,1)}) custom-call(bf16[4,1024,512]{2,1,0:T(8,128)(2,1)} %copy-done.6, bf16[2,1024,512]{2,1,0:T(8,128)(2,1)} %pad_maximum_fusion.lin, ...), custom_call_target="tpu_custom_call" | custom-call | bytes 720000000 | tf_op jit(solution)/shard_map/streams_back/pallas_call | solution.py:1173
  841.3 3.2 convert_reduce_fusion
  845.3 2.2 copy-done.2
  848.5 38.7 %last.1 = (f32[4,1024,2048]{2,1,0:T(8,128)}, f32[1,2048]{1,0:T(1,128)S(1)}, f32[16,2048]{1,0:T(8,128)S(1)}, f32[16,16]{1,0:T(8,128)S(1)}) custom-call(bf16[4,1024,2048]{2,1,0:T(8,128)(2,1)} %bitcast.86, bf16[3,1024,2048]{2,1,0:T(8,128)(2,1)} %get-tuple-element.99.streams, bf16[1024,2048]{1,0:T(8,128)(2,1)S(1)} %copy-done.2, f32[1024,16]{1,0:T(8,128)S(1)} %copy-done.15, ...), custom_call_target="tpu_custom_call" | custom-call | bytes 90000000 | tf_op jit(solution)/shard_map/last/pallas_call | solution.py:1387
  887.5 33.9 %small_sums.1 = (f32[24,2048]{1,0:T(8,128)S(1)}, f32[32,128]{1,0:T(8,128)S(1)}) custom-call(f32[24,2048]{1,0:T(8,128)S(1)} %concatenate.33.ours, f32[8,32,128]{2,1,0:T(8,128)S(1)} %reshape.150.share), custom_call_target="tpu_custom_call" | custom-call | bytes 36000000 | tf_op jit(solution)/shard_map/small_sums/pallas_call | solution.py:1248
  923.4 2.8 convert_element_type.56
  926.2 1.6 convert_element_type.57
  932.2 4.8 copy.47
  (148 shorter events, 20.4 us)
Async XLA Ops:
  7.2 4.4 copy-start.36
  7.2 4.6 copy-start.34
  7.2 4.7 copy-start.35
  7.2 4.7 copy-start.24
  7.2 4.7 copy-start.25
  7.2 4.7 copy-start.21
  7.2 4.7 copy-start.23
  7.3 52.2 %all-gather.9.cloned.1.call-start = ((), (), s32[]{:S(2)}) async-start(), calls=%async_computation.5 | async-start | bytes 4718592 | tf_op jit(solution)/shard_map/all_gather | solution.py:1475
  10.1 133.2 %all-gather.17.cloned.1.call-start = ((), (), s32[]{:S(2)}) async-start(), calls=%async_computation.14 | async-start | bytes 2359296 | tf_op jit(solution)/shard_map/all_gather | solution.py:1476
  10.8 156.3 %all-gather.11.cloned.1.call-start = ((), (), s32[]{:S(2)}) async-start(), calls=%async_computation.6 | async-start | bytes 9437184 | tf_op jit(solution)/shard_map/all_gather | solution.py:1488
  11.5 234.2 %all-gather.19.cloned.1.call-start = ((), (), s32[]{:S(2)}) async-start(), calls=%async_computation.15 | async-start | bytes 9437184 | tf_op jit(solution)/shard_map/all_gather | solution.py:1492
  61.8 10.0 %copy-start.13 = (bf16[3,256,512]{2,1,0:T(8,128)(2,1)S(1)}, bf16[3,256,512]{2,1,0:T(8,128)(2,1)}, u32[]{:S(2)}) copy-start(bf16[3,256,512]{2,1,0:T(8,128)(2,1)} %param.26) | copy-start | bytes 2359300
  61.8 10.0 %copy-start.20 = (bf16[256,512]{1,0:T(8,128)(2,1)S(1)}, bf16[256,512]{1,0:T(8,128)(2,1)}, u32[]{:S(2)}) copy-start(bf16[256,512]{1,0:T(8,128)(2,1)} %shard_out.1) | copy-start | bytes 786436
  71.8 71.3 %copy-start.37 = (s32[2]{0:T(128)S(1)}, s32[2]{0:T(128)}, u32[]{:S(2)}) copy-start(s32[2]{0:T(128)} %param.19) | copy-start | bytes 28
  143.1 131.2 %all-gather.15.cloned.1.call-start = ((), (), s32[]{:S(2)}) async-start(), calls=%async_computation.8 | async-start | bytes 9437184 | tf_op jit(solution)/shard_map/all_gather | solution.py:1496
  144.8 5.7 copy-start
  167.1 359.7 %all-gather.13.cloned.1.call-start = ((), (), s32[]{:S(2)}) async-start(), calls=%async_computation.7 | async-start | bytes 28311552 | tf_op jit(solution)/shard_map/all_gather | solution.py:1499
  240.9 355.0 %reduce-scatter.6.cloned.1.call-start = ((), (), s32[]{:S(2)}) async-start(), calls=%async_computation.9 | async-start | bytes 6291456 | tf_op jit(solution)/shard_map/reduce_scatter | solution.py:1516
  241.0 4.7 copy-start.22
  241.1 4.6 copy-start.26
  497.1 5.3 copy-start.4
  526.9 314.4 %reduce-scatter.12.cloned.1.call-start = ((), (), s32[]{:S(2)}) async-start(), calls=%async_computation.12 | async-start | bytes 4718592 | tf_op jit(solution)/shard_map/reduce_scatter | solution.py:1522
  596.0 245.3 %reduce-scatter.10.cloned.1.call-start = ((), (), s32[]{:S(2)}) async-start(), calls=%async_computation.11 | async-start | bytes 9437184 | tf_op jit(solution)/shard_map/reduce_scatter | solution.py:1522
  596.7 244.6 %reduce-scatter.8.cloned.1.call-start = ((), (), s32[]{:S(2)}) async-start(), calls=%async_computation.10 | async-start | bytes 9437184 | tf_op jit(solution)/shard_map/reduce_scatter | solution.py:1522
  597.3 332.6 %reduce-scatter.14.cloned.1.call-start = ((), (), s32[]{:S(2)}) async-start(), calls=%async_computation.13 | async-start | bytes 4718592 | tf_op jit(solution)/shard_map/reduce_scatter | solution.py:1530
  841.3 3.3 copy-start.9
  841.3 3.5 copy-start.29
  841.3 3.9 copy-start.32
  841.3 3.9 copy-start.15
  848.5 38.9 %copy-start.33 = (f32[3,2048]{1,0:T(4,128)S(1)}, f32[3,2048]{1,0:T(4,128)}, u32[]{:S(2)}) copy-start(f32[3,2048]{1,0:T(4,128)} %get-tuple-element.103) | copy-start | bytes 73732
  887.2 39.0 %copy-start.30 = (bf16[256,2048]{1,0:T(8,128)(2,1)S(1)}, bf16[256,2048]{1,0:T(8,128)(2,1)}, u32[]{:S(2)}) copy-start(bf16[256,2048]{1,0:T(8,128)(2,1)} %reduce-scatter.8.cloned.1.call-done) | copy-start | bytes 3145732
  887.2 41.8 %copy-start.31 = (bf16[256,1024]{1,0:T(8,128)(2,1)S(1)}, bf16[256,1024]{1,0:T(8,128)(2,1)}, u32[]{:S(2)}) copy-start(bf16[256,1024]{1,0:T(8,128)(2,1)} %reduce-scatter.12.cloned.1.call-done) | copy-start | bytes 1572868
  (17 other events, 30.3 us)
Sparse Core Ops, SparseCore 0:
  10.5 40.8 all-gather.8
  53.9 31.3 all-gather.16
  87.2 73.6 all-gather.10
  162.6 53.6 all-gather.18
  218.0 54.3 all-gather.14
  274.2 125.3 all-gather.12
  527.0 54.6 reduce-scatter.5
  596.1 52.5 reduce-scatter.11
  652.1 71.2 reduce-scatter.9
  727.1 71.2 reduce-scatter.7
  841.4 57.3 reduce-scatter.13

commit v6 on v5

--- a/solution.py
+++ b/solution.py
@@ -110,7 +110,7 @@
         scale = lax.rsqrt(mean_last(wide * wide) + RMS_EPSILON)
         scratch[part, :] = (wide * scale * gain[...]).astype(BF)
 
-    rows_loop(rows, 64, rms)
+    rows_loop(rows, 16, rms)
     pre = dot(scratch[...], w1_out[...])
     pre_out[...] = pre
     mix_out[...] = dot(pre * normal_cdf(pre), w2[...], precision=EXACT)
@@ -130,7 +130,7 @@
                 normed = centred * inverse * lg[m : m + 1, :] + lb[m : m + 1, :]
                 normed_out[m, part, :] = normed.astype(BF)
 
-    rows_loop(rows, 64, combine)
+    rows_loop(rows, 32, combine)
 
 
 def front(layers, gain, w1, w2, lg, lb, seqs, owners):
@@ -418,7 +418,7 @@
     )
 
 
-def product(lhs, rhs, start, count, write, step=512):
+def product(lhs, rhs, start, count, write, step=256):
     total = rhs.shape[0]
 
     def one(cols):
@@ -579,7 +579,7 @@
             value += dot(slots[z, part, :], weight[z, cols, :], NT)
         total[:, cols] = value
 
-    rows_loop(total.shape[1], 512, columns)
+    rows_loop(total.shape[1], 256, columns)
 
 
 def spread_kernel(vals, out, sems, own_sem):
@@ -726,7 +726,7 @@
         def columns(cols):
             stage[slot, :, cols] = dot(blocks[slot], rhs[:, cols], TN).astype(BF)
 
-        rows_loop(rhs.shape[1], 512, columns)
+        rows_loop(rhs.shape[1], 256, columns)
         store(n, slot).start()
         return carry
 
@@ -939,7 +939,7 @@
         sums[1] += fold(grads)
         sums[2] += fold(low.astype(F32))
 
-    rows_loop(chunk, 64, back)
+    rows_loop(chunk, 16, back)
     local = pltpu.make_async_copy(own, grad_out.at[mine, :], local_sems.at[1])
     local.start()
     first.sent()
@@ -987,7 +987,7 @@
         value = hidden[part, :] + (second.whole(total, part) + down_bias[...])
         rows_out[part, :] = value.astype(BF)
 
-    rows_loop(chunk, 64, add)
+    rows_loop(chunk, 16, add)
     second.sent()
     local.wait()
 
@@ -1121,7 +1121,7 @@
             ring_product(gathered, weights.at[stream % 2], part, total)
             def back(sub):
                 grads = total[sub, :]
-                here = pl.ds(pl.multiple_of(index * tile + sub.start, 64), 64)
+                here = pl.ds(pl.multiple_of(index * tile + sub.start, 16), 16)
                 latest = layers[depth - 1, here, :].astype(F32)
                 share = mix[here, :]
                 mixture = latest
@@ -1133,7 +1133,7 @@
                 sums[stream, 0] += fold(grads * normed)
                 sums[stream, 1] += fold(grads)
 
-            rows_loop(tile, 64, back)
+            rows_loop(tile, 16, back)
             write_out(stream, index, index).start()
             return carry
 

time: 959 us -> 960 us (level); the launches traced: 944 us -> 958 us
  Pallas kernels: 863 us -> 878 us
  transfers between devices with their start and end apart: 11 -> 11, of which waited for: 0 -> 0; matrix products, arithmetic and copies ran while one was open for 3% -> 3% of each run, Pallas kernels for 91% -> 92%
where the time goes in v6:
time: 960 us; the launch traced here: 958 us
  Pallas kernels  878 us (91%)
  local copies, waits for them, and re-layouts  36.1 us (4%)
  other arithmetic  20.6 us (2%)
  between operations  14.6 us (2%)
    pallas_call x1, Pallas kernels, streams_back(): pl.pallas_call(streams_back_kernel, in_specs=[VMEM, VMEM, ANY, ANY, VMEM,...  243 us
    pallas_call x1, Pallas kernels, mlp_back(): pl.pallas_call(mlp_back_kernel, in_specs=[VMEM, VMEM, VMEM, VMEM, VMEM, A...  192 us
    pallas_call x1, Pallas kernels, spread_vals(): pl.pallas_call(spread_kernel, in_specs=[ANY], out_specs=ANY, out_shape=ja...  71.7 us
    pallas_call x1, Pallas kernels, share(): pl.pallas_call(share_kernel, in_specs=[ANY, ANY, ANY], out_specs=[ANY, AN...  71.2 us
    pallas_call x1, Pallas kernels, spread_dq(): pl.pallas_call(spread_dq_kernel, in_specs=[VMEM, ANY, ANY, VMEM], out_spe...  67.2 us
    pallas_call x1, Pallas kernels, front(): pl.pallas_call(functools.partial(front_kernel, seqs, owners), grid=(rows...  48.7 us
    pallas_call x1, Pallas kernels, last(): pl.pallas_call(last_kernel, grid=(rows // tile,), in_specs=[pl.BlockSpec(...  38.6 us
    pallas_call x1, Pallas kernels, mlp(): pl.pallas_call(mlp_kernel, grid=(width // cols, rows // tile), in_specs=[...  32.9 us
  transfers between devices with their start and end apart: 11, of which 0 were waited for; matrix products, arithmetic and copies ran while one was open for 3% of the time, Pallas kernels for 92%

profile of v6, /device:TPU:0, one launch (start us, length us, event | category | flops | bytes accessed | tf_op | source)
XLA Modules:
  0.0 958.0 jit_solution(9604915040868094499)
XLA Ops:
  7.3 1.9 slice_bitcast_fusion.4
  12.0 48.7 %front.1 = (bf16[3,1024,2048]{2,1,0:T(8,128)(2,1)}, f32[1024,2048]{1,0:T(8,128)}, f32[1024,16]{1,0:T(8,128)S(1)}, f32[1024,16]{1,0:T(8,128)S(1)}, bf16[2048,16]{1,0:T(8,128)(2,1)S(1)}) custom-call(bf16[4,1024,2048]{2,1,0:T(8,128)(2,1)} %bitcast.84, f32[1,2048]{1,0:T(1,128)S(1)} %bitcast.80, bf16[256,16]{1,0:T(8,128)(2,1)S(1)} %copy.38.w1, ...), custom_call_target="tpu_custom_call" | custom-call | bytes 135000000 | tf_op jit(solution)/shard_map/front/pallas_call | solution.py:141
  60.7 1.9 multiply_cosine_fusion
  63.4 2.2 copy-done.11
  65.6 10.0 %project.3.kv = bf16[2,1024,512]{2,1,0:T(8,128)(2,1)S(1)} custom-call(bf16[3,1024,2048]{2,1,0:T(8,128)(2,1)} %get-tuple-element.65.lhs.normed.normed_in, bf16[2048,1024]{1,0:T(8,128)(2,1)S(1)} %copy-done.11, f32[2,1,512]{2,1,0:T(1,128)S(1)} %reshape.135.bias, f32[3,1024,128]{2,1,0:T(8,128)S(1)} %pad_maximum_fusion.1.tables.t), custom_call_target="tpu_custom_call" | custom-call | bytes 24000000 | tf_op jit(solution)/shard_map/project/pallas_call | solution.py:222
  75.6 71.2 %share.1 = (bf16[2,2,1024,512]{3,2,1,0:T(8,128)(2,1)}, bf16[4,256,512]{2,1,0:T(8,128)(2,1)}, bf16[4,768,512]{2,1,0:T(8,128)(2,1)}) custom-call(bf16[2,1024,512]{2,1,0:T(8,128)(2,1)S(1)} %project.3.kv, bf16[256,512]{1,0:T(8,128)(2,1)S(1)} %copy-done.20, bf16[768,512]{1,0:T(8,128)(2,1)S(1)} %bitcast.76), custom_call_target="tpu_custom_call" | custom-call | bytes 216000000 | tf_op jit(solution)/shard_map/share/pallas_call | solution.py:276
  147.0 1.6 copy-done.16
  148.6 5.7 project.2
  154.3 15.6 %attend.1 = bf16[2,512,512]{2,1,0:T(8,128)(2,1)S(1)} custom-call(s32[3]{0:T(128)S(1)} %pad_add_fusion.scalars, bf16[2,512,512]{2,1,0:T(8,128)(2,1)S(1)} %bitcast.69, bf16[2,2,2,512,512]{4,3,2,1,0:T(8,128)(2,1)S(1)} %bitcast.65, bf16[2,2,2,512,512]{4,3,2,1,0:T(8,128)(2,1)S(1)} %bitcast.66), custom_call_target="tpu_custom_call" | custom-call | bytes 45000000 | tf_op jit(solution)/shard_map/attend/pallas_call | solution.py:314
  170.9 71.7 %spread_vals.1.slots = bf16[4,1024,512]{2,1,0:T(8,128)(2,1)S(1)} custom-call(bf16[1024,512]{1,0:T(8,128)(2,1)S(1)} %bitcast.67), custom_call_target="tpu_custom_call" | custom-call | bytes 210000000 | tf_op jit(solution)/shard_map/spread_vals/pallas_call | solution.py:599
  242.6 2.0 copy-done.1
  244.9 4.6 bitcast_select_fusion.cot
  249.4 26.7 %attn_out.1 = (f32[256,2048]{1,0:T(8,128)S(1)}, bf16[1024,2048]{1,0:T(8,128)(2,1)}) custom-call(bf16[4,1024,512]{2,1,0:T(8,128)(2,1)} %copy-done.1, bf16[8,4,256,512]{3,2,1,0:T(8,128)(2,1)} %bitcast.87, f32[1024,2048]{1,0:T(8,128)} %get-tuple-element.72.resid, f32[1,2048]{1,0:T(1,128)S(1)} %bitcast.82, f32[1,2048]{1,0:T(1,128)S(1)} %slice.72.lg, ...), custom_call_target="tpu_custom_call" | custom-call | bytes 90000000 | tf_op jit(solution)/shard_map/attn_out/pallas_call | solution.py:662
  277.5 3.1 constant_dynamic-slice_fusion
  280.6 32.9 %mlp.1 = (bf16[1024,2048]{1,0:T(8,128)(2,1)S(1)}, bf16[1024,2048]{1,0:T(8,128)(2,1)}, f32[1,2048]{1,0:T(1,128)S(1)}) custom-call(bf16[1024,2048]{1,0:T(8,128)(2,1)} %get-tuple-element.73.mlp_in, bf16[1024,2048]{1,0:T(8,128)(2,1)} %bitcast_select_fusion.cot, bf16[2048,2048]{1,0:T(8,128)(2,1)} %all-gather.11.cloned.1.call-done.up.rhs, ...), custom_call_target="tpu_custom_call" | custom-call | bytes 75000000 | tf_op jit(solution)/shard_map/mlp/pallas_call | solution.py:1288
  313.5 1.9 copy-done.12
  315.4 192.1 %mlp_back.1 = (bf16[1024,2048]{1,0:T(8,128)(2,1)}, f32[3,2048]{1,0:T(4,128)}, bf16[256,2048]{1,0:T(8,128)(2,1)}, bf16[2048,2048]{1,0:T(8,128)(2,1)}, bf16[2048,2048]{1,0:T(8,128)(2,1)}) custom-call(bf16[1024,2048]{1,0:T(8,128)(2,1)} %get-tuple-element.76.lhs, bf16[2048,2048]{1,0:T(8,128)(2,1)} %all-gather.11.cloned.1.call-done.up.rhs, ...), custom_call_target="tpu_custom_call" | custom-call | bytes 525000000 | tf_op jit(solution)/shard_map/mlp_back/pallas_call | solution.py:1000
  507.5 5.3 convolution_convert_fusion
  512.8 23.5 %attend_back.1 = (bf16[2,512,512]{2,1,0:T(8,128)(2,1)S(1)}, bf16[2,2,2,512,512]{4,3,2,1,0:T(8,128)(2,1)}) custom-call(s32[3]{0:T(128)S(1)} %pad_add_fusion.scalars, bf16[2,512,512]{2,1,0:T(8,128)(2,1)S(1)} %bitcast.70, bf16[2,2,2,512,512]{4,3,2,1,0:T(8,128)(2,1)} %bitcast.63, bf16[2,2,2,512,512]{4,3,2,1,0:T(8,128)(2,1)} %bitcast.64, ...), custom_call_target="tpu_custom_call" | custom-call | bytes 75000000 | tf_op jit(solution)/shard_map/attend_back/pallas_call | solution.py:364
  538.5 67.2 %spread_dq.1 = (bf16[4,1024,512]{2,1,0:T(8,128)(2,1)S(1)}, bf16[2048,1024]{1,0:T(8,128)(2,1)S(1)}) custom-call(bf16[1024,512]{1,0:T(8,128)(2,1)S(1)} %bitcast.75, bf16[3,1024,2048]{2,1,0:T(8,128)(2,1)} %get-tuple-element.65.lhs.normed.normed_in, bf16[1024,2048]{1,0:T(8,128)(2,1)} %get-tuple-element.79.grad_attn.attn, bf16[1024,512]{1,0:T(8,128)(2,1)S(1)} %bitcast.68), custom_call_target="tpu_custom_call" | custom-call | bytes 210000000 | tf_op jit(solution)/shard_map/spread_dq/pallas_call | solution.py:761
  605.7 2.0 copy-done.6
  607.7 1.9 copy-done.10
  611.3 1.6 copy-done.5
  614.9 1.5 pad_maximum_fusion.lin
  616.4 242.6 %streams_back.1 = (bf16[3,1024,2048]{2,1,0:T(8,128)(2,1)}, f32[2,3,2048]{2,1,0:T(4,128)}, bf16[2048,1024]{1,0:T(8,128)(2,1)}, bf16[4,256,2048]{2,1,0:T(8,128)(2,1)}) custom-call(bf16[4,1024,512]{2,1,0:T(8,128)(2,1)} %copy-done.6, bf16[2,1024,512]{2,1,0:T(8,128)(2,1)} %pad_maximum_fusion.lin, ...), custom_call_target="tpu_custom_call" | custom-call | bytes 720000000 | tf_op jit(solution)/shard_map/streams_back/pallas_call | solution.py:1173
  859.2 3.2 convert_reduce_fusion
  863.1 2.2 copy-done.2
  866.4 38.6 %last.1 = (f32[4,1024,2048]{2,1,0:T(8,128)}, f32[1,2048]{1,0:T(1,128)S(1)}, f32[16,2048]{1,0:T(8,128)S(1)}, f32[16,16]{1,0:T(8,128)S(1)}) custom-call(bf16[4,1024,2048]{2,1,0:T(8,128)(2,1)} %bitcast.86, bf16[3,1024,2048]{2,1,0:T(8,128)(2,1)} %get-tuple-element.99.streams, bf16[1024,2048]{1,0:T(8,128)(2,1)S(1)} %copy-done.2, f32[1024,16]{1,0:T(8,128)S(1)} %copy-done.15, ...), custom_call_target="tpu_custom_call" | custom-call | bytes 90000000 | tf_op jit(solution)/shard_map/last/pallas_call | solution.py:1387
  905.3 30.6 %small_sums.1 = (f32[24,2048]{1,0:T(8,128)S(1)}, f32[32,128]{1,0:T(8,128)S(1)}) custom-call(f32[24,2048]{1,0:T(8,128)S(1)} %concatenate.33.ours, f32[8,32,128]{2,1,0:T(8,128)S(1)} %reshape.150.share), custom_call_target="tpu_custom_call" | custom-call | bytes 36000000 | tf_op jit(solution)/shard_map/small_sums/pallas_call | solution.py:1248
  937.8 2.8 convert_element_type.56
  940.6 1.6 convert_element_type.57
  946.6 4.8 copy.47
  (148 shorter events, 20.5 us)
Async XLA Ops:
  7.2 4.4 copy-start.36
  7.2 4.6 copy-start.34
  7.2 4.7 copy-start.35
  7.2 4.7 copy-start.24
  7.2 4.7 copy-start.25
  7.2 4.7 copy-start.21
  7.2 4.7 copy-start.23
  7.3 56.1 %all-gather.9.cloned.1.call-start = ((), (), s32[]{:S(2)}) async-start(), calls=%async_computation.5 | async-start | bytes 4718592 | tf_op jit(solution)/shard_map/all_gather | solution.py:1475
  10.1 136.9 %all-gather.17.cloned.1.call-start = ((), (), s32[]{:S(2)}) async-start(), calls=%async_computation.14 | async-start | bytes 2359296 | tf_op jit(solution)/shard_map/all_gather | solution.py:1476
  10.8 160.0 %all-gather.11.cloned.1.call-start = ((), (), s32[]{:S(2)}) async-start(), calls=%async_computation.6 | async-start | bytes 9437184 | tf_op jit(solution)/shard_map/all_gather | solution.py:1488
  11.5 237.9 %all-gather.19.cloned.1.call-start = ((), (), s32[]{:S(2)}) async-start(), calls=%async_computation.15 | async-start | bytes 9437184 | tf_op jit(solution)/shard_map/all_gather | solution.py:1492
  65.6 10.0 %copy-start.13 = (bf16[3,256,512]{2,1,0:T(8,128)(2,1)S(1)}, bf16[3,256,512]{2,1,0:T(8,128)(2,1)}, u32[]{:S(2)}) copy-start(bf16[3,256,512]{2,1,0:T(8,128)(2,1)} %param.26) | copy-start | bytes 2359300
  65.6 10.0 %copy-start.20 = (bf16[256,512]{1,0:T(8,128)(2,1)S(1)}, bf16[256,512]{1,0:T(8,128)(2,1)}, u32[]{:S(2)}) copy-start(bf16[256,512]{1,0:T(8,128)(2,1)} %shard_out.1) | copy-start | bytes 786436
  75.5 71.4 %copy-start.37 = (s32[2]{0:T(128)S(1)}, s32[2]{0:T(128)}, u32[]{:S(2)}) copy-start(s32[2]{0:T(128)} %param.19) | copy-start | bytes 28
  146.8 133.7 %all-gather.15.cloned.1.call-start = ((), (), s32[]{:S(2)}) async-start(), calls=%async_computation.8 | async-start | bytes 9437184 | tf_op jit(solution)/shard_map/all_gather | solution.py:1496
  148.6 5.7 copy-start
  170.8 366.4 %all-gather.13.cloned.1.call-start = ((), (), s32[]{:S(2)}) async-start(), calls=%async_computation.7 | async-start | bytes 28311552 | tf_op jit(solution)/shard_map/all_gather | solution.py:1499
  244.6 365.0 %reduce-scatter.6.cloned.1.call-start = ((), (), s32[]{:S(2)}) async-start(), calls=%async_computation.9 | async-start | bytes 6291456 | tf_op jit(solution)/shard_map/reduce_scatter | solution.py:1516
  244.7 4.7 copy-start.22
  244.9 4.6 copy-start.26
  507.5 5.3 copy-start.4
  537.2 321.8 %reduce-scatter.12.cloned.1.call-start = ((), (), s32[]{:S(2)}) async-start(), calls=%async_computation.12 | async-start | bytes 4718592 | tf_op jit(solution)/shard_map/reduce_scatter | solution.py:1522
  609.7 249.4 %reduce-scatter.10.cloned.1.call-start = ((), (), s32[]{:S(2)}) async-start(), calls=%async_computation.11 | async-start | bytes 9437184 | tf_op jit(solution)/shard_map/reduce_scatter | solution.py:1522
  610.4 248.7 %reduce-scatter.8.cloned.1.call-start = ((), (), s32[]{:S(2)}) async-start(), calls=%async_computation.10 | async-start | bytes 9437184 | tf_op jit(solution)/shard_map/reduce_scatter | solution.py:1522
  611.0 333.3 %reduce-scatter.14.cloned.1.call-start = ((), (), s32[]{:S(2)}) async-start(), calls=%async_computation.13 | async-start | bytes 4718592 | tf_op jit(solution)/shard_map/reduce_scatter | solution.py:1530
  859.1 3.3 copy-start.9
  859.2 3.5 copy-start.29
  859.2 3.9 copy-start.32
  859.2 3.9 copy-start.15
  866.4 38.7 %copy-start.33 = (f32[3,2048]{1,0:T(4,128)S(1)}, f32[3,2048]{1,0:T(4,128)}, u32[]{:S(2)}) copy-start(f32[3,2048]{1,0:T(4,128)} %get-tuple-element.103) | copy-start | bytes 73732
  905.0 35.6 %copy-start.30 = (bf16[256,2048]{1,0:T(8,128)(2,1)S(1)}, bf16[256,2048]{1,0:T(8,128)(2,1)}, u32[]{:S(2)}) copy-start(bf16[256,2048]{1,0:T(8,128)(2,1)} %reduce-scatter.8.cloned.1.call-done) | copy-start | bytes 3145732
  905.0 38.5 %copy-start.31 = (bf16[256,1024]{1,0:T(8,128)(2,1)S(1)}, bf16[256,1024]{1,0:T(8,128)(2,1)}, u32[]{:S(2)}) copy-start(bf16[256,1024]{1,0:T(8,128)(2,1)} %reduce-scatter.12.cloned.1.call-done) | copy-start | bytes 1572868
  (17 other events, 30.2 us)
Sparse Core Ops, SparseCore 0:
  10.5 40.8 all-gather.8
  53.9 28.0 all-gather.16
  83.9 77.4 all-gather.10
  163.1 54.2 all-gather.18
  219.1 54.3 all-gather.14
  275.3 125.3 all-gather.12
  537.4 58.3 reduce-scatter.5
  609.8 52.4 reduce-scatter.11
  665.8 71.3 reduce-scatter.9
  740.9 71.3 reduce-scatter.7
  859.3 53.0 reduce-scatter.13
